TPU v7x, 32 devices: a whole 2x2x4 slice. The times are simulated.
32 devices in a mesh: lon: 2 (over x), lat: 4 (over z), mem: 4 (over y, core).
Axes of the slice: x: 2, y: 2, z: 4, core: 2. Of those that a mesh axis runs over, the one named last changes fastest.
Arguments:
- control: float32 [640, 32, 256], P('mem', 'lat', 'lon'), may hold values from -6 to 6
- residual: float32 [640, 32, 256], P('mem', 'lat', 'lon'), may hold values from -6 to 6
- direction: float32 [640, 32, 256], P('mem', 'lat', 'lon'), may hold values from -6 to 6
- members: bfloat16 [80, 32, 32, 256], P('mem', None, 'lat', 'lon'), may hold values from -0.625 to 0.625
- vert_modes: float32 [8, 32], replicated, may hold values from -2 to 2
- eig_count: int32 [80], P('mem'), may hold values from 1 to 8, as said below
- lon_decay: float32 [32], P('lat'), may hold values from 0.001953125 to 0.125
- lat_decay: float32 [256], P('lon'), may hold values from 0.015625 to 1
- obs_weight: float32 [32, 32, 256], P(None, 'lat', 'lon'), may hold values from 0.25 to 4
Outputs:
- new_control: float32 [640, 32, 256], P('mem', 'lat', 'lon')
- new_residual: float32 [640, 32, 256], P('mem', 'lat', 'lon')
- new_direction: float32 [640, 32, 256], P('mem', 'lat', 'lon')
Inputs may be any that keep to these rules, and one draw needn't show every extreme that they name: Member m uses its first eig_count[m] vertical modes; some member uses all 8.
All inputs are finite; a program needn't handle non-finite values.
Results may differ from a plain program's by a relative error of at most 0.0009.
Values sent between devices are 32-bit elements; how exact they have to be, the bound alone decides.
No kernel may reach another device: no remote copies, remote signals or barrier semaphores. Data moves between devices by JAX's collectives and lax.ppermute only.
A program may use at most 64 MiB of HBM per device.

v0:
```python
import functools
import jax
import jax.numpy as jnp
from jax import lax
from jax.experimental import pallas as pl
from jax.experimental.pallas import tpu as pltpu
from jax.sharding import PartitionSpec as P


f32 = jnp.float32
bf16 = jnp.bfloat16
VM = pl.BlockSpec(memory_space=pltpu.VMEM)
SM = pl.BlockSpec(memory_space=pltpu.SMEM)


def choose(length, i):
    r = 1.0
    for k in range(i):
        r = r * (length + k) / (k + 1)
    return r


def rising(v, degree):
    r = jnp.ones_like(v)
    for k in range(degree):
        r = r * (v + (k + 1.0)) * (1.0 / (k + 1.0))
    return r


def halves(v):
    high = v.astype(bf16)
    return high, (v - high.astype(f32)).astype(bf16)


def left3(v, axis):
    high, low = halves(v)
    return jnp.concatenate([high, low, high], axis=axis)


def right3(v, axis):
    high, low = halves(v)
    return jnp.concatenate([high, high, low], axis=axis)


def product3(a, b):
    return jnp.dot(a, b, preferred_element_type=f32)


def iota(shape, dim):
    return lax.broadcasted_iota(jnp.int32, shape, dim).astype(f32)


def lon_consts(lonc):
    c = lonc
    q = jnp.exp(-c)
    leak = 1.0 - q
    return c, leak, 2.5 / jnp.sqrt(leak)


def lon_kernel_matrix(c_row, gain_row, cells, backward):
    a = iota((cells, cells), 0)
    b = iota((cells, cells), 1)
    lag = a - b if backward else b - a
    pos = jnp.maximum(lag, 0.0)
    shaped = rising(pos, 3) * jnp.exp(-pos * c_row) * gain_row
    return jnp.where(lag >= 0.0, shaped, 0.0)


def masked_rows(parts, y):
    rows = iota(parts[0].shape, 0)
    return jnp.concatenate([jnp.where(rows == float(y), p, 0.0) for p in parts], axis=0)


def lon_finals(c, leak, scale, cells, backward):
    x = iota(c.shape, 1)
    remain = x if backward else (cells - 1.0) - x
    decay = jnp.exp(-remain * c)
    return [leak ** (s + 1) * scale * rising(remain, s) * decay for s in range(4)]


def lon_entering(c, leak, cells, backward):
    x = iota(c.shape, 1)
    place = (cells - 1.0) - x if backward else x
    decay = jnp.exp(-(place + 1.0) * c)
    return [leak ** (3 - s) * rising(place, 3 - s) * decay for s in range(4)]


def lon_tables(lonc, rows, cells, backward, table_ref):
    c, leak, scale = lon_consts(lonc)
    gain = leak**4 * scale
    finals = lon_finals(c, leak, scale, cells, backward)
    spare = jnp.zeros((cells - 4 * rows, cells), f32)
    finals = jnp.concatenate(finals + [spare], axis=0).T
    column = lax.broadcasted_iota(jnp.int32, (cells, cells), 1)
    for y in range(rows):
        inside = lon_kernel_matrix(c[y : y + 1], gain[y : y + 1], cells, backward)
        leaving = jnp.where(lax.rem(column, rows) == y, finals, 0.0)
        table_ref[y] = right3(jnp.concatenate([inside, leaving], axis=1), 0)


def lon_local_rows(load_row, table_ref, rows, cells, inside_ref, carried_ref):
    carried = None
    for y in range(rows):
        both = product3(left3(load_row(y), 1), table_ref[y])
        inside_ref[y] = both[:, :cells]
        carried = both[:, cells:] if carried is None else carried + both[:, cells:]
    carried_ref[...] = carried.T[: 4 * rows]


def lon_incoming_states(lonc, blocks, rows, cells):
    k = blocks[0].shape[1]
    n = len(blocks)
    c = jnp.broadcast_to(lonc[:, :1], (rows, k))
    leak = 1.0 - jnp.exp(-c)

    def trans(r):
        closing = jnp.exp(-float(r * cells) * c)
        return [choose(r * cells, i) * leak**i * closing for i in range(4)]

    total = [jnp.zeros((rows, k), f32) for _ in range(4)]
    for r in range(n):
        part = [blocks[r][s * rows : (s + 1) * rows] for s in range(4)]
        if r:
            t = trans(r)
            part = [sum(t[i - j] * part[j] for j in range(i + 1)) for i in range(4)]
        total = [a + b for a, b in zip(total, part)]
    t = trans(n)
    solved = []
    for i in range(4):
        v = total[i]
        for j in range(i):
            v = v + t[i - j] * solved[j]
        solved.append(v / (1.0 - t[0]))
    return jnp.concatenate(solved, axis=0)


def lon_correction(states, entering, rows, cells):
    high = states.astype(bf16).astype(f32)
    low = states - high
    spare = jnp.zeros((cells - 12 * rows, states.shape[1]), f32)
    left = jnp.concatenate([high, low, high, spare], axis=0).T.astype(bf16)
    spare = jnp.zeros((cells - 12 * rows, cells), bf16)
    return lambda y: product3(left, jnp.concatenate([right3(masked_rows(entering, y), 0), spare], axis=0))


def lat_consts(dec):
    q = jnp.exp(-dec)
    leak = 1.0 - q
    return q, leak, leak * (2.5 / jnp.sqrt(leak))


def lat_sweep(load, store, start, dec, rows, k, backward, block):
    q1, l1, g1 = lat_consts(dec)
    x = dec.shape[1]
    q = jnp.broadcast_to(q1, (block, x))
    leak = jnp.broadcast_to(l1, (block, x))
    gain = jnp.broadcast_to(g1, (block, x))
    order = range(rows - 1, -1, -1) if backward else range(rows)

    def step(i, carry):
        at = pl.ds(pl.multiple_of(i * block, 8), block)
        u = start(at)
        for y in order:
            feed = gain * load(y, at, i * block)
            u0 = q * u[0] + feed
            u1 = q * u[1] + leak * u0
            u2 = q * u[2] + leak * u1
            u3 = q * u[3] + leak * u2
            u = [u0, u1, u2, u3]
            store(y, at, i * block, u3, u if y == order[-1] else None)
        return carry

    lax.fori_loop(0, k // block, step, 0)


def swap_halves(a, b):
    half = a.shape[-1] // 2
    low = iota((1,) * (a.ndim - 1) + (a.shape[-1],), a.ndim - 1) < float(half)
    turn = lambda v: pltpu.roll(v, half, v.ndim - 1)
    return jnp.where(low, a, turn(b)), jnp.where(low, turn(a), b)


def both_halves(v):
    return swap_halves(v, v)


def lat_trans(dec, rows):
    leak = 1.0 - jnp.exp(-dec)
    closing = jnp.exp(-float(rows) * dec)
    return [choose(rows, i) * leak**i * closing for i in range(4)]


def entering_states(got, chunks, block):
    hops = len(got) // chunks
    mine = [block == float(h + 1) for h in range(hops)]

    def at(chunk, where):
        out = []
        for s in range(4):
            v = jnp.zeros(block.shape, f32)
            for m, p in zip(mine, got[chunk * hops : (chunk + 1) * hops]):
                v = jnp.where(m, p[s, where, :], v)
            out.append(v)
        return out

    return at


def sweep_chunks(load, store, start, dec, rows, k, chunks, backward):
    size = k // chunks
    for ch in range(chunks):
        lat_sweep(
            lambda y, at, base, ch=ch: load(y, ch * size + base),
            lambda y, at, base, value, last, ch=ch: store(y, ch, at, ch * size + base, value, last),
            lambda at, ch=ch: start(ch, at),
            dec,
            rows,
            size,
            backward,
            8,
        )


def k_tables(rows, cells, dec_ref, lonc_ref, latc_ref, table_ref, block_ref):
    block_ref[...] = jnp.full((8, cells), lax.axis_index("lat").astype(f32))
    row = jnp.broadcast_to(dec_ref[:, cells:], (rows, rows))
    own = iota((rows, rows), 0) == iota((rows, rows), 1)
    column = jnp.sum(jnp.where(own, row, 0.0), axis=1, keepdims=True)
    lonc = jnp.broadcast_to(column, (rows, cells))
    lonc_ref[...] = lonc
    first, second = both_halves(jnp.broadcast_to(dec_ref[:, :cells], (8, cells)))
    latc_ref[0] = first
    latc_ref[1] = second
    lon_tables(lonc, rows, cells, False, table_ref)


def k_lon_fwd(rows, k, cells, d_ref, table_ref, inside_ref, carried_ref):
    d_ref = d_ref.reshape(k * rows, cells)
    lon_local_rows(
        lambda y: d_ref[pl.ds(y, k, stride=rows), :], table_ref, rows, cells, inside_ref, carried_ref
    )


def spread_modes(v, pairs, transposed):
    source = v.T if transposed else v
    r, c = source.shape
    rows, columns = pairs * r, 3 * pairs * c
    exact = functools.partial(jnp.dot, precision=lax.Precision.HIGHEST, preferred_element_type=f32)
    block = lambda at, size: jnp.floor((at + 0.5) * (1.0 / size))
    at_row, at_column = iota((rows, r), 0), iota((c, columns), 1)
    pick_row = (at_row - block(at_row, r) * r == iota((rows, r), 1)).astype(f32)
    pick_column = (at_column - block(at_column, c) * c == iota((c, columns), 0)).astype(f32)
    everywhere = exact(exact(pick_row, source), pick_column)
    column = iota((1, columns), 1)
    part = block(column, pairs * c)
    own = block(iota((rows, 1), 0), r) == block(column - part * (pairs * c), c)
    full = jnp.where(own, everywhere, 0.0)
    high, low = halves(full)
    return jnp.where(part == 1.0, low.astype(f32), high.astype(f32)).astype(bf16)


def k_out_modes(pairs, v_ref, eig_ref, mask_ref, modes_ref):
    modes = v_ref.shape[0]
    cells = mask_ref.shape[1]
    modes_ref[...] = spread_modes(v_ref[...], pairs, True)
    e = lax.broadcasted_iota(jnp.int32, (modes, cells), 0)
    low = lax.broadcasted_iota(jnp.int32, (modes, cells), 1) < cells // 2
    for m in range(pairs):
        used = jnp.where(low, eig_ref[m], eig_ref[m + pairs])
        mask_ref[m * modes : (m + 1) * modes] = jnp.where(e < used, 1.0, 0.0)


def k_in_modes(pairs, v_ref, modes_ref):
    modes_ref[...] = spread_modes(v_ref[...], pairs, False)


def row_spacing(size):
    return size + 8 if size // 8 % 2 == 0 else size


def k_back_tables(lon_ref, table_ref):
    lon_tables(lon_ref[...], *lon_ref.shape, True, table_ref)


def k_prepare(m_ref, a_ref, b_ref):
    members, levels, rows, _ = m_ref.shape
    pairs = members // 2
    apart = row_spacing(pairs * levels)

    def step(i, carry):
        for l in range(levels):
            a, b = swap_halves(m_ref[i, l].astype(f32), m_ref[i + pairs, l].astype(f32))
            at = pl.ds(i * levels + l, rows, stride=apart)
            a_ref[at, :] = a
            b_ref[at, :] = b
        return carry

    lax.fori_loop(0, pairs, step, 0)


def k_lat_first(rows, k, cells, n, chunks, *refs):
    inside_ref, lon_ref, lat_ref, *rest = refs
    blocks = [r[...] for r in rest[:n]]
    f_refs, out_refs = rest[n : n + 2], rest[n + 2 :]
    lonc = lon_ref[...]
    states = lon_incoming_states(lonc, blocks, rows, cells)
    c, leak, _ = lon_consts(lonc)
    added = lon_correction(states, lon_entering(c, leak, cells, False), rows, cells)
    half = k // 2
    for y in range(rows):
        row = inside_ref[y] + added(y)
        f_refs[0][y], f_refs[1][y] = swap_halves(row[:half], row[half:])
    zero = jnp.zeros((8, cells), f32)
    for part, f_ref in enumerate(f_refs):

        def store(y, ch, at, base, value, last, part=part):
            if last is not None:
                for s in range(4):
                    out_refs[part * chunks + ch][s, at, :] = last[s]

        sweep_chunks(
            lambda y, base: f_ref[y, pl.ds(pl.multiple_of(base, 8), 8), :],
            store,
            lambda ch, at: [zero] * 4,
            lat_ref[part, :1],
            rows,
            half,
            chunks,
            False,
        )


def k_pass_on(rows, part, carried_ref, got_ref, lat_ref, out_ref):
    t = lat_trans(lat_ref[part, :1], rows)
    got = [got_ref[s] for s in range(4)]
    for i in range(4):
        v = carried_ref[i]
        for j in range(i + 1):
            v = v + t[i - j] * got[j]
        out_ref[i] = v


def k_increment(rows, k, part, chunks, count, pairs, levels, *refs):
    f_ref, lat_ref, block_ref, m_ref, mask_ref, modes_ref, *rest = refs
    out_ref, s_ref = rest[count:]
    cells = lat_ref.shape[-1]

    def store(y, ch, at, base, value, last):
        where = pl.ds(pl.multiple_of(base, 8), 8)
        s_ref[y, where, :] = value * mask_ref[where, :]

    sweep_chunks(
        lambda y, base: f_ref[y, pl.ds(pl.multiple_of(base, 8), 8), :],
        store,
        entering_states(rest[:count], chunks, block_ref[...]),
        lat_ref[part, :1],
        rows,
        k,
        chunks,
        False,
    )
    half = levels // 2
    low = iota((1, cells), 1) < float(cells // 2)
    apart = row_spacing(pairs * levels)
    for y in range(rows):
        profile = product3(modes_ref[...], right3(s_ref[y], 0))
        inc = None
        for m in range(pairs):
            at = y * apart + m * levels
            p = m_ref[at : at + levels, :] * profile[m * levels : (m + 1) * levels]
            inc = p if inc is None else inc + p
        inc = inc + pltpu.roll(inc, cells // 2, 1)
        out_ref[y] = jnp.where(low, inc[:half], inc[half:])


def k_gradient(rows, k, part, chunks, pairs, levels, *refs):
    inc_ref, got_ref, obs_ref, m_ref, mask_ref, modes_ref, lat_ref, g_ref, *carried_refs = refs
    cells = lat_ref.shape[-1]
    obs_ref = obs_ref.reshape(levels * rows, cells)
    size = pairs * levels
    apart = row_spacing(size)
    for y in range(rows):
        inc = jnp.concatenate(both_halves(inc_ref[y] + got_ref[y]), axis=0)
        w = inc * both_halves(obs_ref[pl.ds(y, levels, stride=rows), :])[part]
        m = m_ref[y * apart : y * apart + size, :]
        weighted = (m.reshape(pairs, levels, cells) * w[None]).reshape(size, cells)
        g_ref[y] = product3(modes_ref[...], right3(weighted, 0)) * mask_ref[...]
    zero8 = jnp.zeros((8, cells), f32)

    def store(y, ch, at, base, value, last):
        if last is not None:
            for s in range(4):
                carried_refs[ch][s, at, :] = last[s]

    sweep_chunks(
        lambda y, base: g_ref[y, pl.ds(pl.multiple_of(base, 8), 8), :],
        store,
        lambda ch, at: [zero8] * 4,
        lat_ref[part, :1],
        rows,
        k,
        chunks,
        True,
    )


def k_lon_bwd(rows, k, cells, chunks, count, blocks, *refs):
    g_refs, lat_ref, block_ref, table_ref, rest = refs[:2], refs[2], refs[3], refs[4], refs[5:]
    block = (blocks - 1.0) - block_ref[...]
    inside_ref, carried_ref, p_ref = rest[2 * count :]
    half = k // 2
    for part in range(2):
        g_ref = g_refs[part]

        def store(y, ch, at, base, value, last, part=part):
            p_ref[part, y, pl.ds(pl.multiple_of(base, 8), 8), :] = value

        sweep_chunks(
            lambda y, base: g_ref[y, pl.ds(pl.multiple_of(base, 8), 8), :],
            store,
            entering_states(rest[part * count : (part + 1) * count], chunks, block),
            lat_ref[part, :1],
            rows,
            half,
            chunks,
            True,
        )

    def load_row(y):
        return jnp.concatenate(swap_halves(p_ref[0, y], p_ref[1, y]), axis=0)

    lon_local_rows(load_row, table_ref, rows, cells, inside_ref, carried_ref)


def k_sums(rows, k, cells, n, *refs):
    inside_ref, lon_ref, d_ref, r_ref, *rest = refs
    d_ref = d_ref.reshape(k * rows, cells)
    r_ref = r_ref.reshape(k * rows, cells)
    blocks = [r[...] for r in rest[:n]]
    h_ref, sums_ref = rest[n:]
    lonc = lon_ref[...]
    states = lon_incoming_states(lonc, blocks, rows, cells)
    c, leak, _ = lon_consts(lonc)
    added = lon_correction(states, lon_entering(c, leak, cells, True), rows, cells)
    for y in range(rows):
        at = pl.ds(y, k, stride=rows)
        h_ref[at, :] = inside_ref[y] + added(y)
    block = 64
    zero = jnp.zeros((8, cells), f32)

    def step(i, acc):
        at = pl.ds(pl.multiple_of(i * block, 8), block)
        d = d_ref[at, :]
        r = r_ref[at, :]
        h = h_ref[at, :] + d
        h_ref[at, :] = h
        fold = lambda v: v.reshape(block // 8, 8, cells).sum(axis=0)
        return (acc[0] + fold(r * r), acc[1] + fold(d * h), acc[2] + fold(r * h), acc[3] + fold(h * h))

    acc = lax.fori_loop(0, (k * rows) // block, step, (zero,) * 4)
    out = [a.sum(axis=0, keepdims=True) for a in acc]
    sums_ref[...] = jnp.concatenate(out + [jnp.zeros((4, cells), f32)], axis=0)


def k_update(pieces, sums_ref, control_ref, r_ref, d_ref, h_ref, *rest):
    outs, news, sems = rest[:3], rest[3:6], rest[6]
    sums = jnp.sum(sums_ref[...], axis=1, keepdims=True)
    rr, dh, rh, hh = (sums[i : i + 1].reshape(1, 1, 1) for i in range(4))
    step = rr / dh
    norm_new = rr - 2.0 * step * rh + step * step * hh
    beta = norm_new / rr
    size = d_ref.shape[0] // pieces
    copies = []
    for i in range(pieces):
        at = pl.ds(i * size, size)
        d = d_ref[at]
        nr = r_ref[at] - step * h_ref[at]
        for j, v in enumerate((control_ref[at] + step * d, nr, nr + beta * d)):
            news[j][at] = v
            copy = pltpu.make_async_copy(news[j].at[at], outs[j].at[at], sems.at[j, i])
            copy.start()
            copies.append(copy)
    for copy in copies:
        copy.wait()


def call(body, outs, ins, specs=None, out_specs=None, scratch=(), cost=None):
    return pl.pallas_call(
        body,
        out_shape=outs,
        in_specs=specs or [VM] * len(ins),
        out_specs=out_specs or jax.tree.map(lambda _: VM, outs),
        scratch_shapes=scratch,
        cost_estimate=None if cost is None else pl.CostEstimate(flops=cost, bytes_accessed=1000, transcendentals=0),
        compiler_params=pltpu.CompilerParams(vmem_limit_bytes=16 * 1024 * 1024),
    )(*ins)


def sds(*shape):
    return jax.ShapeDtypeStruct(shape, f32)


def lon_exchange(carried, backward):
    n = lax.axis_size("lon")
    sign = -1 if backward else 1
    got = [
        lax.ppermute(carried, "lon", [(j, (j + sign * r) % n) for j in range(n)]) for r in range(1, n)
    ]
    return got + [carried]


def pass_on(part, got, latc, rows, c):
    return call(functools.partial(k_pass_on, rows, c), sds(*part.shape), [part, got, latc])


def hop_pairs(a, b):
    n, n_mem = lax.axis_size("lat"), lax.axis_size("mem")
    if n_mem % 2:
        return [(a * n_mem + i, b * n_mem + i) for i in range(n_mem)]
    to = lambda z, i: (b, i) if z == a else (a, i) if z == b else (z, i ^ 1)
    flat = lambda z, i: z * n_mem + i
    return [(flat(z, i), flat(*to(z, i))) for z in range(n) for i in range(n_mem)]


def lat_carry(halves, latc, rows, backward):
    n = lax.axis_size("lat")
    at = (lambda i: n - 1 - i) if backward else (lambda i: i)
    got = [[[] for _ in chunks] for chunks in halves]
    for h in range(n - 1):
        pairs = hop_pairs(at(h), at(h + 1))
        for c, chunks in enumerate(halves):
            for i, part in enumerate(chunks):
                v = pass_on(part, got[c][i][-1], latc, rows, c) if h else part
                got[c][i].append(lax.ppermute(v, ("lat", "mem"), pairs))
    return [[g for chunk in half for g in chunk] for half in got]


def all_sum(v, axes, steps):
    total = 1
    for a in axes:
        total *= lax.axis_size(a)
    masks = [0]
    for s in steps:
        masks = masks + [m ^ s for m in masks]
    got = [lax.ppermute(v, axes, [(i, i ^ m) for i in range(total)]) for m in masks[1:]]
    for g in got:
        v = v + g
    return v


def powers(n):
    out, d = [], 1
    while d < n:
        out.append(d)
        d *= 2
    return out


def reduce_everywhere(v):
    n_lon, n_lat, n_mem = (lax.axis_size(a) for a in ("lon", "lat", "mem"))
    for s in powers(n_mem):
        v = all_sum(v, ("mem",), [s])
    for s in powers(n_lon):
        v = all_sum(v, ("lon",), [s])
    lat = powers(n_lat)
    for i in range(0, len(lat), 2):
        v = all_sum(v, ("lat",), lat[i : i + 2])
    return v


def iteration(control, residual, direction, members, vert_modes, eig_count, lon_decay, lat_decay, obs_weight):
    k, rows, cells = direction.shape
    mcount, levels = members.shape[:2]
    n_lon, n_mem = lax.axis_size("lon"), lax.axis_size("mem")
    half = k // 2
    pairs = mcount // 2
    chunks, back_chunks = 2, 2
    states = lambda chunks: (sds(4, half // chunks, cells),) * chunks

    decays = jnp.concatenate([lat_decay, lon_decay]).reshape(1, cells + rows)
    lonc, latc, tables, block = call(
        functools.partial(k_tables, rows, cells),
        (sds(rows, cells), sds(2, 8, cells), jax.ShapeDtypeStruct((rows, 3 * cells, 2 * cells), bf16), sds(8, cells)),
        [decays],
        cost=10**9,
    )
    inside, carried = call(
        functools.partial(k_lon_fwd, rows, k, cells), (sds(rows, k, cells), sds(4 * rows, k)), [direction, tables]
    )
    packed = call(k_prepare, (sds(rows * row_spacing(pairs * levels), cells),) * 2, [members], cost=10**9)
    back_tables = call(k_back_tables, jax.ShapeDtypeStruct((rows, 3 * cells, 2 * cells), bf16), [lonc], cost=10**9)
    mask, out_modes = call(
        functools.partial(k_out_modes, pairs),
        (sds(half, cells), jax.ShapeDtypeStruct((pairs * levels, 3 * half), bf16)),
        [vert_modes, eig_count],
        specs=[VM, SM],
        cost=10**9,
    )
    in_modes = call(
        functools.partial(k_in_modes, pairs),
        jax.ShapeDtypeStruct((half, 3 * pairs * levels), bf16),
        [vert_modes],
        cost=10**9,
    )
    blocks = lon_exchange(carried, False)
    fa, fb, *parts = call(
        functools.partial(k_lat_first, rows, k, cells, n_lon, chunks),
        (sds(rows, half, cells),) * 2 + states(chunks) * 2,
        [inside, lonc, latc, *blocks],
    )
    got = lat_carry([parts[:chunks], parts[chunks:]], latc, rows, False)
    count = len(got[0])
    fields = (fa, fb)
    inc = [None, None]
    for part in range(2):
        inc[part] = call(
            functools.partial(k_increment, rows, half, part, chunks, count, pairs, levels),
            sds(rows, levels // 2, cells),
            [fields[part], latc, block, packed[part], mask, out_modes, *got[part]],
            scratch=[pltpu.VMEM((rows, half, cells), f32)],
        )
    grads, sends = [None, None], [None, None]
    for part in range(2):
        v = inc[part]
        step = 1
        while step * 2 < n_mem:
            v = v + lax.ppermute(v, "mem", [(i, i ^ step) for i in range(n_mem)])
            step *= 2
        other = lax.ppermute(v, "mem", [(i, i ^ step) for i in range(n_mem)])
        grads[part], *sends[part] = call(
            functools.partial(k_gradient, rows, half, part, back_chunks, pairs, levels),
            (sds(rows, half, cells),) + states(back_chunks),
            [v, other, obs_weight, packed[part], mask, in_modes, latc],
        )
    got = lat_carry(sends, latc, rows, True)
    count = len(got[0])
    inside, carried = call(
        functools.partial(k_lon_bwd, rows, k, cells, back_chunks, count, lax.axis_size("lat")),
        (sds(rows, k, cells), sds(4 * rows, k)),
        [*grads, latc, block, back_tables, *got[0], *got[1]],
        scratch=[pltpu.VMEM((2, rows, half, cells), f32)],
    )
    blocks = lon_exchange(carried, True)
    h, sums = call(
        functools.partial(k_sums, rows, k, cells, n_lon),
        (sds(k * rows, cells), sds(8, cells)),
        [inside, lonc, direction, residual, *blocks],
    )
    sums = reduce_everywhere(sums)
    pieces = 4 if k % 4 == 0 else 1
    outs = call(
        functools.partial(k_update, pieces),
        (sds(k, rows, cells),) * 3,
        [sums, control, residual, direction, h.reshape(k, rows, cells)],
        out_specs=(pl.BlockSpec(memory_space=pl.ANY),) * 3,
        scratch=[pltpu.VMEM((k, rows, cells), f32)] * 3 + [pltpu.SemaphoreType.DMA((3, pieces))],
    )
    return tuple(outs)


def solution(mesh):
    field = P("mem", "lat", "lon")
    placed = (
        field,
        field,
        field,
        P("mem", None, "lat", "lon"),
        P(),
        P("mem"),
        P("lat"),
        P("lon"),
        P(None, "lat", "lon"),
    )
    return jax.shard_map(iteration, mesh=mesh, in_specs=placed, out_specs=(field,) * 3, check_vma=False)
```

profile of v0, /device:TPU:0, one launch (start us, length us, event | category | flops | bytes accessed | tf_op | source)
XLA Modules:
  0.0 76.5 jit_solution(6021651579017369840)
XLA Ops:
  3.0 3.0 %collective-permute-start = (f32[32,160]{1,0:T(8,128)S(1)}, f32[32,160]{1,0:T(8,128)S(1)}, u32[]{:S(2)}, u32[]{:S(2)}) collective-permute-start(f32[32,160]{1,0:T(8,128)S(1)} %get-tuple-element.33.refs_4_), channel_id=1, source_target_pairs={{0,16},{16,0},{1,17},{17,1},{2,18},{18,2},{3,19},{19,3},{4,20},{20... | collective-permute-start | bytes 61448 | tf_op jit(solution)/shard_map/ppermute | solution.py:507
  6.0 1.9 %collective-permute-done.refs_3_ = f32[32,160]{1,0:T(8,128)S(1)} collective-permute-done((f32[32,160]{1,0:T(8,128)S(1)}, f32[32,160]{1,0:T(8,128)S(1)}, u32[]{:S(2)}, u32[]{:S(2)}) %collective-permute-start) | collective-permute-done | bytes 20512 | tf_op jit(solution)/shard_map/ppermute | solution.py:507
  7.9 1.1 %shard_map.114 = (f32[8,80,128]{2,1,0:T(8,128)S(1)}, f32[8,80,128]{2,1,0:T(8,128)S(1)}, f32[4,40,128]{2,1,0:T(8,128)S(1)}, f32[4,40,128]{2,1,0:T(8,128)S(1)}, f3...) custom-call(f32[8,160,128]{2,1,0:T(8,128)S(1)} %get-tuple-element.30.refs_0_, ...), custom_call_target="tpu_custom_call" | custom-call | tf_op jit(solution)/shard_map/pallas_call | solution.py:488
  9.0 2.2 %collective-permute-start.12 = (f32[4,40,128]{2,1,0:T(8,128)S(1)}, f32[4,40,128]{2,1,0:T(8,128)S(1)}, u32[]{:S(2)}, u32[]{:S(2)}) collective-permute-start(f32[4,40,128]{2,1,0:T(8,128)S(1)} %get-tuple-element.45.carried_ref), channel_id=1, source_target_pairs={{0,4},{1,5},{2,6},{3,7},{4,0},{5,1},{6,2},{7,3},{8,9},{9,8},{10,11... | collective-permute-start | bytes 245768 | tf_op jit(solution)/shard_map/ppermute | solution.py:534
  11.2 1.9 %collective-permute-start.4 = (f32[4,40,128]{2,1,0:T(8,128)S(1)}, f32[4,40,128]{2,1,0:T(8,128)S(1)}, u32[]{:S(2)}, u32[]{:S(2)}) collective-permute-start(f32[4,40,128]{2,1,0:T(8,128)S(1)} %get-tuple-element.40.carried_ref), channel_id=1, source_target_pairs={{0,4},{1,5},{2,6},{3,7},{4,0},{5,1},{6,2},{7,3},{8,9},{9,8},{10,11... | collective-permute-start | bytes 245768 | tf_op jit(solution)/shard_map/ppermute | solution.py:534
  13.2 1.2 %collective-permute-done.12.got_ref.refs_9_ = f32[4,40,128]{2,1,0:T(8,128)S(1)} collective-permute-done((f32[4,40,128]{2,1,0:T(8,128)S(1)}, f32[4,40,128]{2,1,0:T(8,128)S(1)}, u32[]{:S(2)}, u32[]{:S(2)}) %collective-permute-start.12) | collective-permute-done | bytes 81952 | tf_op jit(solution)/shard_map/ppermute | solution.py:534
  14.5 1.9 %collective-permute-done.9.got_ref.refs_6_ = f32[4,40,128]{2,1,0:T(8,128)S(1)} collective-permute-done((f32[4,40,128]{2,1,0:T(8,128)S(1)}, f32[4,40,128]{2,1,0:T(8,128)S(1)}, u32[]{:S(2)}, u32[]{:S(2)}) %collective-permute-start.9) | collective-permute-done | bytes 81952 | tf_op jit(solution)/shard_map/ppermute | solution.py:534
  18.4 1.1 %shard_map.115 = (f32[2624,128]{1,0:T(8,128)S(1)}, f32[2624,128]{1,0:T(8,128)S(1)}) custom-call(bf16[20,32,8,128]{3,2,1,0:T(8,128)(2,1)S(1)} %copy-done.4), custom_call_target="tpu_custom_call" | custom-call | flops 1000000000 | bytes 1000 | tf_op jit(solution)/shard_map/pallas_call | solution.py:488
  20.9 1.4 %shard_map.116 = (f32[80,128]{1,0:T(8,128)S(1)}, bf16[320,240]{1,0:T(8,128)(2,1)S(1)}) custom-call(f32[8,32]{1,0:T(8,128)S(1)} %copy-done.5, s32[20]{0:T(128)S(1)} %copy-done.6), custom_call_target="tpu_custom_call" | custom-call | flops 1000000000 | bytes 1000 | tf_op jit(solution)/shard_map/pallas_call | solution.py:488
  24.9 1.6 %collective-permute-start.16 = (f32[8,16,128]{2,1,0:T(8,128)S(1)}, f32[8,16,128]{2,1,0:T(8,128)S(1)}, u32[]{:S(2)}, u32[]{:S(2)}) collective-permute-start(f32[8,16,128]{2,1,0:T(8,128)S(1)} %add.25.refs_0_), channel_id=1, source_target_pairs={{0,2},{1,3},{2,0},{3,1},{4,6},{5,7},{6,4},{7,5},{8,10},{9,11},{10,... | collective-permute-start | bytes 196616 | tf_op jit(solution)/shard_map/ppermute | solution.py:629
  26.5 1.2 %collective-permute-start.8 = (f32[8,16,128]{2,1,0:T(8,128)S(1)}, f32[8,16,128]{2,1,0:T(8,128)S(1)}, u32[]{:S(2)}, u32[]{:S(2)}) collective-permute-start(f32[8,16,128]{2,1,0:T(8,128)S(1)} %add.24.refs_0_), channel_id=1, source_target_pairs={{0,2},{1,3},{2,0},{3,1},{4,6},{5,7},{6,4},{7,5},{8,10},{9,11},{10,... | collective-permute-start | bytes 196616 | tf_op jit(solution)/shard_map/ppermute | solution.py:629
  28.3 1.2 %collective-permute-done.16.refs_1_ = f32[8,16,128]{2,1,0:T(8,128)S(1)} collective-permute-done((f32[8,16,128]{2,1,0:T(8,128)S(1)}, f32[8,16,128]{2,1,0:T(8,128)S(1)}, u32[]{:S(2)}, u32[]{:S(2)}) %collective-permute-start.16) | collective-permute-done | bytes 65568 | tf_op jit(solution)/shard_map/ppermute | solution.py:629
  29.5 0.9 %shard_map.129 = (f32[8,80,128]{2,1,0:T(8,128)S(1)}, f32[4,40,128]{2,1,0:T(8,128)S(1)}, f32[4,40,128]{2,1,0:T(8,128)S(1)}) custom-call(f32[8,16,128]{2,1,0:T(8,128)S(1)} %add.25.refs_0_, f32[8,16,128]{2,1,0:T(8,128)S(1)} %collective-permute-done.16.refs_1_, f32[32,8,128]{2,1,0:T(8,128)S(1)} %copy-done.3, f32[2624,128]{1,0:T(8,128)S(1)} %get-tuple-element.43.refs_3_, ...), custom_call_target="tpu_custom_call" | custom-call | tf_op jit(solution)/shard_map/pallas_call | solution.py:488
  31.0 0.9 %shard_map.123 = (f32[8,80,128]{2,1,0:T(8,128)S(1)}, f32[4,40,128]{2,1,0:T(8,128)S(1)}, f32[4,40,128]{2,1,0:T(8,128)S(1)}) custom-call(f32[8,16,128]{2,1,0:T(8,128)S(1)} %add.24.refs_0_, f32[8,16,128]{2,1,0:T(8,128)S(1)} %collective-permute-done.8.refs_1_, f32[32,8,128]{2,1,0:T(8,128)S(1)} %copy-done.3, f32[2624,128]{1,0:T(8,128)S(1)} %get-tuple-element.36.refs_3_, ...), custom_call_target="tpu_custom_call" | custom-call | tf_op jit(solution)/shard_map/pallas_call | solution.py:488
  34.0 12.9 %collective-permute-start.28 = (f32[4,40,128]{2,1,0:T(8,128)S(1)}, f32[4,40,128]{2,1,0:T(8,128)S(1)}, u32[]{:S(2)}, u32[]{:S(2)}) collective-permute-start(f32[4,40,128]{2,1,0:T(8,128)S(1)} %shard_map.138), channel_id=1, source_target_pairs={{0,4},{1,5},{2,6},{3,7},{4,0},{5,1},{6,2},{7,3},{8,9},{9,8},{10,11... | collective-permute-start | bytes 245768 | tf_op jit(solution)/shard_map/ppermute | solution.py:534
  46.9 1.0 %collective-permute-start.25 = (f32[4,40,128]{2,1,0:T(8,128)S(1)}, f32[4,40,128]{2,1,0:T(8,128)S(1)}, u32[]{:S(2)}, u32[]{:S(2)}) collective-permute-start(f32[4,40,128]{2,1,0:T(8,128)S(1)} %shard_map.136), channel_id=1, source_target_pairs={{0,4},{1,5},{2,6},{3,7},{4,0},{5,1},{6,2},{7,3},{8,9},{9,8},{10,11... | collective-permute-start | bytes 245768 | tf_op jit(solution)/shard_map/ppermute | solution.py:534
  47.9 1.1 %collective-permute-start.22 = (f32[4,40,128]{2,1,0:T(8,128)S(1)}, f32[4,40,128]{2,1,0:T(8,128)S(1)}, u32[]{:S(2)}, u32[]{:S(2)}) collective-permute-start(f32[4,40,128]{2,1,0:T(8,128)S(1)} %shard_map.134), channel_id=1, source_target_pairs={{0,4},{1,5},{2,6},{3,7},{4,0},{5,1},{6,2},{7,3},{8,9},{9,8},{10,11... | collective-permute-start | bytes 245768 | tf_op jit(solution)/shard_map/ppermute | solution.py:534
  49.1 1.4 %collective-permute-start.19 = (f32[4,40,128]{2,1,0:T(8,128)S(1)}, f32[4,40,128]{2,1,0:T(8,128)S(1)}, u32[]{:S(2)}, u32[]{:S(2)}) collective-permute-start(f32[4,40,128]{2,1,0:T(8,128)S(1)} %shard_map.132), channel_id=1, source_target_pairs={{0,4},{1,5},{2,6},{3,7},{4,0},{5,1},{6,2},{7,3},{8,9},{9,8},{10,11... | collective-permute-start | bytes 245768 | tf_op jit(solution)/shard_map/ppermute | solution.py:534
  50.9 1.4 %collective-permute-done.25.refs_13_ = f32[4,40,128]{2,1,0:T(8,128)S(1)} collective-permute-done((f32[4,40,128]{2,1,0:T(8,128)S(1)}, f32[4,40,128]{2,1,0:T(8,128)S(1)}, u32[]{:S(2)}, u32[]{:S(2)}) %collective-permute-start.25) | collective-permute-done | bytes 81952 | tf_op jit(solution)/shard_map/ppermute | solution.py:534
  52.3 0.9 %collective-permute-done.22.refs_10_ = f32[4,40,128]{2,1,0:T(8,128)S(1)} collective-permute-done((f32[4,40,128]{2,1,0:T(8,128)S(1)}, f32[4,40,128]{2,1,0:T(8,128)S(1)}, u32[]{:S(2)}, u32[]{:S(2)}) %collective-permute-start.22) | collective-permute-done | bytes 81952 | tf_op jit(solution)/shard_map/ppermute | solution.py:534
  54.1 1.2 %shard_map.139 = (f32[8,160,128]{2,1,0:T(8,128)S(1)}, f32[32,160]{1,0:T(8,128)S(1)}) custom-call(f32[8,80,128]{2,1,0:T(8,128)S(1)} %get-tuple-element.41.refs_0_, f32[8,80,128]{2,1,0:T(8,128)S(1)} %get-tuple-element.46.refs_1_, f32[2,8,128]{2,1,0:T(8,128)S(1)} %get-tuple-element.32.refs_2_.lat_ref.refs_1_.refs_6_, ...), custom_call_target="tpu_custom_call" | custom-call | tf_op jit(solution)/shard_map/pallas_call | solution.py:488
  55.3 1.5 %collective-permute-start.29 = (f32[32,160]{1,0:T(8,128)S(1)}, f32[32,160]{1,0:T(8,128)S(1)}, u32[]{:S(2)}, u32[]{:S(2)}) collective-permute-start(f32[32,160]{1,0:T(8,128)S(1)} %get-tuple-element.52.refs_5_), channel_id=1, source_target_pairs={{0,16},{16,0},{1,17},{17,1},{2,18},{18,2},{3,19},{19,3},{4,20},{20... | collective-permute-start | bytes 61448 | tf_op jit(solution)/shard_map/ppermute | solution.py:507
  56.9 2.4 %collective-permute-done.29.refs_4_ = f32[32,160]{1,0:T(8,128)S(1)} collective-permute-done((f32[32,160]{1,0:T(8,128)S(1)}, f32[32,160]{1,0:T(8,128)S(1)}, u32[]{:S(2)}, u32[]{:S(2)}) %collective-permute-start.29) | collective-permute-done | bytes 20512 | tf_op jit(solution)/shard_map/ppermute | solution.py:507
  60.1 1.2 %collective-permute-done.30 = f32[8,128]{1,0:T(8,128)S(1)} collective-permute-done((f32[8,128]{1,0:T(8,128)S(1)}, f32[8,128]{1,0:T(8,128)S(1)}, u32[]{:S(2)}, u32[]{:S(2)}) %collective-permute-start.30) | collective-permute-done | bytes 4128 | tf_op jit(solution)/shard_map/ppermute | solution.py:545
  61.3 1.5 %collective-permute-start.31 = (f32[8,128]{1,0:T(8,128)S(1)}, f32[8,128]{1,0:T(8,128)S(1)}, u32[]{:S(2)}, u32[]{:S(2)}) collective-permute-start(f32[8,128]{1,0:T(8,128)S(1)} %add.26), channel_id=1, source_target_pairs={{0,2},{1,3},{2,0},{3,1},{4,6},{5,7},{6,4},{7,5},{8,10},{9,11},{10,... | collective-permute-start | bytes 12296 | tf_op jit(solution)/shard_map/ppermute | solution.py:545
  62.7 2.2 %collective-permute-done.31 = f32[8,128]{1,0:T(8,128)S(1)} collective-permute-done((f32[8,128]{1,0:T(8,128)S(1)}, f32[8,128]{1,0:T(8,128)S(1)}, u32[]{:S(2)}, u32[]{:S(2)}) %collective-permute-start.31) | collective-permute-done | bytes 4128 | tf_op jit(solution)/shard_map/ppermute | solution.py:545
  64.9 1.5 %collective-permute-start.32 = (f32[8,128]{1,0:T(8,128)S(1)}, f32[8,128]{1,0:T(8,128)S(1)}, u32[]{:S(2)}, u32[]{:S(2)}) collective-permute-start(f32[8,128]{1,0:T(8,128)S(1)} %add.27), channel_id=1, source_target_pairs={{0,16},{16,0},{1,17},{17,1},{2,18},{18,2},{3,19},{19,3},{4,20},{20... | collective-permute-start | bytes 12296 | tf_op jit(solution)/shard_map/ppermute | solution.py:545
  66.4 2.1 %collective-permute-done.32 = f32[8,128]{1,0:T(8,128)S(1)} collective-permute-done((f32[8,128]{1,0:T(8,128)S(1)}, f32[8,128]{1,0:T(8,128)S(1)}, u32[]{:S(2)}, u32[]{:S(2)}) %collective-permute-start.32) | collective-permute-done | bytes 4128 | tf_op jit(solution)/shard_map/ppermute | solution.py:545
  68.5 1.1 %collective-permute-start.33 = (f32[8,128]{1,0:T(8,128)S(1)}, f32[8,128]{1,0:T(8,128)S(1)}, u32[]{:S(2)}, u32[]{:S(2)}) collective-permute-start(f32[8,128]{1,0:T(8,128)S(1)} %add.28), channel_id=1, source_target_pairs={{0,4},{4,0},{8,12},{12,8},{1,5},{5,1},{9,13},{13,9},{2,6},{6,2},{1... | collective-permute-start | bytes 12296 | tf_op jit(solution)/shard_map/ppermute | solution.py:545
  69.6 3.3 %collective-permute-start.35 = (f32[8,128]{1,0:T(8,128)S(1)}, f32[8,128]{1,0:T(8,128)S(1)}, u32[]{:S(2)}, u32[]{:S(2)}) collective-permute-start(f32[8,128]{1,0:T(8,128)S(1)} %add.28), channel_id=1, source_target_pairs={{0,12},{4,8},{8,4},{12,0},{1,13},{5,9},{9,5},{13,1},{2,14},{6,10},... | collective-permute-start | bytes 12296 | tf_op jit(solution)/shard_map/ppermute | solution.py:545
  72.9 1.2 %collective-permute-done.34 = f32[8,128]{1,0:T(8,128)S(1)} collective-permute-done((f32[8,128]{1,0:T(8,128)S(1)}, f32[8,128]{1,0:T(8,128)S(1)}, u32[]{:S(2)}, u32[]{:S(2)}) %collective-permute-start.34) | collective-permute-done | bytes 4128 | tf_op jit(solution)/shard_map/ppermute | solution.py:545
  75.0 1.5 %shard_map.141 = (f32[160,8,128]{2,1,0:T(8,128)}, f32[160,8,128]{2,1,0:T(8,128)}, f32[160,8,128]{2,1,0:T(8,128)}) custom-call(f32[8,128]{1,0:T(8,128)S(1)} %add_add_fusion.sums_ref, f32[160,8,128]{2,1,0:T(8,128)S(1)} %copy-done.2, f32[160,8,128]{2,1,0:T(8,128)S(1)} %copy-done.1, f32[160,8,128]{2,1,0:T(8,128)S(1)} %copy-done, f32[160,8,128]{2,1,0:T(8,128)S(1)} %bitcast.2), custom_call_target="tpu_custom_call" | custom-call | tf_op jit(solution)/shard_map/pallas_call | solution.py:488
  (91 shorter events, 14.6 us)
Async XLA Ops:
  3.0 4.9 %collective-permute-start = (f32[32,160]{1,0:T(8,128)S(1)}, f32[32,160]{1,0:T(8,128)S(1)}, u32[]{:S(2)}, u32[]{:S(2)}) collective-permute-start(f32[32,160]{1,0:T(8,128)S(1)} %get-tuple-element.33.refs_4_), channel_id=1, source_target_pairs={{0,16},{16,0},{1,17},{17,1},{2,18},{18,2},{3,19},{19,3},{4,20},{20... | collective-permute-start | bytes 61448 | tf_op jit(solution)/shard_map/ppermute | solution.py:507
  9.0 5.5 %collective-permute-start.12 = (f32[4,40,128]{2,1,0:T(8,128)S(1)}, f32[4,40,128]{2,1,0:T(8,128)S(1)}, u32[]{:S(2)}, u32[]{:S(2)}) collective-permute-start(f32[4,40,128]{2,1,0:T(8,128)S(1)} %get-tuple-element.45.carried_ref), channel_id=1, source_target_pairs={{0,4},{1,5},{2,6},{3,7},{4,0},{5,1},{6,2},{7,3},{8,9},{9,8},{10,11... | collective-permute-start | bytes 245768 | tf_op jit(solution)/shard_map/ppermute | solution.py:534
  11.1 5.3 %collective-permute-start.9 = (f32[4,40,128]{2,1,0:T(8,128)S(1)}, f32[4,40,128]{2,1,0:T(8,128)S(1)}, u32[]{:S(2)}, u32[]{:S(2)}) collective-permute-start(f32[4,40,128]{2,1,0:T(8,128)S(1)} %get-tuple-element.44.carried_ref), channel_id=1, source_target_pairs={{0,4},{1,5},{2,6},{3,7},{4,0},{5,1},{6,2},{7,3},{8,9},{9,8},{10,11... | collective-permute-start | bytes 245768 | tf_op jit(solution)/shard_map/ppermute | solution.py:534
  11.2 6.2 %collective-permute-start.4 = (f32[4,40,128]{2,1,0:T(8,128)S(1)}, f32[4,40,128]{2,1,0:T(8,128)S(1)}, u32[]{:S(2)}, u32[]{:S(2)}) collective-permute-start(f32[4,40,128]{2,1,0:T(8,128)S(1)} %get-tuple-element.40.carried_ref), channel_id=1, source_target_pairs={{0,4},{1,5},{2,6},{3,7},{4,0},{5,1},{6,2},{7,3},{8,9},{9,8},{10,11... | collective-permute-start | bytes 245768 | tf_op jit(solution)/shard_map/ppermute | solution.py:534
  13.1 5.1 %collective-permute-start.1 = (f32[4,40,128]{2,1,0:T(8,128)S(1)}, f32[4,40,128]{2,1,0:T(8,128)S(1)}, u32[]{:S(2)}, u32[]{:S(2)}) collective-permute-start(f32[4,40,128]{2,1,0:T(8,128)S(1)} %get-tuple-element.39.carried_ref), channel_id=1, source_target_pairs={{0,4},{1,5},{2,6},{3,7},{4,0},{5,1},{6,2},{7,3},{8,9},{9,8},{10,11... | collective-permute-start | bytes 245768 | tf_op jit(solution)/shard_map/ppermute | solution.py:534
  14.4 5.0 %collective-permute-start.13 = (f32[4,40,128]{2,1,0:T(8,128)S(1)}, f32[4,40,128]{2,1,0:T(8,128)S(1)}, u32[]{:S(2)}, u32[]{:S(2)}) collective-permute-start(f32[4,40,128]{2,1,0:T(8,128)S(1)} %shard_map.126), channel_id=1, source_target_pairs={{0,1},{1,0},{2,3},{3,2},{4,8},{5,9},{6,10},{7,11},{8,4},{9,5},{10,... | collective-permute-start | bytes 245768 | tf_op jit(solution)/shard_map/ppermute | solution.py:534
  16.5 3.6 %collective-permute-start.10 = (f32[4,40,128]{2,1,0:T(8,128)S(1)}, f32[4,40,128]{2,1,0:T(8,128)S(1)}, u32[]{:S(2)}, u32[]{:S(2)}) collective-permute-start(f32[4,40,128]{2,1,0:T(8,128)S(1)} %shard_map.124), channel_id=1, source_target_pairs={{0,1},{1,0},{2,3},{3,2},{4,8},{5,9},{6,10},{7,11},{8,4},{9,5},{10,... | collective-permute-start | bytes 245768 | tf_op jit(solution)/shard_map/ppermute | solution.py:534
  17.4 2.8 %collective-permute-start.5 = (f32[4,40,128]{2,1,0:T(8,128)S(1)}, f32[4,40,128]{2,1,0:T(8,128)S(1)}, u32[]{:S(2)}, u32[]{:S(2)}) collective-permute-start(f32[4,40,128]{2,1,0:T(8,128)S(1)} %shard_map.119), channel_id=1, source_target_pairs={{0,1},{1,0},{2,3},{3,2},{4,8},{5,9},{6,10},{7,11},{8,4},{9,5},{10,... | collective-permute-start | bytes 245768 | tf_op jit(solution)/shard_map/ppermute | solution.py:534
  18.3 2.5 %collective-permute-start.2 = (f32[4,40,128]{2,1,0:T(8,128)S(1)}, f32[4,40,128]{2,1,0:T(8,128)S(1)}, u32[]{:S(2)}, u32[]{:S(2)}) collective-permute-start(f32[4,40,128]{2,1,0:T(8,128)S(1)} %shard_map.117), channel_id=1, source_target_pairs={{0,1},{1,0},{2,3},{3,2},{4,8},{5,9},{6,10},{7,11},{8,4},{9,5},{10,... | collective-permute-start | bytes 245768 | tf_op jit(solution)/shard_map/ppermute | solution.py:534
  19.5 2.8 %collective-permute-start.14 = (f32[4,40,128]{2,1,0:T(8,128)S(1)}, f32[4,40,128]{2,1,0:T(8,128)S(1)}, u32[]{:S(2)}, u32[]{:S(2)}) collective-permute-start(f32[4,40,128]{2,1,0:T(8,128)S(1)} %shard_map.127), channel_id=1, source_target_pairs={{0,1},{1,0},{2,3},{3,2},{4,5},{5,4},{6,7},{7,6},{8,12},{9,13},{10,... | collective-permute-start | bytes 245768 | tf_op jit(solution)/shard_map/ppermute | solution.py:534
  20.1 2.3 %collective-permute-start.11 = (f32[4,40,128]{2,1,0:T(8,128)S(1)}, f32[4,40,128]{2,1,0:T(8,128)S(1)}, u32[]{:S(2)}, u32[]{:S(2)}) collective-permute-start(f32[4,40,128]{2,1,0:T(8,128)S(1)} %shard_map.125), channel_id=1, source_target_pairs={{0,1},{1,0},{2,3},{3,2},{4,5},{5,4},{6,7},{7,6},{8,12},{9,13},{10,... | collective-permute-start | bytes 245768 | tf_op jit(solution)/shard_map/ppermute | solution.py:534
  20.2 3.6 %collective-permute-start.6 = (f32[4,40,128]{2,1,0:T(8,128)S(1)}, f32[4,40,128]{2,1,0:T(8,128)S(1)}, u32[]{:S(2)}, u32[]{:S(2)}) collective-permute-start(f32[4,40,128]{2,1,0:T(8,128)S(1)} %shard_map.120), channel_id=1, source_target_pairs={{0,1},{1,0},{2,3},{3,2},{4,5},{5,4},{6,7},{7,6},{8,12},{9,13},{10,... | collective-permute-start | bytes 245768 | tf_op jit(solution)/shard_map/ppermute | solution.py:534
  20.8 3.0 %collective-permute-start.3 = (f32[4,40,128]{2,1,0:T(8,128)S(1)}, f32[4,40,128]{2,1,0:T(8,128)S(1)}, u32[]{:S(2)}, u32[]{:S(2)}) collective-permute-start(f32[4,40,128]{2,1,0:T(8,128)S(1)} %shard_map.118), channel_id=1, source_target_pairs={{0,1},{1,0},{2,3},{3,2},{4,5},{5,4},{6,7},{7,6},{8,12},{9,13},{10,... | collective-permute-start | bytes 245768 | tf_op jit(solution)/shard_map/ppermute | solution.py:534
  23.3 1.5 %collective-permute-start.15 = (f32[8,16,128]{2,1,0:T(8,128)S(1)}, f32[8,16,128]{2,1,0:T(8,128)S(1)}, u32[]{:S(2)}, u32[]{:S(2)}) collective-permute-start(f32[8,16,128]{2,1,0:T(8,128)S(1)} %shard_map.128), channel_id=1, source_target_pairs={{0,1},{1,0},{2,3},{3,2},{4,5},{5,4},{6,7},{7,6},{8,9},{9,8},{10,11... | collective-permute-start | bytes 196616 | tf_op jit(solution)/shard_map/ppermute | solution.py:627
  24.8 1.7 %collective-permute-start.7 = (f32[8,16,128]{2,1,0:T(8,128)S(1)}, f32[8,16,128]{2,1,0:T(8,128)S(1)}, u32[]{:S(2)}, u32[]{:S(2)}) collective-permute-start(f32[8,16,128]{2,1,0:T(8,128)S(1)} %shard_map.121), channel_id=1, source_target_pairs={{0,1},{1,0},{2,3},{3,2},{4,5},{5,4},{6,7},{7,6},{8,9},{9,8},{10,11... | collective-permute-start | bytes 196616 | tf_op jit(solution)/shard_map/ppermute | solution.py:627
  24.9 4.6 %collective-permute-start.16 = (f32[8,16,128]{2,1,0:T(8,128)S(1)}, f32[8,16,128]{2,1,0:T(8,128)S(1)}, u32[]{:S(2)}, u32[]{:S(2)}) collective-permute-start(f32[8,16,128]{2,1,0:T(8,128)S(1)} %add.25.refs_0_), channel_id=1, source_target_pairs={{0,2},{1,3},{2,0},{3,1},{4,6},{5,7},{6,4},{7,5},{8,10},{9,11},{10,... | collective-permute-start | bytes 196616 | tf_op jit(solution)/shard_map/ppermute | solution.py:629
  26.5 4.5 %collective-permute-start.8 = (f32[8,16,128]{2,1,0:T(8,128)S(1)}, f32[8,16,128]{2,1,0:T(8,128)S(1)}, u32[]{:S(2)}, u32[]{:S(2)}) collective-permute-start(f32[8,16,128]{2,1,0:T(8,128)S(1)} %add.24.refs_0_), channel_id=1, source_target_pairs={{0,2},{1,3},{2,0},{3,1},{4,6},{5,7},{6,4},{7,5},{8,10},{9,11},{10,... | collective-permute-start | bytes 196616 | tf_op jit(solution)/shard_map/ppermute | solution.py:629
  30.4 2.1 %collective-permute-start.26 = (f32[4,40,128]{2,1,0:T(8,128)S(1)}, f32[4,40,128]{2,1,0:T(8,128)S(1)}, u32[]{:S(2)}, u32[]{:S(2)}) collective-permute-start(f32[4,40,128]{2,1,0:T(8,128)S(1)} %get-tuple-element.50.carried_ref), channel_id=1, source_target_pairs={{0,1},{1,0},{2,3},{3,2},{4,5},{5,4},{6,7},{7,6},{8,12},{9,13},{10,... | collective-permute-start | bytes 245768 | tf_op jit(solution)/shard_map/ppermute | solution.py:534
  30.5 2.2 %collective-permute-start.23 = (f32[4,40,128]{2,1,0:T(8,128)S(1)}, f32[4,40,128]{2,1,0:T(8,128)S(1)}, u32[]{:S(2)}, u32[]{:S(2)}) collective-permute-start(f32[4,40,128]{2,1,0:T(8,128)S(1)} %get-tuple-element.49.carried_ref), channel_id=1, source_target_pairs={{0,1},{1,0},{2,3},{3,2},{4,5},{5,4},{6,7},{7,6},{8,12},{9,13},{10,... | collective-permute-start | bytes 245768 | tf_op jit(solution)/shard_map/ppermute | solution.py:534
  32.7 14.2 %collective-permute-start.24 = (f32[4,40,128]{2,1,0:T(8,128)S(1)}, f32[4,40,128]{2,1,0:T(8,128)S(1)}, u32[]{:S(2)}, u32[]{:S(2)}) collective-permute-start(f32[4,40,128]{2,1,0:T(8,128)S(1)} %shard_map.135), channel_id=1, source_target_pairs={{0,1},{1,0},{2,3},{3,2},{4,8},{5,9},{6,10},{7,11},{8,4},{9,5},{10,... | collective-permute-start | bytes 245768 | tf_op jit(solution)/shard_map/ppermute | solution.py:534
  33.3 14.6 %collective-permute-start.21 = (f32[4,40,128]{2,1,0:T(8,128)S(1)}, f32[4,40,128]{2,1,0:T(8,128)S(1)}, u32[]{:S(2)}, u32[]{:S(2)}) collective-permute-start(f32[4,40,128]{2,1,0:T(8,128)S(1)} %shard_map.133), channel_id=1, source_target_pairs={{0,1},{1,0},{2,3},{3,2},{4,8},{5,9},{6,10},{7,11},{8,4},{9,5},{10,... | collective-permute-start | bytes 245768 | tf_op jit(solution)/shard_map/ppermute | solution.py:534
  33.5 15.6 %collective-permute-start.18 = (f32[4,40,128]{2,1,0:T(8,128)S(1)}, f32[4,40,128]{2,1,0:T(8,128)S(1)}, u32[]{:S(2)}, u32[]{:S(2)}) collective-permute-start(f32[4,40,128]{2,1,0:T(8,128)S(1)} %shard_map.131), channel_id=1, source_target_pairs={{0,1},{1,0},{2,3},{3,2},{4,8},{5,9},{6,10},{7,11},{8,4},{9,5},{10,... | collective-permute-start | bytes 245768 | tf_op jit(solution)/shard_map/ppermute | solution.py:534
  34.0 16.9 %collective-permute-start.28 = (f32[4,40,128]{2,1,0:T(8,128)S(1)}, f32[4,40,128]{2,1,0:T(8,128)S(1)}, u32[]{:S(2)}, u32[]{:S(2)}) collective-permute-start(f32[4,40,128]{2,1,0:T(8,128)S(1)} %shard_map.138), channel_id=1, source_target_pairs={{0,4},{1,5},{2,6},{3,7},{4,0},{5,1},{6,2},{7,3},{8,9},{9,8},{10,11... | collective-permute-start | bytes 245768 | tf_op jit(solution)/shard_map/ppermute | solution.py:534
  46.9 5.4 %collective-permute-start.25 = (f32[4,40,128]{2,1,0:T(8,128)S(1)}, f32[4,40,128]{2,1,0:T(8,128)S(1)}, u32[]{:S(2)}, u32[]{:S(2)}) collective-permute-start(f32[4,40,128]{2,1,0:T(8,128)S(1)} %shard_map.136), channel_id=1, source_target_pairs={{0,4},{1,5},{2,6},{3,7},{4,0},{5,1},{6,2},{7,3},{8,9},{9,8},{10,11... | collective-permute-start | bytes 245768 | tf_op jit(solution)/shard_map/ppermute | solution.py:534
  47.9 5.3 %collective-permute-start.22 = (f32[4,40,128]{2,1,0:T(8,128)S(1)}, f32[4,40,128]{2,1,0:T(8,128)S(1)}, u32[]{:S(2)}, u32[]{:S(2)}) collective-permute-start(f32[4,40,128]{2,1,0:T(8,128)S(1)} %shard_map.134), channel_id=1, source_target_pairs={{0,4},{1,5},{2,6},{3,7},{4,0},{5,1},{6,2},{7,3},{8,9},{9,8},{10,11... | collective-permute-start | bytes 245768 | tf_op jit(solution)/shard_map/ppermute | solution.py:534
  49.1 5.0 %collective-permute-start.19 = (f32[4,40,128]{2,1,0:T(8,128)S(1)}, f32[4,40,128]{2,1,0:T(8,128)S(1)}, u32[]{:S(2)}, u32[]{:S(2)}) collective-permute-start(f32[4,40,128]{2,1,0:T(8,128)S(1)} %shard_map.132), channel_id=1, source_target_pairs={{0,4},{1,5},{2,6},{3,7},{4,0},{5,1},{6,2},{7,3},{8,9},{9,8},{10,11... | collective-permute-start | bytes 245768 | tf_op jit(solution)/shard_map/ppermute | solution.py:534
  55.3 4.0 %collective-permute-start.29 = (f32[32,160]{1,0:T(8,128)S(1)}, f32[32,160]{1,0:T(8,128)S(1)}, u32[]{:S(2)}, u32[]{:S(2)}) collective-permute-start(f32[32,160]{1,0:T(8,128)S(1)} %get-tuple-element.52.refs_5_), channel_id=1, source_target_pairs={{0,16},{16,0},{1,17},{17,1},{2,18},{18,2},{3,19},{19,3},{4,20},{20... | collective-permute-start | bytes 61448 | tf_op jit(solution)/shard_map/ppermute | solution.py:507
  61.3 3.6 %collective-permute-start.31 = (f32[8,128]{1,0:T(8,128)S(1)}, f32[8,128]{1,0:T(8,128)S(1)}, u32[]{:S(2)}, u32[]{:S(2)}) collective-permute-start(f32[8,128]{1,0:T(8,128)S(1)} %add.26), channel_id=1, source_target_pairs={{0,2},{1,3},{2,0},{3,1},{4,6},{5,7},{6,4},{7,5},{8,10},{9,11},{10,... | collective-permute-start | bytes 12296 | tf_op jit(solution)/shard_map/ppermute | solution.py:545
  64.9 3.6 %collective-permute-start.32 = (f32[8,128]{1,0:T(8,128)S(1)}, f32[8,128]{1,0:T(8,128)S(1)}, u32[]{:S(2)}, u32[]{:S(2)}) collective-permute-start(f32[8,128]{1,0:T(8,128)S(1)} %add.27), channel_id=1, source_target_pairs={{0,16},{16,0},{1,17},{17,1},{2,18},{18,2},{3,19},{19,3},{4,20},{20... | collective-permute-start | bytes 12296 | tf_op jit(solution)/shard_map/ppermute | solution.py:545
  68.5 4.4 %collective-permute-start.33 = (f32[8,128]{1,0:T(8,128)S(1)}, f32[8,128]{1,0:T(8,128)S(1)}, u32[]{:S(2)}, u32[]{:S(2)}) collective-permute-start(f32[8,128]{1,0:T(8,128)S(1)} %add.28), channel_id=1, source_target_pairs={{0,4},{4,0},{8,12},{12,8},{1,5},{5,1},{9,13},{13,9},{2,6},{6,2},{1... | collective-permute-start | bytes 12296 | tf_op jit(solution)/shard_map/ppermute | solution.py:545
  69.6 4.5 %collective-permute-start.34 = (f32[8,128]{1,0:T(8,128)S(1)}, f32[8,128]{1,0:T(8,128)S(1)}, u32[]{:S(2)}, u32[]{:S(2)}) collective-permute-start(f32[8,128]{1,0:T(8,128)S(1)} %add.28), channel_id=1, source_target_pairs={{0,8},{4,12},{8,0},{12,4},{1,9},{5,13},{9,1},{13,5},{2,10},{6,14},... | collective-permute-start | bytes 12296 | tf_op jit(solution)/shard_map/ppermute | solution.py:545
  69.6 5.4 %collective-permute-start.35 = (f32[8,128]{1,0:T(8,128)S(1)}, f32[8,128]{1,0:T(8,128)S(1)}, u32[]{:S(2)}, u32[]{:S(2)}) collective-permute-start(f32[8,128]{1,0:T(8,128)S(1)} %add.28), channel_id=1, source_target_pairs={{0,12},{4,8},{8,4},{12,0},{1,13},{5,9},{9,5},{13,1},{2,14},{6,10},... | collective-permute-start | bytes 12296 | tf_op jit(solution)/shard_map/ppermute | solution.py:545
  (11 other events, 55.1 us)
where the time goes:
time: 76.6 us; the launch traced here: 76.5 us
  starting transfers between devices  40.1 us (52%)
  waiting for transfers between devices  21 us (27%)
  Pallas kernels  13 us (17%)
  between operations  0.97 us (1%)
    ppermute x24, starting transfers between devices, lat_carry(): got[c][i].append(lax.ppermute(v, ('lat', 'mem'), pairs))  24.7 us
    pallas_call x30, Pallas kernels, call(): pl.pallas_call(body, out_shape=outs, in_specs=specs or [VM] * len(ins), o...  13 us
    ppermute x24, waiting for transfers between devices, lat_carry(): got[c][i].append(lax.ppermute(v, ('lat', 'mem'), pairs))  8.01 us
    ppermute x6, waiting for transfers between devices, all_sum(): lax.ppermute(v, axes, [(i, i ^ m) for i in range(total)])  7.5 us
    ppermute x6, starting transfers between devices, all_sum(): lax.ppermute(v, axes, [(i, i ^ m) for i in range(total)])  7.4 us
    ppermute x2, starting transfers between devices, lon_exchange(): lax.ppermute(carried, 'lon', [(j, (j + sign * r) % n) for j in range(n)])  4.54 us
    ppermute x2, waiting for transfers between devices, lon_exchange(): lax.ppermute(carried, 'lon', [(j, (j + sign * r) % n) for j in range(n)])  4.32 us
    ppermute x2, starting transfers between devices, iteration(): other = lax.ppermute(v, 'mem', [(i, i ^ step) for i in range(n_mem)])  2.79 us
  transfers between devices with their start and end apart: 36, of which 16 were waited for; matrix products, arithmetic and copies ran while one was open for 0% of the time, Pallas kernels for 10%

commit v1 on v0

--- a/solution.py
+++ b/solution.py
@@ -170,7 +170,10 @@
             store(y, at, i * block, u3, u if y == order[-1] else None)
         return carry
 
-    lax.fori_loop(0, k // block, step, 0)
+    if k == block:
+        step(0, 0)
+    else:
+        lax.fori_loop(0, k // block, step, 0)
 
 
 def swap_halves(a, b):
@@ -192,22 +195,28 @@
 
 def entering_states(got, chunks, block):
     hops = len(got) // chunks
-    mine = [block == float(h + 1) for h in range(hops)]
+    mine = [block[:1] == float(h + 1) for h in range(hops)]
 
     def at(chunk, where):
         out = []
         for s in range(4):
-            v = jnp.zeros(block.shape, f32)
+            v = None
             for m, p in zip(mine, got[chunk * hops : (chunk + 1) * hops]):
-                v = jnp.where(m, p[s, where, :], v)
+                new = p[s, where, :]
+                v = jnp.where(m, new, jnp.zeros_like(new) if v is None else v)
             out.append(v)
         return out
 
     return at
 
 
+def rows_at_once(size):
+    return 40 if size % 40 == 0 else 8
+
+
 def sweep_chunks(load, store, start, dec, rows, k, chunks, backward):
     size = k // chunks
+    block = rows_at_once(size)
     for ch in range(chunks):
         lat_sweep(
             lambda y, at, base, ch=ch: load(y, ch * size + base),
@@ -217,7 +226,7 @@
             rows,
             size,
             backward,
-            8,
+            block,
         )
 
 
@@ -310,7 +319,6 @@
     for y in range(rows):
         row = inside_ref[y] + added(y)
         f_refs[0][y], f_refs[1][y] = swap_halves(row[:half], row[half:])
-    zero = jnp.zeros((8, cells), f32)
     for part, f_ref in enumerate(f_refs):
 
         def store(y, ch, at, base, value, last, part=part):
@@ -319,9 +327,9 @@
                     out_refs[part * chunks + ch][s, at, :] = last[s]
 
         sweep_chunks(
-            lambda y, base: f_ref[y, pl.ds(pl.multiple_of(base, 8), 8), :],
+            lambda y, base: f_ref[y, pl.ds(pl.multiple_of(base, 8), rows_at_once(half // chunks)), :],
             store,
-            lambda ch, at: [zero] * 4,
+            lambda ch, at: [jnp.zeros((1, cells), f32)] * 4,
             lat_ref[part, :1],
             rows,
             half,
@@ -346,11 +354,11 @@
     cells = lat_ref.shape[-1]
 
     def store(y, ch, at, base, value, last):
-        where = pl.ds(pl.multiple_of(base, 8), 8)
+        where = pl.ds(pl.multiple_of(base, 8), rows_at_once(k // chunks))
         s_ref[y, where, :] = value * mask_ref[where, :]
 
     sweep_chunks(
-        lambda y, base: f_ref[y, pl.ds(pl.multiple_of(base, 8), 8), :],
+        lambda y, base: f_ref[y, pl.ds(pl.multiple_of(base, 8), rows_at_once(k // chunks)), :],
         store,
         entering_states(rest[:count], chunks, block_ref[...]),
         lat_ref[part, :1],
@@ -385,7 +393,6 @@
         m = m_ref[y * apart : y * apart + size, :]
         weighted = (m.reshape(pairs, levels, cells) * w[None]).reshape(size, cells)
         g_ref[y] = product3(modes_ref[...], right3(weighted, 0)) * mask_ref[...]
-    zero8 = jnp.zeros((8, cells), f32)
 
     def store(y, ch, at, base, value, last):
         if last is not None:
@@ -393,9 +400,9 @@
                 carried_refs[ch][s, at, :] = last[s]
 
     sweep_chunks(
-        lambda y, base: g_ref[y, pl.ds(pl.multiple_of(base, 8), 8), :],
+        lambda y, base: g_ref[y, pl.ds(pl.multiple_of(base, 8), rows_at_once(k // chunks)), :],
         store,
-        lambda ch, at: [zero8] * 4,
+        lambda ch, at: [jnp.zeros((1, cells), f32)] * 4,
         lat_ref[part, :1],
         rows,
         k,
@@ -413,10 +420,10 @@
         g_ref = g_refs[part]
 
         def store(y, ch, at, base, value, last, part=part):
-            p_ref[part, y, pl.ds(pl.multiple_of(base, 8), 8), :] = value
+            p_ref[part, y, pl.ds(pl.multiple_of(base, 8), rows_at_once(half // chunks)), :] = value
 
         sweep_chunks(
-            lambda y, base: g_ref[y, pl.ds(pl.multiple_of(base, 8), 8), :],
+            lambda y, base: g_ref[y, pl.ds(pl.multiple_of(base, 8), rows_at_once(half // chunks)), :],
             store,
             entering_states(rest[part * count : (part + 1) * count], chunks, block),
             lat_ref[part, :1],

time: 76.6 us -> 75.4 us (0.984)
  Pallas kernels: 13 us -> 11.5 us
    pallas_call x30, Pallas kernels: 13 us -> 11.5 us  [call(): pl.pallas_call(body, out_shape=outs, in_specs=specs or [VM] * len(ins), o...]
  transfers between devices with their start and end apart: 36 -> 36, of which waited for: 16 -> 18; matrix products, arithmetic and copies ran while one was open for 0% -> 0% of each run, Pallas kernels for 10% -> 9%
where the time goes in v1:
time: 75.4 us; the launch traced here: 75.2 us
  starting transfers between devices  40.2 us (53%)
  waiting for transfers between devices  21.1 us (28%)
  Pallas kernels  11.5 us (15%)
  between operations  0.97 us (1%)
    ppermute x24, starting transfers between devices, lat_carry(): got[c][i].append(lax.ppermute(v, ('lat', 'mem'), pairs))  25 us
    pallas_call x30, Pallas kernels, call(): pl.pallas_call(body, out_shape=outs, in_specs=specs or [VM] * len(ins), o...  11.5 us
    ppermute x24, waiting for transfers between devices, lat_carry(): got[c][i].append(lax.ppermute(v, ('lat', 'mem'), pairs))  7.87 us
    ppermute x6, starting transfers between devices, all_sum(): lax.ppermute(v, axes, [(i, i ^ m) for i in range(total)])  7.47 us
    ppermute x6, waiting for transfers between devices, all_sum(): lax.ppermute(v, axes, [(i, i ^ m) for i in range(total)])  7.43 us
    ppermute x2, starting transfers between devices, lon_exchange(): lax.ppermute(carried, 'lon', [(j, (j + sign * r) % n) for j in range(n)])  4.54 us
    ppermute x2, waiting for transfers between devices, lon_exchange(): lax.ppermute(carried, 'lon', [(j, (j + sign * r) % n) for j in range(n)])  4.32 us
    ppermute x2, starting transfers between devices, iteration(): other = lax.ppermute(v, 'mem', [(i, i ^ step) for i in range(n_mem)])  2.65 us
  transfers between devices with their start and end apart: 36, of which 18 were waited for; matrix products, arithmetic and copies ran while one was open for 0% of the time, Pallas kernels for 9%

profile of v1, /device:TPU:0, one launch (start us, length us, event | category | flops | bytes accessed | tf_op | source)
XLA Modules:
  0.0 75.2 jit_solution(298566578447408182)
XLA Ops:
  3.0 3.0 %collective-permute-start = (f32[32,160]{1,0:T(8,128)S(1)}, f32[32,160]{1,0:T(8,128)S(1)}, u32[]{:S(2)}, u32[]{:S(2)}) collective-permute-start(f32[32,160]{1,0:T(8,128)S(1)} %get-tuple-element.33.refs_4_), channel_id=1, source_target_pairs={{0,16},{16,0},{1,17},{17,1},{2,18},{18,2},{3,19},{19,3},{4,20},{20... | collective-permute-start | bytes 61448 | tf_op jit(solution)/shard_map/ppermute | solution.py:514
  6.0 1.9 %collective-permute-done.refs_3_ = f32[32,160]{1,0:T(8,128)S(1)} collective-permute-done((f32[32,160]{1,0:T(8,128)S(1)}, f32[32,160]{1,0:T(8,128)S(1)}, u32[]{:S(2)}, u32[]{:S(2)}) %collective-permute-start) | collective-permute-done | bytes 20512 | tf_op jit(solution)/shard_map/ppermute | solution.py:514
  8.6 2.2 %collective-permute-start.12 = (f32[4,40,128]{2,1,0:T(8,128)S(1)}, f32[4,40,128]{2,1,0:T(8,128)S(1)}, u32[]{:S(2)}, u32[]{:S(2)}) collective-permute-start(f32[4,40,128]{2,1,0:T(8,128)S(1)} %get-tuple-element.45.carried_ref), channel_id=1, source_target_pairs={{0,4},{1,5},{2,6},{3,7},{4,0},{5,1},{6,2},{7,3},{8,9},{9,8},{10,11... | collective-permute-start | bytes 245768 | tf_op jit(solution)/shard_map/ppermute | solution.py:541
  10.8 1.9 %collective-permute-start.4 = (f32[4,40,128]{2,1,0:T(8,128)S(1)}, f32[4,40,128]{2,1,0:T(8,128)S(1)}, u32[]{:S(2)}, u32[]{:S(2)}) collective-permute-start(f32[4,40,128]{2,1,0:T(8,128)S(1)} %get-tuple-element.40.carried_ref), channel_id=1, source_target_pairs={{0,4},{1,5},{2,6},{3,7},{4,0},{5,1},{6,2},{7,3},{8,9},{9,8},{10,11... | collective-permute-start | bytes 245768 | tf_op jit(solution)/shard_map/ppermute | solution.py:541
  12.8 1.2 %collective-permute-done.12.got_ref.refs_9_ = f32[4,40,128]{2,1,0:T(8,128)S(1)} collective-permute-done((f32[4,40,128]{2,1,0:T(8,128)S(1)}, f32[4,40,128]{2,1,0:T(8,128)S(1)}, u32[]{:S(2)}, u32[]{:S(2)}) %collective-permute-start.12) | collective-permute-done | bytes 81952 | tf_op jit(solution)/shard_map/ppermute | solution.py:541
  14.1 1.9 %collective-permute-done.9.got_ref.refs_6_ = f32[4,40,128]{2,1,0:T(8,128)S(1)} collective-permute-done((f32[4,40,128]{2,1,0:T(8,128)S(1)}, f32[4,40,128]{2,1,0:T(8,128)S(1)}, u32[]{:S(2)}, u32[]{:S(2)}) %collective-permute-start.9) | collective-permute-done | bytes 81952 | tf_op jit(solution)/shard_map/ppermute | solution.py:541
  16.2 0.8 %collective-permute-done.4.got_ref.refs_9_ = f32[4,40,128]{2,1,0:T(8,128)S(1)} collective-permute-done((f32[4,40,128]{2,1,0:T(8,128)S(1)}, f32[4,40,128]{2,1,0:T(8,128)S(1)}, u32[]{:S(2)}, u32[]{:S(2)}) %collective-permute-start.4) | collective-permute-done | bytes 81952 | tf_op jit(solution)/shard_map/ppermute | solution.py:541
  18.0 1.1 %shard_map.115 = (f32[2624,128]{1,0:T(8,128)S(1)}, f32[2624,128]{1,0:T(8,128)S(1)}) custom-call(bf16[20,32,8,128]{3,2,1,0:T(8,128)(2,1)S(1)} %copy-done.4), custom_call_target="tpu_custom_call" | custom-call | flops 1000000000 | bytes 1000 | tf_op jit(solution)/shard_map/pallas_call | solution.py:495
  20.5 1.4 %shard_map.116 = (f32[80,128]{1,0:T(8,128)S(1)}, bf16[320,240]{1,0:T(8,128)(2,1)S(1)}) custom-call(f32[8,32]{1,0:T(8,128)S(1)} %copy-done.5, s32[20]{0:T(128)S(1)} %copy-done.6), custom_call_target="tpu_custom_call" | custom-call | flops 1000000000 | bytes 1000 | tf_op jit(solution)/shard_map/pallas_call | solution.py:495
  24.1 1.6 %collective-permute-start.16 = (f32[8,16,128]{2,1,0:T(8,128)S(1)}, f32[8,16,128]{2,1,0:T(8,128)S(1)}, u32[]{:S(2)}, u32[]{:S(2)}) collective-permute-start(f32[8,16,128]{2,1,0:T(8,128)S(1)} %add.25.refs_0_), channel_id=1, source_target_pairs={{0,2},{1,3},{2,0},{3,1},{4,6},{5,7},{6,4},{7,5},{8,10},{9,11},{10,... | collective-permute-start | bytes 196616 | tf_op jit(solution)/shard_map/ppermute | solution.py:636
  25.7 1.1 %collective-permute-start.8 = (f32[8,16,128]{2,1,0:T(8,128)S(1)}, f32[8,16,128]{2,1,0:T(8,128)S(1)}, u32[]{:S(2)}, u32[]{:S(2)}) collective-permute-start(f32[8,16,128]{2,1,0:T(8,128)S(1)} %add.24.refs_0_), channel_id=1, source_target_pairs={{0,2},{1,3},{2,0},{3,1},{4,6},{5,7},{6,4},{7,5},{8,10},{9,11},{10,... | collective-permute-start | bytes 196616 | tf_op jit(solution)/shard_map/ppermute | solution.py:636
  27.4 1.2 %collective-permute-done.16.refs_1_ = f32[8,16,128]{2,1,0:T(8,128)S(1)} collective-permute-done((f32[8,16,128]{2,1,0:T(8,128)S(1)}, f32[8,16,128]{2,1,0:T(8,128)S(1)}, u32[]{:S(2)}, u32[]{:S(2)}) %collective-permute-start.16) | collective-permute-done | bytes 65568 | tf_op jit(solution)/shard_map/ppermute | solution.py:636
  32.9 13.2 %collective-permute-start.28 = (f32[4,40,128]{2,1,0:T(8,128)S(1)}, f32[4,40,128]{2,1,0:T(8,128)S(1)}, u32[]{:S(2)}, u32[]{:S(2)}) collective-permute-start(f32[4,40,128]{2,1,0:T(8,128)S(1)} %shard_map.138), channel_id=1, source_target_pairs={{0,4},{1,5},{2,6},{3,7},{4,0},{5,1},{6,2},{7,3},{8,9},{9,8},{10,11... | collective-permute-start | bytes 245768 | tf_op jit(solution)/shard_map/ppermute | solution.py:541
  46.1 1.4 %collective-permute-start.25 = (f32[4,40,128]{2,1,0:T(8,128)S(1)}, f32[4,40,128]{2,1,0:T(8,128)S(1)}, u32[]{:S(2)}, u32[]{:S(2)}) collective-permute-start(f32[4,40,128]{2,1,0:T(8,128)S(1)} %shard_map.136), channel_id=1, source_target_pairs={{0,4},{1,5},{2,6},{3,7},{4,0},{5,1},{6,2},{7,3},{8,9},{9,8},{10,11... | collective-permute-start | bytes 245768 | tf_op jit(solution)/shard_map/ppermute | solution.py:541
  47.5 0.9 %collective-permute-start.22 = (f32[4,40,128]{2,1,0:T(8,128)S(1)}, f32[4,40,128]{2,1,0:T(8,128)S(1)}, u32[]{:S(2)}, u32[]{:S(2)}) collective-permute-start(f32[4,40,128]{2,1,0:T(8,128)S(1)} %shard_map.134), channel_id=1, source_target_pairs={{0,4},{1,5},{2,6},{3,7},{4,0},{5,1},{6,2},{7,3},{8,9},{9,8},{10,11... | collective-permute-start | bytes 245768 | tf_op jit(solution)/shard_map/ppermute | solution.py:541
  48.4 1.3 %collective-permute-start.19 = (f32[4,40,128]{2,1,0:T(8,128)S(1)}, f32[4,40,128]{2,1,0:T(8,128)S(1)}, u32[]{:S(2)}, u32[]{:S(2)}) collective-permute-start(f32[4,40,128]{2,1,0:T(8,128)S(1)} %shard_map.132), channel_id=1, source_target_pairs={{0,4},{1,5},{2,6},{3,7},{4,0},{5,1},{6,2},{7,3},{8,9},{9,8},{10,11... | collective-permute-start | bytes 245768 | tf_op jit(solution)/shard_map/ppermute | solution.py:541
  50.1 1.3 %collective-permute-done.25.refs_13_ = f32[4,40,128]{2,1,0:T(8,128)S(1)} collective-permute-done((f32[4,40,128]{2,1,0:T(8,128)S(1)}, f32[4,40,128]{2,1,0:T(8,128)S(1)}, u32[]{:S(2)}, u32[]{:S(2)}) %collective-permute-start.25) | collective-permute-done | bytes 81952 | tf_op jit(solution)/shard_map/ppermute | solution.py:541
  51.4 0.9 %collective-permute-done.22.refs_10_ = f32[4,40,128]{2,1,0:T(8,128)S(1)} collective-permute-done((f32[4,40,128]{2,1,0:T(8,128)S(1)}, f32[4,40,128]{2,1,0:T(8,128)S(1)}, u32[]{:S(2)}, u32[]{:S(2)}) %collective-permute-start.22) | collective-permute-done | bytes 81952 | tf_op jit(solution)/shard_map/ppermute | solution.py:541
  52.3 0.9 %collective-permute-done.19.refs_7_ = f32[4,40,128]{2,1,0:T(8,128)S(1)} collective-permute-done((f32[4,40,128]{2,1,0:T(8,128)S(1)}, f32[4,40,128]{2,1,0:T(8,128)S(1)}, u32[]{:S(2)}, u32[]{:S(2)}) %collective-permute-start.19) | collective-permute-done | bytes 81952 | tf_op jit(solution)/shard_map/ppermute | solution.py:541
  53.2 0.9 %shard_map.139 = (f32[8,160,128]{2,1,0:T(8,128)S(1)}, f32[32,160]{1,0:T(8,128)S(1)}) custom-call(f32[8,80,128]{2,1,0:T(8,128)S(1)} %get-tuple-element.41.refs_0_, f32[8,80,128]{2,1,0:T(8,128)S(1)} %get-tuple-element.46.refs_1_, f32[2,8,128]{2,1,0:T(8,128)S(1)} %get-tuple-element.32.refs_2_.lat_ref.refs_1_.refs_6_, ...), custom_call_target="tpu_custom_call" | custom-call | tf_op jit(solution)/shard_map/pallas_call | solution.py:495
  54.1 1.5 %collective-permute-start.29 = (f32[32,160]{1,0:T(8,128)S(1)}, f32[32,160]{1,0:T(8,128)S(1)}, u32[]{:S(2)}, u32[]{:S(2)}) collective-permute-start(f32[32,160]{1,0:T(8,128)S(1)} %get-tuple-element.52.refs_5_), channel_id=1, source_target_pairs={{0,16},{16,0},{1,17},{17,1},{2,18},{18,2},{3,19},{19,3},{4,20},{20... | collective-permute-start | bytes 61448 | tf_op jit(solution)/shard_map/ppermute | solution.py:514
  55.6 2.4 %collective-permute-done.29.refs_4_ = f32[32,160]{1,0:T(8,128)S(1)} collective-permute-done((f32[32,160]{1,0:T(8,128)S(1)}, f32[32,160]{1,0:T(8,128)S(1)}, u32[]{:S(2)}, u32[]{:S(2)}) %collective-permute-start.29) | collective-permute-done | bytes 20512 | tf_op jit(solution)/shard_map/ppermute | solution.py:514
  58.9 1.2 %collective-permute-done.30 = f32[8,128]{1,0:T(8,128)S(1)} collective-permute-done((f32[8,128]{1,0:T(8,128)S(1)}, f32[8,128]{1,0:T(8,128)S(1)}, u32[]{:S(2)}, u32[]{:S(2)}) %collective-permute-start.30) | collective-permute-done | bytes 4128 | tf_op jit(solution)/shard_map/ppermute | solution.py:552
  60.0 1.5 %collective-permute-start.31 = (f32[8,128]{1,0:T(8,128)S(1)}, f32[8,128]{1,0:T(8,128)S(1)}, u32[]{:S(2)}, u32[]{:S(2)}) collective-permute-start(f32[8,128]{1,0:T(8,128)S(1)} %add.26), channel_id=1, source_target_pairs={{0,2},{1,3},{2,0},{3,1},{4,6},{5,7},{6,4},{7,5},{8,10},{9,11},{10,... | collective-permute-start | bytes 12296 | tf_op jit(solution)/shard_map/ppermute | solution.py:552
  61.5 2.1 %collective-permute-done.31 = f32[8,128]{1,0:T(8,128)S(1)} collective-permute-done((f32[8,128]{1,0:T(8,128)S(1)}, f32[8,128]{1,0:T(8,128)S(1)}, u32[]{:S(2)}, u32[]{:S(2)}) %collective-permute-start.31) | collective-permute-done | bytes 4128 | tf_op jit(solution)/shard_map/ppermute | solution.py:552
  63.6 1.5 %collective-permute-start.32 = (f32[8,128]{1,0:T(8,128)S(1)}, f32[8,128]{1,0:T(8,128)S(1)}, u32[]{:S(2)}, u32[]{:S(2)}) collective-permute-start(f32[8,128]{1,0:T(8,128)S(1)} %add.27), channel_id=1, source_target_pairs={{0,16},{16,0},{1,17},{17,1},{2,18},{18,2},{3,19},{19,3},{4,20},{20... | collective-permute-start | bytes 12296 | tf_op jit(solution)/shard_map/ppermute | solution.py:552
  65.1 2.1 %collective-permute-done.32 = f32[8,128]{1,0:T(8,128)S(1)} collective-permute-done((f32[8,128]{1,0:T(8,128)S(1)}, f32[8,128]{1,0:T(8,128)S(1)}, u32[]{:S(2)}, u32[]{:S(2)}) %collective-permute-start.32) | collective-permute-done | bytes 4128 | tf_op jit(solution)/shard_map/ppermute | solution.py:552
  67.3 1.1 %collective-permute-start.33 = (f32[8,128]{1,0:T(8,128)S(1)}, f32[8,128]{1,0:T(8,128)S(1)}, u32[]{:S(2)}, u32[]{:S(2)}) collective-permute-start(f32[8,128]{1,0:T(8,128)S(1)} %add.28), channel_id=1, source_target_pairs={{0,4},{4,0},{8,12},{12,8},{1,5},{5,1},{9,13},{13,9},{2,6},{6,2},{1... | collective-permute-start | bytes 12296 | tf_op jit(solution)/shard_map/ppermute | solution.py:552
  68.3 3.3 %collective-permute-start.35 = (f32[8,128]{1,0:T(8,128)S(1)}, f32[8,128]{1,0:T(8,128)S(1)}, u32[]{:S(2)}, u32[]{:S(2)}) collective-permute-start(f32[8,128]{1,0:T(8,128)S(1)} %add.28), channel_id=1, source_target_pairs={{0,12},{4,8},{8,4},{12,0},{1,13},{5,9},{9,5},{13,1},{2,14},{6,10},... | collective-permute-start | bytes 12296 | tf_op jit(solution)/shard_map/ppermute | solution.py:552
  71.6 1.2 %collective-permute-done.34 = f32[8,128]{1,0:T(8,128)S(1)} collective-permute-done((f32[8,128]{1,0:T(8,128)S(1)}, f32[8,128]{1,0:T(8,128)S(1)}, u32[]{:S(2)}, u32[]{:S(2)}) %collective-permute-start.34) | collective-permute-done | bytes 4128 | tf_op jit(solution)/shard_map/ppermute | solution.py:552
  72.8 0.9 %collective-permute-done.35 = f32[8,128]{1,0:T(8,128)S(1)} collective-permute-done((f32[8,128]{1,0:T(8,128)S(1)}, f32[8,128]{1,0:T(8,128)S(1)}, u32[]{:S(2)}, u32[]{:S(2)}) %collective-permute-start.35) | collective-permute-done | bytes 4128 | tf_op jit(solution)/shard_map/ppermute | solution.py:552
  73.7 1.5 %shard_map.141 = (f32[160,8,128]{2,1,0:T(8,128)}, f32[160,8,128]{2,1,0:T(8,128)}, f32[160,8,128]{2,1,0:T(8,128)}) custom-call(f32[8,128]{1,0:T(8,128)S(1)} %add_add_fusion.sums_ref, f32[160,8,128]{2,1,0:T(8,128)S(1)} %copy-done.2, f32[160,8,128]{2,1,0:T(8,128)S(1)} %copy-done.1, f32[160,8,128]{2,1,0:T(8,128)S(1)} %copy-done, f32[160,8,128]{2,1,0:T(8,128)S(1)} %bitcast.2), custom_call_target="tpu_custom_call" | custom-call | tf_op jit(solution)/shard_map/pallas_call | solution.py:495
  (91 shorter events, 14.0 us)
Async XLA Ops:
  3.0 4.9 %collective-permute-start = (f32[32,160]{1,0:T(8,128)S(1)}, f32[32,160]{1,0:T(8,128)S(1)}, u32[]{:S(2)}, u32[]{:S(2)}) collective-permute-start(f32[32,160]{1,0:T(8,128)S(1)} %get-tuple-element.33.refs_4_), channel_id=1, source_target_pairs={{0,16},{16,0},{1,17},{17,1},{2,18},{18,2},{3,19},{19,3},{4,20},{20... | collective-permute-start | bytes 61448 | tf_op jit(solution)/shard_map/ppermute | solution.py:514
  8.6 5.5 %collective-permute-start.12 = (f32[4,40,128]{2,1,0:T(8,128)S(1)}, f32[4,40,128]{2,1,0:T(8,128)S(1)}, u32[]{:S(2)}, u32[]{:S(2)}) collective-permute-start(f32[4,40,128]{2,1,0:T(8,128)S(1)} %get-tuple-element.45.carried_ref), channel_id=1, source_target_pairs={{0,4},{1,5},{2,6},{3,7},{4,0},{5,1},{6,2},{7,3},{8,9},{9,8},{10,11... | collective-permute-start | bytes 245768 | tf_op jit(solution)/shard_map/ppermute | solution.py:541
  10.7 5.3 %collective-permute-start.9 = (f32[4,40,128]{2,1,0:T(8,128)S(1)}, f32[4,40,128]{2,1,0:T(8,128)S(1)}, u32[]{:S(2)}, u32[]{:S(2)}) collective-permute-start(f32[4,40,128]{2,1,0:T(8,128)S(1)} %get-tuple-element.44.carried_ref), channel_id=1, source_target_pairs={{0,4},{1,5},{2,6},{3,7},{4,0},{5,1},{6,2},{7,3},{8,9},{9,8},{10,11... | collective-permute-start | bytes 245768 | tf_op jit(solution)/shard_map/ppermute | solution.py:541
  10.8 6.2 %collective-permute-start.4 = (f32[4,40,128]{2,1,0:T(8,128)S(1)}, f32[4,40,128]{2,1,0:T(8,128)S(1)}, u32[]{:S(2)}, u32[]{:S(2)}) collective-permute-start(f32[4,40,128]{2,1,0:T(8,128)S(1)} %get-tuple-element.40.carried_ref), channel_id=1, source_target_pairs={{0,4},{1,5},{2,6},{3,7},{4,0},{5,1},{6,2},{7,3},{8,9},{9,8},{10,11... | collective-permute-start | bytes 245768 | tf_op jit(solution)/shard_map/ppermute | solution.py:541
  12.8 5.1 %collective-permute-start.1 = (f32[4,40,128]{2,1,0:T(8,128)S(1)}, f32[4,40,128]{2,1,0:T(8,128)S(1)}, u32[]{:S(2)}, u32[]{:S(2)}) collective-permute-start(f32[4,40,128]{2,1,0:T(8,128)S(1)} %get-tuple-element.39.carried_ref), channel_id=1, source_target_pairs={{0,4},{1,5},{2,6},{3,7},{4,0},{5,1},{6,2},{7,3},{8,9},{9,8},{10,11... | collective-permute-start | bytes 245768 | tf_op jit(solution)/shard_map/ppermute | solution.py:541
  14.1 5.0 %collective-permute-start.13 = (f32[4,40,128]{2,1,0:T(8,128)S(1)}, f32[4,40,128]{2,1,0:T(8,128)S(1)}, u32[]{:S(2)}, u32[]{:S(2)}) collective-permute-start(f32[4,40,128]{2,1,0:T(8,128)S(1)} %shard_map.126), channel_id=1, source_target_pairs={{0,1},{1,0},{2,3},{3,2},{4,8},{5,9},{6,10},{7,11},{8,4},{9,5},{10,... | collective-permute-start | bytes 245768 | tf_op jit(solution)/shard_map/ppermute | solution.py:541
  16.1 3.6 %collective-permute-start.10 = (f32[4,40,128]{2,1,0:T(8,128)S(1)}, f32[4,40,128]{2,1,0:T(8,128)S(1)}, u32[]{:S(2)}, u32[]{:S(2)}) collective-permute-start(f32[4,40,128]{2,1,0:T(8,128)S(1)} %shard_map.124), channel_id=1, source_target_pairs={{0,1},{1,0},{2,3},{3,2},{4,8},{5,9},{6,10},{7,11},{8,4},{9,5},{10,... | collective-permute-start | bytes 245768 | tf_op jit(solution)/shard_map/ppermute | solution.py:541
  17.0 2.8 %collective-permute-start.5 = (f32[4,40,128]{2,1,0:T(8,128)S(1)}, f32[4,40,128]{2,1,0:T(8,128)S(1)}, u32[]{:S(2)}, u32[]{:S(2)}) collective-permute-start(f32[4,40,128]{2,1,0:T(8,128)S(1)} %shard_map.119), channel_id=1, source_target_pairs={{0,1},{1,0},{2,3},{3,2},{4,8},{5,9},{6,10},{7,11},{8,4},{9,5},{10,... | collective-permute-start | bytes 245768 | tf_op jit(solution)/shard_map/ppermute | solution.py:541
  17.9 2.5 %collective-permute-start.2 = (f32[4,40,128]{2,1,0:T(8,128)S(1)}, f32[4,40,128]{2,1,0:T(8,128)S(1)}, u32[]{:S(2)}, u32[]{:S(2)}) collective-permute-start(f32[4,40,128]{2,1,0:T(8,128)S(1)} %shard_map.117), channel_id=1, source_target_pairs={{0,1},{1,0},{2,3},{3,2},{4,8},{5,9},{6,10},{7,11},{8,4},{9,5},{10,... | collective-permute-start | bytes 245768 | tf_op jit(solution)/shard_map/ppermute | solution.py:541
  19.1 2.8 %collective-permute-start.14 = (f32[4,40,128]{2,1,0:T(8,128)S(1)}, f32[4,40,128]{2,1,0:T(8,128)S(1)}, u32[]{:S(2)}, u32[]{:S(2)}) collective-permute-start(f32[4,40,128]{2,1,0:T(8,128)S(1)} %shard_map.127), channel_id=1, source_target_pairs={{0,1},{1,0},{2,3},{3,2},{4,5},{5,4},{6,7},{7,6},{8,12},{9,13},{10,... | collective-permute-start | bytes 245768 | tf_op jit(solution)/shard_map/ppermute | solution.py:541
  19.7 2.3 %collective-permute-start.11 = (f32[4,40,128]{2,1,0:T(8,128)S(1)}, f32[4,40,128]{2,1,0:T(8,128)S(1)}, u32[]{:S(2)}, u32[]{:S(2)}) collective-permute-start(f32[4,40,128]{2,1,0:T(8,128)S(1)} %shard_map.125), channel_id=1, source_target_pairs={{0,1},{1,0},{2,3},{3,2},{4,5},{5,4},{6,7},{7,6},{8,12},{9,13},{10,... | collective-permute-start | bytes 245768 | tf_op jit(solution)/shard_map/ppermute | solution.py:541
  19.8 3.4 %collective-permute-start.6 = (f32[4,40,128]{2,1,0:T(8,128)S(1)}, f32[4,40,128]{2,1,0:T(8,128)S(1)}, u32[]{:S(2)}, u32[]{:S(2)}) collective-permute-start(f32[4,40,128]{2,1,0:T(8,128)S(1)} %shard_map.120), channel_id=1, source_target_pairs={{0,1},{1,0},{2,3},{3,2},{4,5},{5,4},{6,7},{7,6},{8,12},{9,13},{10,... | collective-permute-start | bytes 245768 | tf_op jit(solution)/shard_map/ppermute | solution.py:541
  20.4 2.8 %collective-permute-start.3 = (f32[4,40,128]{2,1,0:T(8,128)S(1)}, f32[4,40,128]{2,1,0:T(8,128)S(1)}, u32[]{:S(2)}, u32[]{:S(2)}) collective-permute-start(f32[4,40,128]{2,1,0:T(8,128)S(1)} %shard_map.118), channel_id=1, source_target_pairs={{0,1},{1,0},{2,3},{3,2},{4,5},{5,4},{6,7},{7,6},{8,12},{9,13},{10,... | collective-permute-start | bytes 245768 | tf_op jit(solution)/shard_map/ppermute | solution.py:541
  23.9 1.8 %collective-permute-start.7 = (f32[8,16,128]{2,1,0:T(8,128)S(1)}, f32[8,16,128]{2,1,0:T(8,128)S(1)}, u32[]{:S(2)}, u32[]{:S(2)}) collective-permute-start(f32[8,16,128]{2,1,0:T(8,128)S(1)} %shard_map.121), channel_id=1, source_target_pairs={{0,1},{1,0},{2,3},{3,2},{4,5},{5,4},{6,7},{7,6},{8,9},{9,8},{10,11... | collective-permute-start | bytes 196616 | tf_op jit(solution)/shard_map/ppermute | solution.py:634
  24.1 4.5 %collective-permute-start.16 = (f32[8,16,128]{2,1,0:T(8,128)S(1)}, f32[8,16,128]{2,1,0:T(8,128)S(1)}, u32[]{:S(2)}, u32[]{:S(2)}) collective-permute-start(f32[8,16,128]{2,1,0:T(8,128)S(1)} %add.25.refs_0_), channel_id=1, source_target_pairs={{0,2},{1,3},{2,0},{3,1},{4,6},{5,7},{6,4},{7,5},{8,10},{9,11},{10,... | collective-permute-start | bytes 196616 | tf_op jit(solution)/shard_map/ppermute | solution.py:636
  25.7 4.3 %collective-permute-start.8 = (f32[8,16,128]{2,1,0:T(8,128)S(1)}, f32[8,16,128]{2,1,0:T(8,128)S(1)}, u32[]{:S(2)}, u32[]{:S(2)}) collective-permute-start(f32[8,16,128]{2,1,0:T(8,128)S(1)} %add.24.refs_0_), channel_id=1, source_target_pairs={{0,2},{1,3},{2,0},{3,1},{4,6},{5,7},{6,4},{7,5},{8,10},{9,11},{10,... | collective-permute-start | bytes 196616 | tf_op jit(solution)/shard_map/ppermute | solution.py:636
  29.4 2.0 %collective-permute-start.26 = (f32[4,40,128]{2,1,0:T(8,128)S(1)}, f32[4,40,128]{2,1,0:T(8,128)S(1)}, u32[]{:S(2)}, u32[]{:S(2)}) collective-permute-start(f32[4,40,128]{2,1,0:T(8,128)S(1)} %get-tuple-element.50.carried_ref), channel_id=1, source_target_pairs={{0,1},{1,0},{2,3},{3,2},{4,5},{5,4},{6,7},{7,6},{8,12},{9,13},{10,... | collective-permute-start | bytes 245768 | tf_op jit(solution)/shard_map/ppermute | solution.py:541
  29.5 2.1 %collective-permute-start.23 = (f32[4,40,128]{2,1,0:T(8,128)S(1)}, f32[4,40,128]{2,1,0:T(8,128)S(1)}, u32[]{:S(2)}, u32[]{:S(2)}) collective-permute-start(f32[4,40,128]{2,1,0:T(8,128)S(1)} %get-tuple-element.49.carried_ref), channel_id=1, source_target_pairs={{0,1},{1,0},{2,3},{3,2},{4,5},{5,4},{6,7},{7,6},{8,12},{9,13},{10,... | collective-permute-start | bytes 245768 | tf_op jit(solution)/shard_map/ppermute | solution.py:541
  30.9 1.5 %collective-permute-start.17 = (f32[4,40,128]{2,1,0:T(8,128)S(1)}, f32[4,40,128]{2,1,0:T(8,128)S(1)}, u32[]{:S(2)}, u32[]{:S(2)}) collective-permute-start(f32[4,40,128]{2,1,0:T(8,128)S(1)} %get-tuple-element.47.carried_ref), channel_id=1, source_target_pairs={{0,1},{1,0},{2,3},{3,2},{4,5},{5,4},{6,7},{7,6},{8,12},{9,13},{10,... | collective-permute-start | bytes 245768 | tf_op jit(solution)/shard_map/ppermute | solution.py:541
  31.6 14.5 %collective-permute-start.24 = (f32[4,40,128]{2,1,0:T(8,128)S(1)}, f32[4,40,128]{2,1,0:T(8,128)S(1)}, u32[]{:S(2)}, u32[]{:S(2)}) collective-permute-start(f32[4,40,128]{2,1,0:T(8,128)S(1)} %shard_map.135), channel_id=1, source_target_pairs={{0,1},{1,0},{2,3},{3,2},{4,8},{5,9},{6,10},{7,11},{8,4},{9,5},{10,... | collective-permute-start | bytes 245768 | tf_op jit(solution)/shard_map/ppermute | solution.py:541
  32.2 15.3 %collective-permute-start.21 = (f32[4,40,128]{2,1,0:T(8,128)S(1)}, f32[4,40,128]{2,1,0:T(8,128)S(1)}, u32[]{:S(2)}, u32[]{:S(2)}) collective-permute-start(f32[4,40,128]{2,1,0:T(8,128)S(1)} %shard_map.133), channel_id=1, source_target_pairs={{0,1},{1,0},{2,3},{3,2},{4,8},{5,9},{6,10},{7,11},{8,4},{9,5},{10,... | collective-permute-start | bytes 245768 | tf_op jit(solution)/shard_map/ppermute | solution.py:541
  32.5 15.9 %collective-permute-start.18 = (f32[4,40,128]{2,1,0:T(8,128)S(1)}, f32[4,40,128]{2,1,0:T(8,128)S(1)}, u32[]{:S(2)}, u32[]{:S(2)}) collective-permute-start(f32[4,40,128]{2,1,0:T(8,128)S(1)} %shard_map.131), channel_id=1, source_target_pairs={{0,1},{1,0},{2,3},{3,2},{4,8},{5,9},{6,10},{7,11},{8,4},{9,5},{10,... | collective-permute-start | bytes 245768 | tf_op jit(solution)/shard_map/ppermute | solution.py:541
  32.9 17.2 %collective-permute-start.28 = (f32[4,40,128]{2,1,0:T(8,128)S(1)}, f32[4,40,128]{2,1,0:T(8,128)S(1)}, u32[]{:S(2)}, u32[]{:S(2)}) collective-permute-start(f32[4,40,128]{2,1,0:T(8,128)S(1)} %shard_map.138), channel_id=1, source_target_pairs={{0,4},{1,5},{2,6},{3,7},{4,0},{5,1},{6,2},{7,3},{8,9},{9,8},{10,11... | collective-permute-start | bytes 245768 | tf_op jit(solution)/shard_map/ppermute | solution.py:541
  46.1 5.3 %collective-permute-start.25 = (f32[4,40,128]{2,1,0:T(8,128)S(1)}, f32[4,40,128]{2,1,0:T(8,128)S(1)}, u32[]{:S(2)}, u32[]{:S(2)}) collective-permute-start(f32[4,40,128]{2,1,0:T(8,128)S(1)} %shard_map.136), channel_id=1, source_target_pairs={{0,4},{1,5},{2,6},{3,7},{4,0},{5,1},{6,2},{7,3},{8,9},{9,8},{10,11... | collective-permute-start | bytes 245768 | tf_op jit(solution)/shard_map/ppermute | solution.py:541
  47.5 4.8 %collective-permute-start.22 = (f32[4,40,128]{2,1,0:T(8,128)S(1)}, f32[4,40,128]{2,1,0:T(8,128)S(1)}, u32[]{:S(2)}, u32[]{:S(2)}) collective-permute-start(f32[4,40,128]{2,1,0:T(8,128)S(1)} %shard_map.134), channel_id=1, source_target_pairs={{0,4},{1,5},{2,6},{3,7},{4,0},{5,1},{6,2},{7,3},{8,9},{9,8},{10,11... | collective-permute-start | bytes 245768 | tf_op jit(solution)/shard_map/ppermute | solution.py:541
  48.4 4.7 %collective-permute-start.19 = (f32[4,40,128]{2,1,0:T(8,128)S(1)}, f32[4,40,128]{2,1,0:T(8,128)S(1)}, u32[]{:S(2)}, u32[]{:S(2)}) collective-permute-start(f32[4,40,128]{2,1,0:T(8,128)S(1)} %shard_map.132), channel_id=1, source_target_pairs={{0,4},{1,5},{2,6},{3,7},{4,0},{5,1},{6,2},{7,3},{8,9},{9,8},{10,11... | collective-permute-start | bytes 245768 | tf_op jit(solution)/shard_map/ppermute | solution.py:541
  54.1 4.0 %collective-permute-start.29 = (f32[32,160]{1,0:T(8,128)S(1)}, f32[32,160]{1,0:T(8,128)S(1)}, u32[]{:S(2)}, u32[]{:S(2)}) collective-permute-start(f32[32,160]{1,0:T(8,128)S(1)} %get-tuple-element.52.refs_5_), channel_id=1, source_target_pairs={{0,16},{16,0},{1,17},{17,1},{2,18},{18,2},{3,19},{19,3},{4,20},{20... | collective-permute-start | bytes 61448 | tf_op jit(solution)/shard_map/ppermute | solution.py:514
  60.0 3.6 %collective-permute-start.31 = (f32[8,128]{1,0:T(8,128)S(1)}, f32[8,128]{1,0:T(8,128)S(1)}, u32[]{:S(2)}, u32[]{:S(2)}) collective-permute-start(f32[8,128]{1,0:T(8,128)S(1)} %add.26), channel_id=1, source_target_pairs={{0,2},{1,3},{2,0},{3,1},{4,6},{5,7},{6,4},{7,5},{8,10},{9,11},{10,... | collective-permute-start | bytes 12296 | tf_op jit(solution)/shard_map/ppermute | solution.py:552
  63.6 3.6 %collective-permute-start.32 = (f32[8,128]{1,0:T(8,128)S(1)}, f32[8,128]{1,0:T(8,128)S(1)}, u32[]{:S(2)}, u32[]{:S(2)}) collective-permute-start(f32[8,128]{1,0:T(8,128)S(1)} %add.27), channel_id=1, source_target_pairs={{0,16},{16,0},{1,17},{17,1},{2,18},{18,2},{3,19},{19,3},{4,20},{20... | collective-permute-start | bytes 12296 | tf_op jit(solution)/shard_map/ppermute | solution.py:552
  67.3 4.4 %collective-permute-start.33 = (f32[8,128]{1,0:T(8,128)S(1)}, f32[8,128]{1,0:T(8,128)S(1)}, u32[]{:S(2)}, u32[]{:S(2)}) collective-permute-start(f32[8,128]{1,0:T(8,128)S(1)} %add.28), channel_id=1, source_target_pairs={{0,4},{4,0},{8,12},{12,8},{1,5},{5,1},{9,13},{13,9},{2,6},{6,2},{1... | collective-permute-start | bytes 12296 | tf_op jit(solution)/shard_map/ppermute | solution.py:552
  68.3 4.5 %collective-permute-start.34 = (f32[8,128]{1,0:T(8,128)S(1)}, f32[8,128]{1,0:T(8,128)S(1)}, u32[]{:S(2)}, u32[]{:S(2)}) collective-permute-start(f32[8,128]{1,0:T(8,128)S(1)} %add.28), channel_id=1, source_target_pairs={{0,8},{4,12},{8,0},{12,4},{1,9},{5,13},{9,1},{13,5},{2,10},{6,14},... | collective-permute-start | bytes 12296 | tf_op jit(solution)/shard_map/ppermute | solution.py:552
  68.3 5.4 %collective-permute-start.35 = (f32[8,128]{1,0:T(8,128)S(1)}, f32[8,128]{1,0:T(8,128)S(1)}, u32[]{:S(2)}, u32[]{:S(2)}) collective-permute-start(f32[8,128]{1,0:T(8,128)S(1)} %add.28), channel_id=1, source_target_pairs={{0,12},{4,8},{8,4},{12,0},{1,13},{5,9},{9,5},{13,1},{2,14},{6,10},... | collective-permute-start | bytes 12296 | tf_op jit(solution)/shard_map/ppermute | solution.py:552
  (11 other events, 54.2 us)

commit v2 on v1

--- a/solution.py
+++ b/solution.py
@@ -85,6 +85,14 @@
     return [leak ** (3 - s) * rising(place, 3 - s) * decay for s in range(4)]
 
 
+def entering_columns(lonc, rows, cells, backward, first):
+    c, leak, _ = lon_consts(lonc)
+    before = [jnp.zeros((first, cells), f32)] if first else []
+    after = cells - first - 4 * rows
+    after = [jnp.zeros((after, cells), f32)] if after else []
+    return jnp.concatenate(before + lon_entering(c, leak, cells, backward) + after, axis=0).T
+
+
 def lon_tables(lonc, rows, cells, backward, table_ref):
     c, leak, scale = lon_consts(lonc)
     gain = leak**4 * scale
@@ -92,19 +100,28 @@
     spare = jnp.zeros((cells - 4 * rows, cells), f32)
     finals = jnp.concatenate(finals + [spare], axis=0).T
     column = lax.broadcasted_iota(jnp.int32, (cells, cells), 1)
+    if backward:
+        products = entering_columns(lonc, rows, cells, backward, cells - 4 * rows)
     for y in range(rows):
         inside = lon_kernel_matrix(c[y : y + 1], gain[y : y + 1], cells, backward)
         leaving = jnp.where(lax.rem(column, rows) == y, finals, 0.0)
+        if backward:
+            mine = jnp.where(lax.rem(column, rows) == y, products, 0.0)
+            leaving = leaving + jnp.dot(
+                inside, mine, precision=lax.Precision.HIGHEST, preferred_element_type=f32
+            )
         table_ref[y] = right3(jnp.concatenate([inside, leaving], axis=1), 0)
 
 
-def lon_local_rows(load_row, table_ref, rows, cells, inside_ref, carried_ref):
-    carried = None
+def lon_local_rows(load_row, table_ref, rows, cells, inside_ref, also=None):
+    total = None
     for y in range(rows):
         both = product3(left3(load_row(y), 1), table_ref[y])
         inside_ref[y] = both[:, :cells]
-        carried = both[:, cells:] if carried is None else carried + both[:, cells:]
-    carried_ref[...] = carried.T[: 4 * rows]
+        if also is not None:
+            also(y, both[:, :cells])
+        total = both[:, cells:] if total is None else total + both[:, cells:]
+    return total
 
 
 def lon_incoming_states(lonc, blocks, rows, cells):
@@ -245,9 +262,8 @@
 
 def k_lon_fwd(rows, k, cells, d_ref, table_ref, inside_ref, carried_ref):
     d_ref = d_ref.reshape(k * rows, cells)
-    lon_local_rows(
-        lambda y: d_ref[pl.ds(y, k, stride=rows), :], table_ref, rows, cells, inside_ref, carried_ref
-    )
+    total = lon_local_rows(lambda y: d_ref[pl.ds(y, k, stride=rows), :], table_ref, rows, cells, inside_ref)
+    carried_ref[...] = total.T[: 4 * rows]
 
 
 def spread_modes(v, pairs, transposed):
@@ -414,7 +430,9 @@
 def k_lon_bwd(rows, k, cells, chunks, count, blocks, *refs):
     g_refs, lat_ref, block_ref, table_ref, rest = refs[:2], refs[2], refs[3], refs[4], refs[5:]
     block = (blocks - 1.0) - block_ref[...]
-    inside_ref, carried_ref, p_ref = rest[2 * count :]
+    d_ref, r_ref, known_ref, inside_ref, sent_ref, p_ref = rest[2 * count :]
+    d_ref = d_ref.reshape(k * rows, cells)
+    r_ref = r_ref.reshape(k * rows, cells)
     half = k // 2
     for part in range(2):
         g_ref = g_refs[part]
@@ -436,35 +454,90 @@
     def load_row(y):
         return jnp.concatenate(swap_halves(p_ref[0, y], p_ref[1, y]), axis=0)
 
-    lon_local_rows(load_row, table_ref, rows, cells, inside_ref, carried_ref)
-
-
-def k_sums(rows, k, cells, n, *refs):
+    acc = [jnp.zeros((8, cells), f32)] * 4
+
+    def also(y, q):
+        at = pl.ds(y, k, stride=rows)
+        d, r = d_ref[at, :], r_ref[at, :]
+        h = d + q
+        fold = lambda v: v.reshape(k // 8, 8, cells).sum(axis=0)
+        acc[:] = [a + fold(v) for a, v in zip(acc, (r * r, d * h, r * h, h * h))]
+
+    total = lon_local_rows(load_row, table_ref, rows, cells, inside_ref, also)
+    sent_ref[:k] = total + known_ref[...]
+    out = [a.sum(axis=0, keepdims=True) for a in acc]
+    sent_ref[k:] = jnp.concatenate(out + [jnp.zeros((4, cells), f32)], axis=0)
+
+
+def k_known(rows, k, cells, d_ref, r_ref, lon_ref, out_ref):
+    d_ref = d_ref.reshape(k * rows, cells)
+    r_ref = r_ref.reshape(k * rows, cells)
+    columns = entering_columns(lon_ref[...], rows, cells, True, 0)
+    column = lax.broadcasted_iota(jnp.int32, (cells, cells), 1)
+    total = [None, None]
+    for y in range(rows):
+        table = right3(jnp.where(lax.rem(column, rows) == y, columns, 0.0), 0)
+        for i, ref in enumerate((d_ref, r_ref)):
+            part = product3(left3(ref[pl.ds(y, k, stride=rows), :], 1), table)
+            total[i] = part if total[i] is None else total[i] + part
+    group = 4 * rows
+    d, r = total
+    out_ref[...] = pltpu.roll(d, group, 1) + pltpu.roll(r, 2 * group, 1) + pltpu.roll(d, cells - group, 1)
+
+
+def k_sums(rows, k, cells, lon_ref, own_ref, other_ref, sums_ref, states_ref):
+    lonc = lon_ref[...]
+    group = 4 * rows
+    own, other = own_ref[:k].T, other_ref[:k].T
+    c, leak, _ = lon_consts(lonc)
+    entering = lon_entering(c, leak, cells, True)
+    sums = own_ref[k:] + other_ref[k:]
+    extra = [jnp.zeros((rows, k), f32)] * 3
+    for here, there in ((own, other), (other, own)):
+        states = lon_incoming_states(lonc, [there[:group], here[:group]], rows, cells)
+        if here is own:
+            states_ref[...] = states
+        v = [states[s * rows : (s + 1) * rows] for s in range(4)]
+        for s in range(4):
+            d, r, h = (here[g * group + s * rows : g * group + (s + 1) * rows] for g in (1, 2, 3))
+            both = 2.0 * h
+            for t in range(4):
+                both = both + jnp.sum(entering[s] * entering[t], axis=1, keepdims=True) * v[t]
+            extra = [extra[0] + v[s] * d, extra[1] + v[s] * r, extra[2] + v[s] * both]
+    lane, row = iota(sums.shape, 1), iota(sums.shape, 0)
+    for i, e in enumerate(extra):
+        e = jnp.sum(jnp.sum(e, axis=1, keepdims=True), axis=0, keepdims=True)
+        sums = sums + jnp.where((lane == 0.0) & (row == float(i + 1)), e, 0.0)
+    sums_ref[...] = sums
+
+
+def k_finish(rows, k, cells, inside_ref, lon_ref, d_ref, states_ref, h_ref):
+    d_ref = d_ref.reshape(k * rows, cells)
+    c, leak, _ = lon_consts(lon_ref[...])
+    added = lon_correction(states_ref[...], lon_entering(c, leak, cells, True), rows, cells)
+    for y in range(rows):
+        at = pl.ds(y, k, stride=rows)
+        h_ref[at, :] = inside_ref[y] + added(y) + d_ref[at, :]
+
+
+def k_sums_any(rows, k, cells, n, *refs):
     inside_ref, lon_ref, d_ref, r_ref, *rest = refs
     d_ref = d_ref.reshape(k * rows, cells)
     r_ref = r_ref.reshape(k * rows, cells)
-    blocks = [r[...] for r in rest[:n]]
+    blocks = [r[:k].T[: 4 * rows] for r in rest[:n]]
     h_ref, sums_ref = rest[n:]
     lonc = lon_ref[...]
     states = lon_incoming_states(lonc, blocks, rows, cells)
     c, leak, _ = lon_consts(lonc)
     added = lon_correction(states, lon_entering(c, leak, cells, True), rows, cells)
+    acc = [jnp.zeros((8, cells), f32)] * 4
+    fold = lambda v: v.reshape(k // 8, 8, cells).sum(axis=0)
     for y in range(rows):
         at = pl.ds(y, k, stride=rows)
-        h_ref[at, :] = inside_ref[y] + added(y)
-    block = 64
-    zero = jnp.zeros((8, cells), f32)
-
-    def step(i, acc):
-        at = pl.ds(pl.multiple_of(i * block, 8), block)
-        d = d_ref[at, :]
-        r = r_ref[at, :]
-        h = h_ref[at, :] + d
+        d, r = d_ref[at, :], r_ref[at, :]
+        h = inside_ref[y] + added(y) + d
         h_ref[at, :] = h
-        fold = lambda v: v.reshape(block // 8, 8, cells).sum(axis=0)
-        return (acc[0] + fold(r * r), acc[1] + fold(d * h), acc[2] + fold(r * h), acc[3] + fold(h * h))
-
-    acc = lax.fori_loop(0, (k * rows) // block, step, (zero,) * 4)
+        acc = [a + fold(v) for a, v in zip(acc, (r * r, d * h, r * h, h * h))]
     out = [a.sum(axis=0, keepdims=True) for a in acc]
     sums_ref[...] = jnp.concatenate(out + [jnp.zeros((4, cells), f32)], axis=0)
 
@@ -563,11 +636,11 @@
     return out
 
 
-def reduce_everywhere(v):
+def reduce_everywhere(v, over_lon):
     n_lon, n_lat, n_mem = (lax.axis_size(a) for a in ("lon", "lat", "mem"))
     for s in powers(n_mem):
         v = all_sum(v, ("mem",), [s])
-    for s in powers(n_lon):
+    for s in powers(n_lon) if over_lon else ():
         v = all_sum(v, ("lon",), [s])
     lat = powers(n_lat)
     for i in range(0, len(lat), 2):
@@ -641,19 +714,32 @@
         )
     got = lat_carry(sends, latc, rows, True)
     count = len(got[0])
-    inside, carried = call(
+    known = call(functools.partial(k_known, rows, k, cells), sds(k, cells), [direction, residual, lonc], cost=10**9)
+    inside, sent = call(
         functools.partial(k_lon_bwd, rows, k, cells, back_chunks, count, lax.axis_size("lat")),
-        (sds(rows, k, cells), sds(4 * rows, k)),
-        [*grads, latc, block, back_tables, *got[0], *got[1]],
+        (sds(rows, k, cells), sds(k + 8, cells)),
+        [*grads, latc, block, back_tables, *got[0], *got[1], direction, residual, known],
         scratch=[pltpu.VMEM((2, rows, half, cells), f32)],
     )
-    blocks = lon_exchange(carried, True)
-    h, sums = call(
-        functools.partial(k_sums, rows, k, cells, n_lon),
-        (sds(k * rows, cells), sds(8, cells)),
-        [inside, lonc, direction, residual, *blocks],
-    )
-    sums = reduce_everywhere(sums)
+    blocks = lon_exchange(sent, True)
+    if n_lon == 2:
+        sums, states = call(
+            functools.partial(k_sums, rows, k, cells), (sds(8, cells), sds(4 * rows, k)), [lonc, sent, blocks[0]]
+        )
+        sums = reduce_everywhere(sums, False)
+        h = call(
+            functools.partial(k_finish, rows, k, cells),
+            sds(k * rows, cells),
+            [inside, lonc, direction, states],
+            cost=10**9,
+        )
+    else:
+        h, sums = call(
+            functools.partial(k_sums_any, rows, k, cells, n_lon),
+            (sds(k * rows, cells), sds(8, cells)),
+            [inside, lonc, direction, residual, *blocks],
+        )
+        sums = reduce_everywhere(sums, True)
     pieces = 4 if k % 4 == 0 else 1
     outs = call(
         functools.partial(k_update, pieces),

time: 75.4 us -> 72.9 us (0.967)
  starting transfers between devices: 40.2 us -> 38 us
  waiting for transfers between devices: 21.1 us -> 19.4 us
  Pallas kernels: 11.5 us -> 12.9 us
    ppermute x6 -> x5, waiting for transfers between devices: 7.43 us -> 4.92 us  [all_sum(): lax.ppermute(v, axes, [(i, i ^ m) for i in range(total)])]
    ppermute x6 -> x5, starting transfers between devices: 7.47 us -> 5.97 us  [all_sum(): lax.ppermute(v, axes, [(i, i ^ m) for i in range(total)])]
    pallas_call x30 -> x32, Pallas kernels: 11.5 us -> 12.9 us  [call(): pl.pallas_call(body, out_shape=outs, in_specs=specs or [VM] * len(ins), o...]
    ppermute x24, starting transfers between devices: 25 us -> 24.1 us  [lat_carry(): got[c][i].append(lax.ppermute(v, ('lat', 'mem'), pairs))]
  transfers between devices with their start and end apart: 36 -> 35, of which waited for: 18 -> 17; matrix products, arithmetic and copies ran while one was open for 0% -> 0% of each run, Pallas kernels for 9% -> 12%
where the time goes in v2:
time: 72.9 us; the launch traced here: 72.7 us
  starting transfers between devices  38 us (52%)
  waiting for transfers between devices  19.4 us (27%)
  Pallas kernels  12.9 us (18%)
  between operations  1 us (1%)
  local copies, waits for them, and re-layouts  0.73 us (1%)
    ppermute x24, starting transfers between devices, lat_carry(): got[c][i].append(lax.ppermute(v, ('lat', 'mem'), pairs))  24.1 us
    pallas_call x32, Pallas kernels, call(): pl.pallas_call(body, out_shape=outs, in_specs=specs or [VM] * len(ins), o...  12.9 us
    ppermute x24, waiting for transfers between devices, lat_carry(): got[c][i].append(lax.ppermute(v, ('lat', 'mem'), pairs))  8.18 us
    ppermute x5, starting transfers between devices, all_sum(): lax.ppermute(v, axes, [(i, i ^ m) for i in range(total)])  5.97 us
    ppermute x5, waiting for transfers between devices, all_sum(): lax.ppermute(v, axes, [(i, i ^ m) for i in range(total)])  4.92 us
    ppermute x2, waiting for transfers between devices, lon_exchange(): lax.ppermute(carried, 'lon', [(j, (j + sign * r) % n) for j in range(n)])  4.89 us
    ppermute x2, starting transfers between devices, lon_exchange(): lax.ppermute(carried, 'lon', [(j, (j + sign * r) % n) for j in range(n)])  4.56 us
    ppermute x2, starting transfers between devices, iteration(): other = lax.ppermute(v, 'mem', [(i, i ^ step) for i in range(n_mem)])  2.65 us
  transfers between devices with their start and end apart: 35, of which 17 were waited for; matrix products, arithmetic and copies ran while one was open for 0% of the time, Pallas kernels for 12%

profile of v2, /device:TPU:0, one launch (start us, length us, event | category | flops | bytes accessed | tf_op | source)
XLA Modules:
  0.0 72.7 jit_solution(11755532473968995347)
XLA Ops:
  3.0 3.0 %collective-permute-start = (f32[32,160]{1,0:T(8,128)S(1)}, f32[32,160]{1,0:T(8,128)S(1)}, u32[]{:S(2)}, u32[]{:S(2)}) collective-permute-start(f32[32,160]{1,0:T(8,128)S(1)} %get-tuple-element.33.refs_4_), channel_id=1, source_target_pairs={{0,16},{16,0},{1,17},{17,1},{2,18},{18,2},{3,19},{19,3},{4,20},{20... | collective-permute-start | bytes 61448 | tf_op jit(solution)/shard_map/ppermute | solution.py:587
  6.0 1.9 %collective-permute-done.refs_3_ = f32[32,160]{1,0:T(8,128)S(1)} collective-permute-done((f32[32,160]{1,0:T(8,128)S(1)}, f32[32,160]{1,0:T(8,128)S(1)}, u32[]{:S(2)}, u32[]{:S(2)}) %collective-permute-start) | collective-permute-done | bytes 20512 | tf_op jit(solution)/shard_map/ppermute | solution.py:587
  8.6 2.2 %collective-permute-start.12 = (f32[4,40,128]{2,1,0:T(8,128)S(1)}, f32[4,40,128]{2,1,0:T(8,128)S(1)}, u32[]{:S(2)}, u32[]{:S(2)}) collective-permute-start(f32[4,40,128]{2,1,0:T(8,128)S(1)} %get-tuple-element.45.carried_ref), channel_id=1, source_target_pairs={{0,4},{1,5},{2,6},{3,7},{4,0},{5,1},{6,2},{7,3},{8,9},{9,8},{10,11... | collective-permute-start | bytes 245768 | tf_op jit(solution)/shard_map/ppermute | solution.py:614
  10.8 1.9 %collective-permute-start.4 = (f32[4,40,128]{2,1,0:T(8,128)S(1)}, f32[4,40,128]{2,1,0:T(8,128)S(1)}, u32[]{:S(2)}, u32[]{:S(2)}) collective-permute-start(f32[4,40,128]{2,1,0:T(8,128)S(1)} %get-tuple-element.40.carried_ref), channel_id=1, source_target_pairs={{0,4},{1,5},{2,6},{3,7},{4,0},{5,1},{6,2},{7,3},{8,9},{9,8},{10,11... | collective-permute-start | bytes 245768 | tf_op jit(solution)/shard_map/ppermute | solution.py:614
  12.8 1.2 %collective-permute-done.12.got_ref.refs_9_ = f32[4,40,128]{2,1,0:T(8,128)S(1)} collective-permute-done((f32[4,40,128]{2,1,0:T(8,128)S(1)}, f32[4,40,128]{2,1,0:T(8,128)S(1)}, u32[]{:S(2)}, u32[]{:S(2)}) %collective-permute-start.12) | collective-permute-done | bytes 81952 | tf_op jit(solution)/shard_map/ppermute | solution.py:614
  14.1 1.9 %collective-permute-done.9.got_ref.refs_6_ = f32[4,40,128]{2,1,0:T(8,128)S(1)} collective-permute-done((f32[4,40,128]{2,1,0:T(8,128)S(1)}, f32[4,40,128]{2,1,0:T(8,128)S(1)}, u32[]{:S(2)}, u32[]{:S(2)}) %collective-permute-start.9) | collective-permute-done | bytes 81952 | tf_op jit(solution)/shard_map/ppermute | solution.py:614
  16.2 0.8 %collective-permute-done.4.got_ref.refs_9_ = f32[4,40,128]{2,1,0:T(8,128)S(1)} collective-permute-done((f32[4,40,128]{2,1,0:T(8,128)S(1)}, f32[4,40,128]{2,1,0:T(8,128)S(1)}, u32[]{:S(2)}, u32[]{:S(2)}) %collective-permute-start.4) | collective-permute-done | bytes 81952 | tf_op jit(solution)/shard_map/ppermute | solution.py:614
  17.1 0.8 %collective-permute-done.1.got_ref.refs_6_ = f32[4,40,128]{2,1,0:T(8,128)S(1)} collective-permute-done((f32[4,40,128]{2,1,0:T(8,128)S(1)}, f32[4,40,128]{2,1,0:T(8,128)S(1)}, u32[]{:S(2)}, u32[]{:S(2)}) %collective-permute-start.1) | collective-permute-done | bytes 81952 | tf_op jit(solution)/shard_map/ppermute | solution.py:614
  18.0 1.1 %shard_map.115 = (f32[2624,128]{1,0:T(8,128)S(1)}, f32[2624,128]{1,0:T(8,128)S(1)}) custom-call(bf16[20,32,8,128]{3,2,1,0:T(8,128)(2,1)S(1)} %copy-done.4), custom_call_target="tpu_custom_call" | custom-call | flops 1000000000 | bytes 1000 | tf_op jit(solution)/shard_map/pallas_call | solution.py:568
  20.5 1.4 %shard_map.116 = (f32[80,128]{1,0:T(8,128)S(1)}, bf16[320,240]{1,0:T(8,128)(2,1)S(1)}) custom-call(f32[8,32]{1,0:T(8,128)S(1)} %copy-done.5, s32[20]{0:T(128)S(1)} %copy-done.6), custom_call_target="tpu_custom_call" | custom-call | flops 1000000000 | bytes 1000 | tf_op jit(solution)/shard_map/pallas_call | solution.py:568
  24.1 1.6 %collective-permute-start.16 = (f32[8,16,128]{2,1,0:T(8,128)S(1)}, f32[8,16,128]{2,1,0:T(8,128)S(1)}, u32[]{:S(2)}, u32[]{:S(2)}) collective-permute-start(f32[8,16,128]{2,1,0:T(8,128)S(1)} %add.22.refs_0_), channel_id=1, source_target_pairs={{0,2},{1,3},{2,0},{3,1},{4,6},{5,7},{6,4},{7,5},{8,10},{9,11},{10,... | collective-permute-start | bytes 196616 | tf_op jit(solution)/shard_map/ppermute | solution.py:709
  25.7 1.1 %collective-permute-start.8 = (f32[8,16,128]{2,1,0:T(8,128)S(1)}, f32[8,16,128]{2,1,0:T(8,128)S(1)}, u32[]{:S(2)}, u32[]{:S(2)}) collective-permute-start(f32[8,16,128]{2,1,0:T(8,128)S(1)} %add.21.refs_0_), channel_id=1, source_target_pairs={{0,2},{1,3},{2,0},{3,1},{4,6},{5,7},{6,4},{7,5},{8,10},{9,11},{10,... | collective-permute-start | bytes 196616 | tf_op jit(solution)/shard_map/ppermute | solution.py:709
  27.4 1.2 %collective-permute-done.16.refs_1_ = f32[8,16,128]{2,1,0:T(8,128)S(1)} collective-permute-done((f32[8,16,128]{2,1,0:T(8,128)S(1)}, f32[8,16,128]{2,1,0:T(8,128)S(1)}, u32[]{:S(2)}, u32[]{:S(2)}) %collective-permute-start.16) | collective-permute-done | bytes 65568 | tf_op jit(solution)/shard_map/ppermute | solution.py:709
  28.6 0.8 %shard_map.129 = (f32[8,80,128]{2,1,0:T(8,128)S(1)}, f32[4,40,128]{2,1,0:T(8,128)S(1)}, f32[4,40,128]{2,1,0:T(8,128)S(1)}) custom-call(f32[8,16,128]{2,1,0:T(8,128)S(1)} %add.22.refs_0_, f32[8,16,128]{2,1,0:T(8,128)S(1)} %collective-permute-done.16.refs_1_, f32[32,8,128]{2,1,0:T(8,128)S(1)} %copy-done.3, f32[2624,128]{1,0:T(8,128)S(1)} %get-tuple-element.43.refs_3_, ...), custom_call_target="tpu_custom_call" | custom-call | tf_op jit(solution)/shard_map/pallas_call | solution.py:568
  32.9 0.8 %shard_map.130.refs_4_ = bf16[8,384,256]{2,1,0:T(8,128)(2,1)S(1)} custom-call(f32[8,128]{1,0:T(8,128)S(1)} %get-tuple-element.29.refs_1_.lon_ref), custom_call_target="tpu_custom_call" | custom-call | flops 1000000000 | bytes 1000 | tf_op jit(solution)/shard_map/pallas_call | solution.py:568
  33.8 13.2 %collective-permute-start.28 = (f32[4,40,128]{2,1,0:T(8,128)S(1)}, f32[4,40,128]{2,1,0:T(8,128)S(1)}, u32[]{:S(2)}, u32[]{:S(2)}) collective-permute-start(f32[4,40,128]{2,1,0:T(8,128)S(1)} %shard_map.138), channel_id=1, source_target_pairs={{0,4},{1,5},{2,6},{3,7},{4,0},{5,1},{6,2},{7,3},{8,9},{9,8},{10,11... | collective-permute-start | bytes 245768 | tf_op jit(solution)/shard_map/ppermute | solution.py:614
  47.5 1.6 %collective-permute-start.22 = (f32[4,40,128]{2,1,0:T(8,128)S(1)}, f32[4,40,128]{2,1,0:T(8,128)S(1)}, u32[]{:S(2)}, u32[]{:S(2)}) collective-permute-start(f32[4,40,128]{2,1,0:T(8,128)S(1)} %shard_map.134), channel_id=1, source_target_pairs={{0,4},{1,5},{2,6},{3,7},{4,0},{5,1},{6,2},{7,3},{8,9},{9,8},{10,11... | collective-permute-start | bytes 245768 | tf_op jit(solution)/shard_map/ppermute | solution.py:614
  49.8 0.9 %shard_map.139.refs_19_ = f32[160,128]{1,0:T(8,128)S(1)} custom-call(f32[160,8,128]{2,1,0:T(8,128)S(1)} %copy-done, f32[160,8,128]{2,1,0:T(8,128)S(1)} %copy-done.1, f32[8,128]{1,0:T(8,128)S(1)} %get-tuple-element.29.refs_1_.lon_ref), custom_call_target="tpu_custom_call" | custom-call | flops 1000000000 | bytes 1000 | tf_op jit(solution)/shard_map/pallas_call | solution.py:568
  50.6 1.6 %collective-permute-done.25.refs_13_ = f32[4,40,128]{2,1,0:T(8,128)S(1)} collective-permute-done((f32[4,40,128]{2,1,0:T(8,128)S(1)}, f32[4,40,128]{2,1,0:T(8,128)S(1)}, u32[]{:S(2)}, u32[]{:S(2)}) %collective-permute-start.25) | collective-permute-done | bytes 81952 | tf_op jit(solution)/shard_map/ppermute | solution.py:614
  52.3 0.9 %collective-permute-done.22.refs_10_ = f32[4,40,128]{2,1,0:T(8,128)S(1)} collective-permute-done((f32[4,40,128]{2,1,0:T(8,128)S(1)}, f32[4,40,128]{2,1,0:T(8,128)S(1)}, u32[]{:S(2)}, u32[]{:S(2)}) %collective-permute-start.22) | collective-permute-done | bytes 81952 | tf_op jit(solution)/shard_map/ppermute | solution.py:614
  53.1 0.9 %collective-permute-done.19.refs_7_ = f32[4,40,128]{2,1,0:T(8,128)S(1)} collective-permute-done((f32[4,40,128]{2,1,0:T(8,128)S(1)}, f32[4,40,128]{2,1,0:T(8,128)S(1)}, u32[]{:S(2)}, u32[]{:S(2)}) %collective-permute-start.19) | collective-permute-done | bytes 81952 | tf_op jit(solution)/shard_map/ppermute | solution.py:614
  54.0 1.0 %shard_map.140 = (f32[8,160,128]{2,1,0:T(8,128)S(1)}, f32[168,128]{1,0:T(8,128)S(1)}) custom-call(f32[8,80,128]{2,1,0:T(8,128)S(1)} %get-tuple-element.41.refs_0_, f32[8,80,128]{2,1,0:T(8,128)S(1)} %get-tuple-element.46.refs_1_, f32[2,8,128]{2,1,0:T(8,128)S(1)} %get-tuple-element.32.refs_2_.lat_ref.refs_1_.refs_6_, ...), custom_call_target="tpu_custom_call" | custom-call | tf_op jit(solution)/shard_map/pallas_call | solution.py:568
  55.1 1.6 %collective-permute-start.29 = (f32[168,128]{1,0:T(8,128)S(1)}, f32[168,128]{1,0:T(8,128)S(1)}, u32[]{:S(2)}, u32[]{:S(2)}) collective-permute-start(f32[168,128]{1,0:T(8,128)S(1)} %get-tuple-element.51.own_ref), channel_id=1, source_target_pairs={{0,16},{16,0},{1,17},{17,1},{2,18},{18,2},{3,19},{19,3},{4,20},{20... | collective-permute-start | bytes 258056 | tf_op jit(solution)/shard_map/ppermute | solution.py:587
  56.6 3.0 %collective-permute-done.29.other_ref = f32[168,128]{1,0:T(8,128)S(1)} collective-permute-done((f32[168,128]{1,0:T(8,128)S(1)}, f32[168,128]{1,0:T(8,128)S(1)}, u32[]{:S(2)}, u32[]{:S(2)}) %collective-permute-start.29) | collective-permute-done | bytes 86048 | tf_op jit(solution)/shard_map/ppermute | solution.py:587
  60.0 1.2 %collective-permute-done.30 = f32[8,128]{1,0:T(8,128)S(1)} collective-permute-done((f32[8,128]{1,0:T(8,128)S(1)}, f32[8,128]{1,0:T(8,128)S(1)}, u32[]{:S(2)}, u32[]{:S(2)}) %collective-permute-start.30) | collective-permute-done | bytes 4128 | tf_op jit(solution)/shard_map/ppermute | solution.py:625
  61.1 1.5 %collective-permute-start.31 = (f32[8,128]{1,0:T(8,128)S(1)}, f32[8,128]{1,0:T(8,128)S(1)}, u32[]{:S(2)}, u32[]{:S(2)}) collective-permute-start(f32[8,128]{1,0:T(8,128)S(1)} %add.23), channel_id=1, source_target_pairs={{0,2},{1,3},{2,0},{3,1},{4,6},{5,7},{6,4},{7,5},{8,10},{9,11},{10,... | collective-permute-start | bytes 12296 | tf_op jit(solution)/shard_map/ppermute | solution.py:625
  62.6 2.1 %collective-permute-done.31 = f32[8,128]{1,0:T(8,128)S(1)} collective-permute-done((f32[8,128]{1,0:T(8,128)S(1)}, f32[8,128]{1,0:T(8,128)S(1)}, u32[]{:S(2)}, u32[]{:S(2)}) %collective-permute-start.31) | collective-permute-done | bytes 4128 | tf_op jit(solution)/shard_map/ppermute | solution.py:625
  64.7 1.1 %collective-permute-start.32 = (f32[8,128]{1,0:T(8,128)S(1)}, f32[8,128]{1,0:T(8,128)S(1)}, u32[]{:S(2)}, u32[]{:S(2)}) collective-permute-start(f32[8,128]{1,0:T(8,128)S(1)} %add.24), channel_id=1, source_target_pairs={{0,4},{4,0},{8,12},{12,8},{1,5},{5,1},{9,13},{13,9},{2,6},{6,2},{1... | collective-permute-start | bytes 12296 | tf_op jit(solution)/shard_map/ppermute | solution.py:625
  65.8 3.3 %collective-permute-start.34 = (f32[8,128]{1,0:T(8,128)S(1)}, f32[8,128]{1,0:T(8,128)S(1)}, u32[]{:S(2)}, u32[]{:S(2)}) collective-permute-start(f32[8,128]{1,0:T(8,128)S(1)} %add.24), channel_id=1, source_target_pairs={{0,12},{4,8},{8,4},{12,0},{1,13},{5,9},{9,5},{13,1},{2,14},{6,10},... | collective-permute-start | bytes 12296 | tf_op jit(solution)/shard_map/ppermute | solution.py:625
  69.5 0.8 %collective-permute-done.33 = f32[8,128]{1,0:T(8,128)S(1)} collective-permute-done((f32[8,128]{1,0:T(8,128)S(1)}, f32[8,128]{1,0:T(8,128)S(1)}, u32[]{:S(2)}, u32[]{:S(2)}) %collective-permute-start.33) | collective-permute-done | bytes 4128 | tf_op jit(solution)/shard_map/ppermute | solution.py:625
  70.3 0.9 %collective-permute-done.34 = f32[8,128]{1,0:T(8,128)S(1)} collective-permute-done((f32[8,128]{1,0:T(8,128)S(1)}, f32[8,128]{1,0:T(8,128)S(1)}, u32[]{:S(2)}, u32[]{:S(2)}) %collective-permute-start.34) | collective-permute-done | bytes 4128 | tf_op jit(solution)/shard_map/ppermute | solution.py:625
  71.2 1.5 %shard_map.143 = (f32[160,8,128]{2,1,0:T(8,128)}, f32[160,8,128]{2,1,0:T(8,128)}, f32[160,8,128]{2,1,0:T(8,128)}) custom-call(f32[8,128]{1,0:T(8,128)S(1)} %add_add_fusion.sums_ref, f32[160,8,128]{2,1,0:T(8,128)S(1)} %copy-done.2, f32[160,8,128]{2,1,0:T(8,128)S(1)} %copy-done.1, f32[160,8,128]{2,1,0:T(8,128)S(1)} %copy-done, f32[160,8,128]{2,1,0:T(8,128)S(1)} %bitcast.2), custom_call_target="tpu_custom_call" | custom-call | tf_op jit(solution)/shard_map/pallas_call | solution.py:568
  (90 shorter events, 13.1 us)
Async XLA Ops:
  3.0 4.9 %collective-permute-start = (f32[32,160]{1,0:T(8,128)S(1)}, f32[32,160]{1,0:T(8,128)S(1)}, u32[]{:S(2)}, u32[]{:S(2)}) collective-permute-start(f32[32,160]{1,0:T(8,128)S(1)} %get-tuple-element.33.refs_4_), channel_id=1, source_target_pairs={{0,16},{16,0},{1,17},{17,1},{2,18},{18,2},{3,19},{19,3},{4,20},{20... | collective-permute-start | bytes 61448 | tf_op jit(solution)/shard_map/ppermute | solution.py:587
  8.6 5.5 %collective-permute-start.12 = (f32[4,40,128]{2,1,0:T(8,128)S(1)}, f32[4,40,128]{2,1,0:T(8,128)S(1)}, u32[]{:S(2)}, u32[]{:S(2)}) collective-permute-start(f32[4,40,128]{2,1,0:T(8,128)S(1)} %get-tuple-element.45.carried_ref), channel_id=1, source_target_pairs={{0,4},{1,5},{2,6},{3,7},{4,0},{5,1},{6,2},{7,3},{8,9},{9,8},{10,11... | collective-permute-start | bytes 245768 | tf_op jit(solution)/shard_map/ppermute | solution.py:614
  10.7 5.3 %collective-permute-start.9 = (f32[4,40,128]{2,1,0:T(8,128)S(1)}, f32[4,40,128]{2,1,0:T(8,128)S(1)}, u32[]{:S(2)}, u32[]{:S(2)}) collective-permute-start(f32[4,40,128]{2,1,0:T(8,128)S(1)} %get-tuple-element.44.carried_ref), channel_id=1, source_target_pairs={{0,4},{1,5},{2,6},{3,7},{4,0},{5,1},{6,2},{7,3},{8,9},{9,8},{10,11... | collective-permute-start | bytes 245768 | tf_op jit(solution)/shard_map/ppermute | solution.py:614
  10.8 6.2 %collective-permute-start.4 = (f32[4,40,128]{2,1,0:T(8,128)S(1)}, f32[4,40,128]{2,1,0:T(8,128)S(1)}, u32[]{:S(2)}, u32[]{:S(2)}) collective-permute-start(f32[4,40,128]{2,1,0:T(8,128)S(1)} %get-tuple-element.40.carried_ref), channel_id=1, source_target_pairs={{0,4},{1,5},{2,6},{3,7},{4,0},{5,1},{6,2},{7,3},{8,9},{9,8},{10,11... | collective-permute-start | bytes 245768 | tf_op jit(solution)/shard_map/ppermute | solution.py:614
  12.8 5.1 %collective-permute-start.1 = (f32[4,40,128]{2,1,0:T(8,128)S(1)}, f32[4,40,128]{2,1,0:T(8,128)S(1)}, u32[]{:S(2)}, u32[]{:S(2)}) collective-permute-start(f32[4,40,128]{2,1,0:T(8,128)S(1)} %get-tuple-element.39.carried_ref), channel_id=1, source_target_pairs={{0,4},{1,5},{2,6},{3,7},{4,0},{5,1},{6,2},{7,3},{8,9},{9,8},{10,11... | collective-permute-start | bytes 245768 | tf_op jit(solution)/shard_map/ppermute | solution.py:614
  14.1 5.0 %collective-permute-start.13 = (f32[4,40,128]{2,1,0:T(8,128)S(1)}, f32[4,40,128]{2,1,0:T(8,128)S(1)}, u32[]{:S(2)}, u32[]{:S(2)}) collective-permute-start(f32[4,40,128]{2,1,0:T(8,128)S(1)} %shard_map.126), channel_id=1, source_target_pairs={{0,1},{1,0},{2,3},{3,2},{4,8},{5,9},{6,10},{7,11},{8,4},{9,5},{10,... | collective-permute-start | bytes 245768 | tf_op jit(solution)/shard_map/ppermute | solution.py:614
  16.1 3.6 %collective-permute-start.10 = (f32[4,40,128]{2,1,0:T(8,128)S(1)}, f32[4,40,128]{2,1,0:T(8,128)S(1)}, u32[]{:S(2)}, u32[]{:S(2)}) collective-permute-start(f32[4,40,128]{2,1,0:T(8,128)S(1)} %shard_map.124), channel_id=1, source_target_pairs={{0,1},{1,0},{2,3},{3,2},{4,8},{5,9},{6,10},{7,11},{8,4},{9,5},{10,... | collective-permute-start | bytes 245768 | tf_op jit(solution)/shard_map/ppermute | solution.py:614
  17.0 2.8 %collective-permute-start.5 = (f32[4,40,128]{2,1,0:T(8,128)S(1)}, f32[4,40,128]{2,1,0:T(8,128)S(1)}, u32[]{:S(2)}, u32[]{:S(2)}) collective-permute-start(f32[4,40,128]{2,1,0:T(8,128)S(1)} %shard_map.119), channel_id=1, source_target_pairs={{0,1},{1,0},{2,3},{3,2},{4,8},{5,9},{6,10},{7,11},{8,4},{9,5},{10,... | collective-permute-start | bytes 245768 | tf_op jit(solution)/shard_map/ppermute | solution.py:614
  17.9 2.5 %collective-permute-start.2 = (f32[4,40,128]{2,1,0:T(8,128)S(1)}, f32[4,40,128]{2,1,0:T(8,128)S(1)}, u32[]{:S(2)}, u32[]{:S(2)}) collective-permute-start(f32[4,40,128]{2,1,0:T(8,128)S(1)} %shard_map.117), channel_id=1, source_target_pairs={{0,1},{1,0},{2,3},{3,2},{4,8},{5,9},{6,10},{7,11},{8,4},{9,5},{10,... | collective-permute-start | bytes 245768 | tf_op jit(solution)/shard_map/ppermute | solution.py:614
  19.1 2.8 %collective-permute-start.14 = (f32[4,40,128]{2,1,0:T(8,128)S(1)}, f32[4,40,128]{2,1,0:T(8,128)S(1)}, u32[]{:S(2)}, u32[]{:S(2)}) collective-permute-start(f32[4,40,128]{2,1,0:T(8,128)S(1)} %shard_map.127), channel_id=1, source_target_pairs={{0,1},{1,0},{2,3},{3,2},{4,5},{5,4},{6,7},{7,6},{8,12},{9,13},{10,... | collective-permute-start | bytes 245768 | tf_op jit(solution)/shard_map/ppermute | solution.py:614
  19.7 2.3 %collective-permute-start.11 = (f32[4,40,128]{2,1,0:T(8,128)S(1)}, f32[4,40,128]{2,1,0:T(8,128)S(1)}, u32[]{:S(2)}, u32[]{:S(2)}) collective-permute-start(f32[4,40,128]{2,1,0:T(8,128)S(1)} %shard_map.125), channel_id=1, source_target_pairs={{0,1},{1,0},{2,3},{3,2},{4,5},{5,4},{6,7},{7,6},{8,12},{9,13},{10,... | collective-permute-start | bytes 245768 | tf_op jit(solution)/shard_map/ppermute | solution.py:614
  19.9 3.4 %collective-permute-start.6 = (f32[4,40,128]{2,1,0:T(8,128)S(1)}, f32[4,40,128]{2,1,0:T(8,128)S(1)}, u32[]{:S(2)}, u32[]{:S(2)}) collective-permute-start(f32[4,40,128]{2,1,0:T(8,128)S(1)} %shard_map.120), channel_id=1, source_target_pairs={{0,1},{1,0},{2,3},{3,2},{4,5},{5,4},{6,7},{7,6},{8,12},{9,13},{10,... | collective-permute-start | bytes 245768 | tf_op jit(solution)/shard_map/ppermute | solution.py:614
  20.4 2.8 %collective-permute-start.3 = (f32[4,40,128]{2,1,0:T(8,128)S(1)}, f32[4,40,128]{2,1,0:T(8,128)S(1)}, u32[]{:S(2)}, u32[]{:S(2)}) collective-permute-start(f32[4,40,128]{2,1,0:T(8,128)S(1)} %shard_map.118), channel_id=1, source_target_pairs={{0,1},{1,0},{2,3},{3,2},{4,5},{5,4},{6,7},{7,6},{8,12},{9,13},{10,... | collective-permute-start | bytes 245768 | tf_op jit(solution)/shard_map/ppermute | solution.py:614
  23.9 1.8 %collective-permute-start.7 = (f32[8,16,128]{2,1,0:T(8,128)S(1)}, f32[8,16,128]{2,1,0:T(8,128)S(1)}, u32[]{:S(2)}, u32[]{:S(2)}) collective-permute-start(f32[8,16,128]{2,1,0:T(8,128)S(1)} %shard_map.121), channel_id=1, source_target_pairs={{0,1},{1,0},{2,3},{3,2},{4,5},{5,4},{6,7},{7,6},{8,9},{9,8},{10,11... | collective-permute-start | bytes 196616 | tf_op jit(solution)/shard_map/ppermute | solution.py:707
  24.1 4.5 %collective-permute-start.16 = (f32[8,16,128]{2,1,0:T(8,128)S(1)}, f32[8,16,128]{2,1,0:T(8,128)S(1)}, u32[]{:S(2)}, u32[]{:S(2)}) collective-permute-start(f32[8,16,128]{2,1,0:T(8,128)S(1)} %add.22.refs_0_), channel_id=1, source_target_pairs={{0,2},{1,3},{2,0},{3,1},{4,6},{5,7},{6,4},{7,5},{8,10},{9,11},{10,... | collective-permute-start | bytes 196616 | tf_op jit(solution)/shard_map/ppermute | solution.py:709
  25.7 4.3 %collective-permute-start.8 = (f32[8,16,128]{2,1,0:T(8,128)S(1)}, f32[8,16,128]{2,1,0:T(8,128)S(1)}, u32[]{:S(2)}, u32[]{:S(2)}) collective-permute-start(f32[8,16,128]{2,1,0:T(8,128)S(1)} %add.21.refs_0_), channel_id=1, source_target_pairs={{0,2},{1,3},{2,0},{3,1},{4,6},{5,7},{6,4},{7,5},{8,10},{9,11},{10,... | collective-permute-start | bytes 196616 | tf_op jit(solution)/shard_map/ppermute | solution.py:709
  29.4 2.0 %collective-permute-start.26 = (f32[4,40,128]{2,1,0:T(8,128)S(1)}, f32[4,40,128]{2,1,0:T(8,128)S(1)}, u32[]{:S(2)}, u32[]{:S(2)}) collective-permute-start(f32[4,40,128]{2,1,0:T(8,128)S(1)} %get-tuple-element.50.carried_ref), channel_id=1, source_target_pairs={{0,1},{1,0},{2,3},{3,2},{4,5},{5,4},{6,7},{7,6},{8,12},{9,13},{10,... | collective-permute-start | bytes 245768 | tf_op jit(solution)/shard_map/ppermute | solution.py:614
  29.5 2.1 %collective-permute-start.23 = (f32[4,40,128]{2,1,0:T(8,128)S(1)}, f32[4,40,128]{2,1,0:T(8,128)S(1)}, u32[]{:S(2)}, u32[]{:S(2)}) collective-permute-start(f32[4,40,128]{2,1,0:T(8,128)S(1)} %get-tuple-element.49.carried_ref), channel_id=1, source_target_pairs={{0,1},{1,0},{2,3},{3,2},{4,5},{5,4},{6,7},{7,6},{8,12},{9,13},{10,... | collective-permute-start | bytes 245768 | tf_op jit(solution)/shard_map/ppermute | solution.py:614
  30.9 1.5 %collective-permute-start.17 = (f32[4,40,128]{2,1,0:T(8,128)S(1)}, f32[4,40,128]{2,1,0:T(8,128)S(1)}, u32[]{:S(2)}, u32[]{:S(2)}) collective-permute-start(f32[4,40,128]{2,1,0:T(8,128)S(1)} %get-tuple-element.47.carried_ref), channel_id=1, source_target_pairs={{0,1},{1,0},{2,3},{3,2},{4,5},{5,4},{6,7},{7,6},{8,12},{9,13},{10,... | collective-permute-start | bytes 245768 | tf_op jit(solution)/shard_map/ppermute | solution.py:614
  31.4 2.3 %collective-permute-start.27 = (f32[4,40,128]{2,1,0:T(8,128)S(1)}, f32[4,40,128]{2,1,0:T(8,128)S(1)}, u32[]{:S(2)}, u32[]{:S(2)}) collective-permute-start(f32[4,40,128]{2,1,0:T(8,128)S(1)} %shard_map.137), channel_id=1, source_target_pairs={{0,1},{1,0},{2,3},{3,2},{4,8},{5,9},{6,10},{7,11},{8,4},{9,5},{10,... | collective-permute-start | bytes 245768 | tf_op jit(solution)/shard_map/ppermute | solution.py:614
  31.6 15.3 %collective-permute-start.24 = (f32[4,40,128]{2,1,0:T(8,128)S(1)}, f32[4,40,128]{2,1,0:T(8,128)S(1)}, u32[]{:S(2)}, u32[]{:S(2)}) collective-permute-start(f32[4,40,128]{2,1,0:T(8,128)S(1)} %shard_map.135), channel_id=1, source_target_pairs={{0,1},{1,0},{2,3},{3,2},{4,8},{5,9},{6,10},{7,11},{8,4},{9,5},{10,... | collective-permute-start | bytes 245768 | tf_op jit(solution)/shard_map/ppermute | solution.py:614
  32.2 15.3 %collective-permute-start.21 = (f32[4,40,128]{2,1,0:T(8,128)S(1)}, f32[4,40,128]{2,1,0:T(8,128)S(1)}, u32[]{:S(2)}, u32[]{:S(2)}) collective-permute-start(f32[4,40,128]{2,1,0:T(8,128)S(1)} %shard_map.133), channel_id=1, source_target_pairs={{0,1},{1,0},{2,3},{3,2},{4,8},{5,9},{6,10},{7,11},{8,4},{9,5},{10,... | collective-permute-start | bytes 245768 | tf_op jit(solution)/shard_map/ppermute | solution.py:614
  32.5 16.7 %collective-permute-start.18 = (f32[4,40,128]{2,1,0:T(8,128)S(1)}, f32[4,40,128]{2,1,0:T(8,128)S(1)}, u32[]{:S(2)}, u32[]{:S(2)}) collective-permute-start(f32[4,40,128]{2,1,0:T(8,128)S(1)} %shard_map.131), channel_id=1, source_target_pairs={{0,1},{1,0},{2,3},{3,2},{4,8},{5,9},{6,10},{7,11},{8,4},{9,5},{10,... | collective-permute-start | bytes 245768 | tf_op jit(solution)/shard_map/ppermute | solution.py:614
  33.8 16.9 %collective-permute-start.28 = (f32[4,40,128]{2,1,0:T(8,128)S(1)}, f32[4,40,128]{2,1,0:T(8,128)S(1)}, u32[]{:S(2)}, u32[]{:S(2)}) collective-permute-start(f32[4,40,128]{2,1,0:T(8,128)S(1)} %shard_map.138), channel_id=1, source_target_pairs={{0,4},{1,5},{2,6},{3,7},{4,0},{5,1},{6,2},{7,3},{8,9},{9,8},{10,11... | collective-permute-start | bytes 245768 | tf_op jit(solution)/shard_map/ppermute | solution.py:614
  47.0 5.3 %collective-permute-start.25 = (f32[4,40,128]{2,1,0:T(8,128)S(1)}, f32[4,40,128]{2,1,0:T(8,128)S(1)}, u32[]{:S(2)}, u32[]{:S(2)}) collective-permute-start(f32[4,40,128]{2,1,0:T(8,128)S(1)} %shard_map.136), channel_id=1, source_target_pairs={{0,4},{1,5},{2,6},{3,7},{4,0},{5,1},{6,2},{7,3},{8,9},{9,8},{10,11... | collective-permute-start | bytes 245768 | tf_op jit(solution)/shard_map/ppermute | solution.py:614
  47.5 5.6 %collective-permute-start.22 = (f32[4,40,128]{2,1,0:T(8,128)S(1)}, f32[4,40,128]{2,1,0:T(8,128)S(1)}, u32[]{:S(2)}, u32[]{:S(2)}) collective-permute-start(f32[4,40,128]{2,1,0:T(8,128)S(1)} %shard_map.134), channel_id=1, source_target_pairs={{0,4},{1,5},{2,6},{3,7},{4,0},{5,1},{6,2},{7,3},{8,9},{9,8},{10,11... | collective-permute-start | bytes 245768 | tf_op jit(solution)/shard_map/ppermute | solution.py:614
  49.2 4.8 %collective-permute-start.19 = (f32[4,40,128]{2,1,0:T(8,128)S(1)}, f32[4,40,128]{2,1,0:T(8,128)S(1)}, u32[]{:S(2)}, u32[]{:S(2)}) collective-permute-start(f32[4,40,128]{2,1,0:T(8,128)S(1)} %shard_map.132), channel_id=1, source_target_pairs={{0,4},{1,5},{2,6},{3,7},{4,0},{5,1},{6,2},{7,3},{8,9},{9,8},{10,11... | collective-permute-start | bytes 245768 | tf_op jit(solution)/shard_map/ppermute | solution.py:614
  55.1 4.6 %collective-permute-start.29 = (f32[168,128]{1,0:T(8,128)S(1)}, f32[168,128]{1,0:T(8,128)S(1)}, u32[]{:S(2)}, u32[]{:S(2)}) collective-permute-start(f32[168,128]{1,0:T(8,128)S(1)} %get-tuple-element.51.own_ref), channel_id=1, source_target_pairs={{0,16},{16,0},{1,17},{17,1},{2,18},{18,2},{3,19},{19,3},{4,20},{20... | collective-permute-start | bytes 258056 | tf_op jit(solution)/shard_map/ppermute | solution.py:587
  61.1 3.6 %collective-permute-start.31 = (f32[8,128]{1,0:T(8,128)S(1)}, f32[8,128]{1,0:T(8,128)S(1)}, u32[]{:S(2)}, u32[]{:S(2)}) collective-permute-start(f32[8,128]{1,0:T(8,128)S(1)} %add.23), channel_id=1, source_target_pairs={{0,2},{1,3},{2,0},{3,1},{4,6},{5,7},{6,4},{7,5},{8,10},{9,11},{10,... | collective-permute-start | bytes 12296 | tf_op jit(solution)/shard_map/ppermute | solution.py:625
  64.7 4.8 %collective-permute-start.32 = (f32[8,128]{1,0:T(8,128)S(1)}, f32[8,128]{1,0:T(8,128)S(1)}, u32[]{:S(2)}, u32[]{:S(2)}) collective-permute-start(f32[8,128]{1,0:T(8,128)S(1)} %add.24), channel_id=1, source_target_pairs={{0,4},{4,0},{8,12},{12,8},{1,5},{5,1},{9,13},{13,9},{2,6},{6,2},{1... | collective-permute-start | bytes 12296 | tf_op jit(solution)/shard_map/ppermute | solution.py:625
  65.8 4.5 %collective-permute-start.33 = (f32[8,128]{1,0:T(8,128)S(1)}, f32[8,128]{1,0:T(8,128)S(1)}, u32[]{:S(2)}, u32[]{:S(2)}) collective-permute-start(f32[8,128]{1,0:T(8,128)S(1)} %add.24), channel_id=1, source_target_pairs={{0,8},{4,12},{8,0},{12,4},{1,9},{5,13},{9,1},{13,5},{2,10},{6,14},... | collective-permute-start | bytes 12296 | tf_op jit(solution)/shard_map/ppermute | solution.py:625
  65.8 5.4 %collective-permute-start.34 = (f32[8,128]{1,0:T(8,128)S(1)}, f32[8,128]{1,0:T(8,128)S(1)}, u32[]{:S(2)}, u32[]{:S(2)}) collective-permute-start(f32[8,128]{1,0:T(8,128)S(1)} %add.24), channel_id=1, source_target_pairs={{0,12},{4,8},{8,4},{12,0},{1,13},{5,9},{9,5},{13,1},{2,14},{6,10},... | collective-permute-start | bytes 12296 | tf_op jit(solution)/shard_map/ppermute | solution.py:625
  (10 other events, 47.6 us)

commit v3 on v2

--- a/solution.py
+++ b/solution.py
@@ -272,10 +272,9 @@
     rows, columns = pairs * r, 3 * pairs * c
     exact = functools.partial(jnp.dot, precision=lax.Precision.HIGHEST, preferred_element_type=f32)
     block = lambda at, size: jnp.floor((at + 0.5) * (1.0 / size))
-    at_row, at_column = iota((rows, r), 0), iota((c, columns), 1)
-    pick_row = (at_row - block(at_row, r) * r == iota((rows, r), 1)).astype(f32)
+    at_column = iota((c, columns), 1)
     pick_column = (at_column - block(at_column, c) * c == iota((c, columns), 0)).astype(f32)
-    everywhere = exact(exact(pick_row, source), pick_column)
+    everywhere = jnp.concatenate([exact(source, pick_column)] * pairs, axis=0)
     column = iota((1, columns), 1)
     part = block(column, pairs * c)
     own = block(iota((rows, 1), 0), r) == block(column - part * (pairs * c), c)
@@ -340,16 +339,16 @@
         def store(y, ch, at, base, value, last, part=part):
             if last is not None:
                 for s in range(4):
-                    out_refs[part * chunks + ch][s, at, :] = last[s]
+                    out_refs[sum(chunks[:part]) + ch][s, at, :] = last[s]
 
         sweep_chunks(
-            lambda y, base: f_ref[y, pl.ds(pl.multiple_of(base, 8), rows_at_once(half // chunks)), :],
+            lambda y, base, part=part: f_ref[y, pl.ds(pl.multiple_of(base, 8), rows_at_once(half // chunks[part])), :],
             store,
             lambda ch, at: [jnp.zeros((1, cells), f32)] * 4,
             lat_ref[part, :1],
             rows,
             half,
-            chunks,
+            chunks[part],
             False,
         )
 
@@ -430,7 +429,7 @@
 def k_lon_bwd(rows, k, cells, chunks, count, blocks, *refs):
     g_refs, lat_ref, block_ref, table_ref, rest = refs[:2], refs[2], refs[3], refs[4], refs[5:]
     block = (blocks - 1.0) - block_ref[...]
-    d_ref, r_ref, known_ref, inside_ref, sent_ref, p_ref = rest[2 * count :]
+    d_ref, r_ref, known_ref, inside_ref, sent_ref, p_ref = rest[sum(count) :]
     d_ref = d_ref.reshape(k * rows, cells)
     r_ref = r_ref.reshape(k * rows, cells)
     half = k // 2
@@ -438,16 +437,16 @@
         g_ref = g_refs[part]
 
         def store(y, ch, at, base, value, last, part=part):
-            p_ref[part, y, pl.ds(pl.multiple_of(base, 8), rows_at_once(half // chunks)), :] = value
+            p_ref[part, y, pl.ds(pl.multiple_of(base, 8), rows_at_once(half // chunks[part])), :] = value
 
         sweep_chunks(
-            lambda y, base: g_ref[y, pl.ds(pl.multiple_of(base, 8), rows_at_once(half // chunks)), :],
+            lambda y, base: g_ref[y, pl.ds(pl.multiple_of(base, 8), rows_at_once(half // chunks[part])), :],
             store,
-            entering_states(rest[part * count : (part + 1) * count], chunks, block),
+            entering_states(rest[sum(count[:part]) : sum(count[: part + 1])], chunks[part], block),
             lat_ref[part, :1],
             rows,
             half,
-            chunks,
+            chunks[part],
             True,
         )
 
@@ -654,7 +653,7 @@
     n_lon, n_mem = lax.axis_size("lon"), lax.axis_size("mem")
     half = k // 2
     pairs = mcount // 2
-    chunks, back_chunks = 2, 2
+    chunks, back_chunks = (2, 1), (2, 1)
     states = lambda chunks: (sds(4, half // chunks, cells),) * chunks
 
     decays = jnp.concatenate([lat_decay, lon_decay]).reshape(1, cells + rows)
@@ -662,7 +661,7 @@
         functools.partial(k_tables, rows, cells),
         (sds(rows, cells), sds(2, 8, cells), jax.ShapeDtypeStruct((rows, 3 * cells, 2 * cells), bf16), sds(8, cells)),
         [decays],
-        cost=10**9,
+        cost=4 * 10**8,
     )
     inside, carried = call(
         functools.partial(k_lon_fwd, rows, k, cells), (sds(rows, k, cells), sds(4 * rows, k)), [direction, tables]
@@ -685,16 +684,16 @@
     blocks = lon_exchange(carried, False)
     fa, fb, *parts = call(
         functools.partial(k_lat_first, rows, k, cells, n_lon, chunks),
-        (sds(rows, half, cells),) * 2 + states(chunks) * 2,
+        (sds(rows, half, cells),) * 2 + states(chunks[0]) + states(chunks[1]),
         [inside, lonc, latc, *blocks],
     )
-    got = lat_carry([parts[:chunks], parts[chunks:]], latc, rows, False)
-    count = len(got[0])
+    got = lat_carry([parts[: chunks[0]], parts[chunks[0] :]], latc, rows, False)
+    count = tuple(len(g) for g in got)
     fields = (fa, fb)
     inc = [None, None]
     for part in range(2):
         inc[part] = call(
-            functools.partial(k_increment, rows, half, part, chunks, count, pairs, levels),
+            functools.partial(k_increment, rows, half, part, chunks[part], count[part], pairs, levels),
             sds(rows, levels // 2, cells),
             [fields[part], latc, block, packed[part], mask, out_modes, *got[part]],
             scratch=[pltpu.VMEM((rows, half, cells), f32)],
@@ -708,12 +707,12 @@
             step *= 2
         other = lax.ppermute(v, "mem", [(i, i ^ step) for i in range(n_mem)])
         grads[part], *sends[part] = call(
-            functools.partial(k_gradient, rows, half, part, back_chunks, pairs, levels),
-            (sds(rows, half, cells),) + states(back_chunks),
+            functools.partial(k_gradient, rows, half, part, back_chunks[part], pairs, levels),
+            (sds(rows, half, cells),) + states(back_chunks[part]),
             [v, other, obs_weight, packed[part], mask, in_modes, latc],
         )
     got = lat_carry(sends, latc, rows, True)
-    count = len(got[0])
+    count = tuple(len(g) for g in got)
     known = call(functools.partial(k_known, rows, k, cells), sds(k, cells), [direction, residual, lonc], cost=10**9)
     inside, sent = call(
         functools.partial(k_lon_bwd, rows, k, cells, back_chunks, count, lax.axis_size("lat")),

time: 72.9 us -> 83 us (1.14)
  waiting for transfers between devices: 19.4 us -> 27.9 us
  starting transfers between devices: 38 us -> 41 us
    ppermute x2, waiting for transfers between devices: 1.31 us -> 5.47 us  [iteration(): other = lax.ppermute(v, 'mem', [(i, i ^ step) for i in range(n_mem)])]
    ppermute x24 -> x18, waiting for transfers between devices: 8.18 us -> 11.6 us  [lat_carry(): got[c][i].append(lax.ppermute(v, ('lat', 'mem'), pairs))]
    ppermute x24 -> x18, starting transfers between devices: 24.1 us -> 26.9 us  [lat_carry(): got[c][i].append(lax.ppermute(v, ('lat', 'mem'), pairs))]
    pallas_call x32 -> x28, Pallas kernels: 12.9 us -> 12.1 us  [call(): pl.pallas_call(body, out_shape=outs, in_specs=specs or [VM] * len(ins), o...]
  transfers between devices with their start and end apart: 35 -> 29, of which waited for: 17 -> 18; matrix products, arithmetic and copies ran while one was open for 0% -> 0% of each run, Pallas kernels for 12% -> 9%
where the time goes in v3:
time: 83 us; the launch traced here: 82.8 us
  starting transfers between devices  41 us (49%)
  waiting for transfers between devices  27.9 us (34%)
  Pallas kernels  12.1 us (15%)
  between operations  0.96 us (1%)
    ppermute x18, starting transfers between devices, lat_carry(): got[c][i].append(lax.ppermute(v, ('lat', 'mem'), pairs))  26.9 us
    pallas_call x28, Pallas kernels, call(): pl.pallas_call(body, out_shape=outs, in_specs=specs or [VM] * len(ins), o...  12.1 us
    ppermute x18, waiting for transfers between devices, lat_carry(): got[c][i].append(lax.ppermute(v, ('lat', 'mem'), pairs))  11.6 us
    ppermute x5, starting transfers between devices, all_sum(): lax.ppermute(v, axes, [(i, i ^ m) for i in range(total)])  5.97 us
    ppermute x2, waiting for transfers between devices, iteration(): other = lax.ppermute(v, 'mem', [(i, i ^ step) for i in range(n_mem)])  5.47 us
    ppermute x5, waiting for transfers between devices, all_sum(): lax.ppermute(v, axes, [(i, i ^ m) for i in range(total)])  5.26 us
    ppermute x2, waiting for transfers between devices, lon_exchange(): lax.ppermute(carried, 'lon', [(j, (j + sign * r) % n) for j in range(n)])  4.89 us
    ppermute x2, starting transfers between devices, lon_exchange(): lax.ppermute(carried, 'lon', [(j, (j + sign * r) % n) for j in range(n)])  4.56 us
  transfers between devices with their start and end apart: 29, of which 18 were waited for; matrix products, arithmetic and copies ran while one was open for 0% of the time, Pallas kernels for 9%

profile of v3, /device:TPU:0, one launch (start us, length us, event | category | flops | bytes accessed | tf_op | source)
XLA Modules:
  0.0 82.8 jit_solution(16989226194078477390)
XLA Ops:
  2.4 3.0 %collective-permute-start = (f32[32,160]{1,0:T(8,128)S(1)}, f32[32,160]{1,0:T(8,128)S(1)}, u32[]{:S(2)}, u32[]{:S(2)}) collective-permute-start(f32[32,160]{1,0:T(8,128)S(1)} %get-tuple-element.31.refs_4_), channel_id=1, source_target_pairs={{0,16},{16,0},{1,17},{17,1},{2,18},{18,2},{3,19},{19,3},{4,20},{20... | collective-permute-start | bytes 61448 | tf_op jit(solution)/shard_map/ppermute | solution.py:586
  5.4 1.9 %collective-permute-done.refs_3_ = f32[32,160]{1,0:T(8,128)S(1)} collective-permute-done((f32[32,160]{1,0:T(8,128)S(1)}, f32[32,160]{1,0:T(8,128)S(1)}, u32[]{:S(2)}, u32[]{:S(2)}) %collective-permute-start) | collective-permute-done | bytes 20512 | tf_op jit(solution)/shard_map/ppermute | solution.py:586
  8.0 2.2 %collective-permute-start.9 = (f32[4,80,128]{2,1,0:T(8,128)S(1)}, f32[4,80,128]{2,1,0:T(8,128)S(1)}, u32[]{:S(2)}, u32[]{:S(2)}) collective-permute-start(f32[4,80,128]{2,1,0:T(8,128)S(1)} %get-tuple-element.42.carried_ref), channel_id=1, source_target_pairs={{0,4},{1,5},{2,6},{3,7},{4,0},{5,1},{6,2},{7,3},{8,9},{9,8},{10,11... | collective-permute-start | bytes 491528 | tf_op jit(solution)/shard_map/ppermute | solution.py:613
  10.2 3.3 %collective-permute-done.9.got_ref.refs_6_ = f32[4,80,128]{2,1,0:T(8,128)S(1)} collective-permute-done((f32[4,80,128]{2,1,0:T(8,128)S(1)}, f32[4,80,128]{2,1,0:T(8,128)S(1)}, u32[]{:S(2)}, u32[]{:S(2)}) %collective-permute-start.9) | collective-permute-done | bytes 163872 | tf_op jit(solution)/shard_map/ppermute | solution.py:613
  13.6 1.4 %collective-permute-done.10.got_ref.refs_7_ = f32[4,80,128]{2,1,0:T(8,128)S(1)} collective-permute-done((f32[4,80,128]{2,1,0:T(8,128)S(1)}, f32[4,80,128]{2,1,0:T(8,128)S(1)}, u32[]{:S(2)}, u32[]{:S(2)}) %collective-permute-start.10) | collective-permute-done | bytes 163872 | tf_op jit(solution)/shard_map/ppermute | solution.py:613
  15.3 1.1 %shard_map.115 = (f32[2624,128]{1,0:T(8,128)S(1)}, f32[2624,128]{1,0:T(8,128)S(1)}) custom-call(bf16[20,32,8,128]{3,2,1,0:T(8,128)(2,1)S(1)} %copy-done.4), custom_call_target="tpu_custom_call" | custom-call | flops 1000000000 | bytes 1000 | tf_op jit(solution)/shard_map/pallas_call | solution.py:567
  16.3 5.9 %collective-permute-start.4 = (f32[4,40,128]{2,1,0:T(8,128)S(1)}, f32[4,40,128]{2,1,0:T(8,128)S(1)}, u32[]{:S(2)}, u32[]{:S(2)}) collective-permute-start(f32[4,40,128]{2,1,0:T(8,128)S(1)} %get-tuple-element.38.carried_ref), channel_id=1, source_target_pairs={{0,4},{1,5},{2,6},{3,7},{4,0},{5,1},{6,2},{7,3},{8,9},{9,8},{10,11... | collective-permute-start | bytes 245768 | tf_op jit(solution)/shard_map/ppermute | solution.py:613
  22.3 0.8 %shard_map.116 = (f32[80,128]{1,0:T(8,128)S(1)}, bf16[320,240]{1,0:T(8,128)(2,1)S(1)}) custom-call(f32[8,32]{1,0:T(8,128)S(1)} %copy-done.5, s32[20]{0:T(128)S(1)} %copy-done.6), custom_call_target="tpu_custom_call" | custom-call | flops 1000000000 | bytes 1000 | tf_op jit(solution)/shard_map/pallas_call | solution.py:567
  24.2 1.3 %collective-permute-done.4.got_ref.refs_9_ = f32[4,40,128]{2,1,0:T(8,128)S(1)} collective-permute-done((f32[4,40,128]{2,1,0:T(8,128)S(1)}, f32[4,40,128]{2,1,0:T(8,128)S(1)}, u32[]{:S(2)}, u32[]{:S(2)}) %collective-permute-start.4) | collective-permute-done | bytes 81952 | tf_op jit(solution)/shard_map/ppermute | solution.py:613
  25.6 1.4 %collective-permute-done.1.got_ref.refs_6_ = f32[4,40,128]{2,1,0:T(8,128)S(1)} collective-permute-done((f32[4,40,128]{2,1,0:T(8,128)S(1)}, f32[4,40,128]{2,1,0:T(8,128)S(1)}, u32[]{:S(2)}, u32[]{:S(2)}) %collective-permute-start.1) | collective-permute-done | bytes 81952 | tf_op jit(solution)/shard_map/ppermute | solution.py:613
  27.2 1.6 %collective-permute-start.13 = (f32[8,16,128]{2,1,0:T(8,128)S(1)}, f32[8,16,128]{2,1,0:T(8,128)S(1)}, u32[]{:S(2)}, u32[]{:S(2)}) collective-permute-start(f32[8,16,128]{2,1,0:T(8,128)S(1)} %add.22.refs_0_), channel_id=1, source_target_pairs={{0,2},{1,3},{2,0},{3,1},{4,6},{5,7},{6,4},{7,5},{8,10},{9,11},{10,... | collective-permute-start | bytes 196616 | tf_op jit(solution)/shard_map/ppermute | solution.py:708
  29.1 2.7 %collective-permute-done.13.refs_1_ = f32[8,16,128]{2,1,0:T(8,128)S(1)} collective-permute-done((f32[8,16,128]{2,1,0:T(8,128)S(1)}, f32[8,16,128]{2,1,0:T(8,128)S(1)}, u32[]{:S(2)}, u32[]{:S(2)}) %collective-permute-start.13) | collective-permute-done | bytes 65568 | tf_op jit(solution)/shard_map/ppermute | solution.py:708
  31.8 0.8 shard_map.127
  36.6 1.6 %collective-permute-start.8 = (f32[8,16,128]{2,1,0:T(8,128)S(1)}, f32[8,16,128]{2,1,0:T(8,128)S(1)}, u32[]{:S(2)}, u32[]{:S(2)}) collective-permute-start(f32[8,16,128]{2,1,0:T(8,128)S(1)} %add.21.refs_0_), channel_id=1, source_target_pairs={{0,2},{1,3},{2,0},{3,1},{4,6},{5,7},{6,4},{7,5},{8,10},{9,11},{10,... | collective-permute-start | bytes 196616 | tf_op jit(solution)/shard_map/ppermute | solution.py:708
  38.2 2.7 %collective-permute-done.8.refs_1_ = f32[8,16,128]{2,1,0:T(8,128)S(1)} collective-permute-done((f32[8,16,128]{2,1,0:T(8,128)S(1)}, f32[8,16,128]{2,1,0:T(8,128)S(1)}, u32[]{:S(2)}, u32[]{:S(2)}) %collective-permute-start.8) | collective-permute-done | bytes 65568 | tf_op jit(solution)/shard_map/ppermute | solution.py:708
  43.9 13.2 %collective-permute-start.22 = (f32[4,80,128]{2,1,0:T(8,128)S(1)}, f32[4,80,128]{2,1,0:T(8,128)S(1)}, u32[]{:S(2)}, u32[]{:S(2)}) collective-permute-start(f32[4,80,128]{2,1,0:T(8,128)S(1)} %shard_map.134), channel_id=1, source_target_pairs={{0,4},{1,5},{2,6},{3,7},{4,0},{5,1},{6,2},{7,3},{8,9},{9,8},{10,11... | collective-permute-start | bytes 491528 | tf_op jit(solution)/shard_map/ppermute | solution.py:613
  57.1 0.8 shard_map.128.refs_4_
  58.6 2.1 %collective-permute-start.16 = (f32[4,40,128]{2,1,0:T(8,128)S(1)}, f32[4,40,128]{2,1,0:T(8,128)S(1)}, u32[]{:S(2)}, u32[]{:S(2)}) collective-permute-start(f32[4,40,128]{2,1,0:T(8,128)S(1)} %shard_map.130), channel_id=1, source_target_pairs={{0,4},{1,5},{2,6},{3,7},{4,0},{5,1},{6,2},{7,3},{8,9},{9,8},{10,11... | collective-permute-start | bytes 245768 | tf_op jit(solution)/shard_map/ppermute | solution.py:613
  60.7 0.9 %shard_map.135.refs_16_ = f32[160,128]{1,0:T(8,128)S(1)} custom-call(f32[160,8,128]{2,1,0:T(8,128)S(1)} %copy-done, f32[160,8,128]{2,1,0:T(8,128)S(1)} %copy-done.1, f32[8,128]{1,0:T(8,128)S(1)} %get-tuple-element.27.refs_1_.lon_ref), custom_call_target="tpu_custom_call" | custom-call | flops 1000000000 | bytes 1000 | tf_op jit(solution)/shard_map/pallas_call | solution.py:567
  61.6 1.3 %collective-permute-done.19.refs_10_ = f32[4,40,128]{2,1,0:T(8,128)S(1)} collective-permute-done((f32[4,40,128]{2,1,0:T(8,128)S(1)}, f32[4,40,128]{2,1,0:T(8,128)S(1)}, u32[]{:S(2)}, u32[]{:S(2)}) %collective-permute-start.19) | collective-permute-done | bytes 81952 | tf_op jit(solution)/shard_map/ppermute | solution.py:613
  62.9 0.9 %collective-permute-done.16.refs_7_ = f32[4,40,128]{2,1,0:T(8,128)S(1)} collective-permute-done((f32[4,40,128]{2,1,0:T(8,128)S(1)}, f32[4,40,128]{2,1,0:T(8,128)S(1)}, u32[]{:S(2)}, u32[]{:S(2)}) %collective-permute-start.16) | collective-permute-done | bytes 81952 | tf_op jit(solution)/shard_map/ppermute | solution.py:613
  63.8 1.1 %shard_map.136 = (f32[8,160,128]{2,1,0:T(8,128)S(1)}, f32[168,128]{1,0:T(8,128)S(1)}) custom-call(f32[8,80,128]{2,1,0:T(8,128)S(1)} %get-tuple-element.39.refs_0_, f32[8,80,128]{2,1,0:T(8,128)S(1)} %get-tuple-element.43.refs_1_, f32[2,8,128]{2,1,0:T(8,128)S(1)} %get-tuple-element.30.refs_2_.lat_ref.refs_1_.refs_6_, ...), custom_call_target="tpu_custom_call" | custom-call | tf_op jit(solution)/shard_map/pallas_call | solution.py:567
  64.8 1.6 %collective-permute-start.23 = (f32[168,128]{1,0:T(8,128)S(1)}, f32[168,128]{1,0:T(8,128)S(1)}, u32[]{:S(2)}, u32[]{:S(2)}) collective-permute-start(f32[168,128]{1,0:T(8,128)S(1)} %get-tuple-element.47.own_ref), channel_id=1, source_target_pairs={{0,16},{16,0},{1,17},{17,1},{2,18},{18,2},{3,19},{19,3},{4,20},{20... | collective-permute-start | bytes 258056 | tf_op jit(solution)/shard_map/ppermute | solution.py:586
  66.4 3.0 %collective-permute-done.23.other_ref = f32[168,128]{1,0:T(8,128)S(1)} collective-permute-done((f32[168,128]{1,0:T(8,128)S(1)}, f32[168,128]{1,0:T(8,128)S(1)}, u32[]{:S(2)}, u32[]{:S(2)}) %collective-permute-start.23) | collective-permute-done | bytes 86048 | tf_op jit(solution)/shard_map/ppermute | solution.py:586
  69.7 1.2 %collective-permute-done.24 = f32[8,128]{1,0:T(8,128)S(1)} collective-permute-done((f32[8,128]{1,0:T(8,128)S(1)}, f32[8,128]{1,0:T(8,128)S(1)}, u32[]{:S(2)}, u32[]{:S(2)}) %collective-permute-start.24) | collective-permute-done | bytes 4128 | tf_op jit(solution)/shard_map/ppermute | solution.py:624
  70.9 1.5 %collective-permute-start.25 = (f32[8,128]{1,0:T(8,128)S(1)}, f32[8,128]{1,0:T(8,128)S(1)}, u32[]{:S(2)}, u32[]{:S(2)}) collective-permute-start(f32[8,128]{1,0:T(8,128)S(1)} %add.23), channel_id=1, source_target_pairs={{0,2},{1,3},{2,0},{3,1},{4,6},{5,7},{6,4},{7,5},{8,10},{9,11},{10,... | collective-permute-start | bytes 12296 | tf_op jit(solution)/shard_map/ppermute | solution.py:624
  72.4 2.1 %collective-permute-done.25 = f32[8,128]{1,0:T(8,128)S(1)} collective-permute-done((f32[8,128]{1,0:T(8,128)S(1)}, f32[8,128]{1,0:T(8,128)S(1)}, u32[]{:S(2)}, u32[]{:S(2)}) %collective-permute-start.25) | collective-permute-done | bytes 4128 | tf_op jit(solution)/shard_map/ppermute | solution.py:624
  74.5 1.4 %collective-permute-start.26 = (f32[8,128]{1,0:T(8,128)S(1)}, f32[8,128]{1,0:T(8,128)S(1)}, u32[]{:S(2)}, u32[]{:S(2)}) collective-permute-start(f32[8,128]{1,0:T(8,128)S(1)} %add.24), channel_id=1, source_target_pairs={{0,4},{4,0},{8,12},{12,8},{1,5},{5,1},{9,13},{13,9},{2,6},{6,2},{1... | collective-permute-start | bytes 12296 | tf_op jit(solution)/shard_map/ppermute | solution.py:624
  75.9 3.0 %collective-permute-start.28 = (f32[8,128]{1,0:T(8,128)S(1)}, f32[8,128]{1,0:T(8,128)S(1)}, u32[]{:S(2)}, u32[]{:S(2)}) collective-permute-start(f32[8,128]{1,0:T(8,128)S(1)} %add.24), channel_id=1, source_target_pairs={{0,12},{4,8},{8,4},{12,0},{1,13},{5,9},{9,5},{13,1},{2,14},{6,10},... | collective-permute-start | bytes 12296 | tf_op jit(solution)/shard_map/ppermute | solution.py:624
  79.3 1.1 %collective-permute-done.27 = f32[8,128]{1,0:T(8,128)S(1)} collective-permute-done((f32[8,128]{1,0:T(8,128)S(1)}, f32[8,128]{1,0:T(8,128)S(1)}, u32[]{:S(2)}, u32[]{:S(2)}) %collective-permute-start.27) | collective-permute-done | bytes 4128 | tf_op jit(solution)/shard_map/ppermute | solution.py:624
  80.4 0.9 %collective-permute-done.28 = f32[8,128]{1,0:T(8,128)S(1)} collective-permute-done((f32[8,128]{1,0:T(8,128)S(1)}, f32[8,128]{1,0:T(8,128)S(1)}, u32[]{:S(2)}, u32[]{:S(2)}) %collective-permute-start.28) | collective-permute-done | bytes 4128 | tf_op jit(solution)/shard_map/ppermute | solution.py:624
  81.3 1.5 %shard_map.139 = (f32[160,8,128]{2,1,0:T(8,128)}, f32[160,8,128]{2,1,0:T(8,128)}, f32[160,8,128]{2,1,0:T(8,128)}) custom-call(f32[8,128]{1,0:T(8,128)S(1)} %add_add_fusion.sums_ref, f32[160,8,128]{2,1,0:T(8,128)S(1)} %copy-done.2, f32[160,8,128]{2,1,0:T(8,128)S(1)} %copy-done.1, f32[160,8,128]{2,1,0:T(8,128)S(1)} %copy-done, f32[160,8,128]{2,1,0:T(8,128)S(1)} %bitcast.2), custom_call_target="tpu_custom_call" | custom-call | tf_op jit(solution)/shard_map/pallas_call | solution.py:567
  (74 shorter events, 12.7 us)
Async XLA Ops:
  2.4 12.9 %copy-start.4 = (bf16[20,32,8,128]{3,2,1,0:T(8,128)(2,1)S(1)}, bf16[20,32,8,128]{3,2,1,0:T(8,128)(2,1)}, u32[]{:S(2)}) copy-start(bf16[20,32,8,128]{3,2,1,0:T(8,128)(2,1)} %m_ref.1) | copy-start | bytes 3932164
  2.4 4.9 %collective-permute-start = (f32[32,160]{1,0:T(8,128)S(1)}, f32[32,160]{1,0:T(8,128)S(1)}, u32[]{:S(2)}, u32[]{:S(2)}) collective-permute-start(f32[32,160]{1,0:T(8,128)S(1)} %get-tuple-element.31.refs_4_), channel_id=1, source_target_pairs={{0,16},{16,0},{1,17},{17,1},{2,18},{18,2},{3,19},{19,3},{4,20},{20... | collective-permute-start | bytes 61448 | tf_op jit(solution)/shard_map/ppermute | solution.py:586
  8.0 5.5 %collective-permute-start.9 = (f32[4,80,128]{2,1,0:T(8,128)S(1)}, f32[4,80,128]{2,1,0:T(8,128)S(1)}, u32[]{:S(2)}, u32[]{:S(2)}) collective-permute-start(f32[4,80,128]{2,1,0:T(8,128)S(1)} %get-tuple-element.42.carried_ref), channel_id=1, source_target_pairs={{0,4},{1,5},{2,6},{3,7},{4,0},{5,1},{6,2},{7,3},{8,9},{9,8},{10,11... | collective-permute-start | bytes 491528 | tf_op jit(solution)/shard_map/ppermute | solution.py:613
  13.5 1.5 %collective-permute-start.10 = (f32[4,80,128]{2,1,0:T(8,128)S(1)}, f32[4,80,128]{2,1,0:T(8,128)S(1)}, u32[]{:S(2)}, u32[]{:S(2)}) collective-permute-start(f32[4,80,128]{2,1,0:T(8,128)S(1)} %shard_map.124), channel_id=1, source_target_pairs={{0,1},{1,0},{2,3},{3,2},{4,8},{5,9},{6,10},{7,11},{8,4},{9,5},{10,... | collective-permute-start | bytes 491528 | tf_op jit(solution)/shard_map/ppermute | solution.py:613
  15.0 7.3 %copy-start.5 = (f32[8,32]{1,0:T(8,128)S(1)}, f32[8,32]{1,0:T(8,128)}, u32[]{:S(2)}) copy-start(f32[8,32]{1,0:T(8,128)} %v_ref.3) | copy-start | bytes 3076
  15.1 8.1 %collective-permute-start.11 = (f32[4,80,128]{2,1,0:T(8,128)S(1)}, f32[4,80,128]{2,1,0:T(8,128)S(1)}, u32[]{:S(2)}, u32[]{:S(2)}) collective-permute-start(f32[4,80,128]{2,1,0:T(8,128)S(1)} %shard_map.125), channel_id=1, source_target_pairs={{0,1},{1,0},{2,3},{3,2},{4,5},{5,4},{6,7},{7,6},{8,12},{9,13},{10,... | collective-permute-start | bytes 491528 | tf_op jit(solution)/shard_map/ppermute | solution.py:613
  16.3 9.2 %collective-permute-start.4 = (f32[4,40,128]{2,1,0:T(8,128)S(1)}, f32[4,40,128]{2,1,0:T(8,128)S(1)}, u32[]{:S(2)}, u32[]{:S(2)}) collective-permute-start(f32[4,40,128]{2,1,0:T(8,128)S(1)} %get-tuple-element.38.carried_ref), channel_id=1, source_target_pairs={{0,4},{1,5},{2,6},{3,7},{4,0},{5,1},{6,2},{7,3},{8,9},{9,8},{10,11... | collective-permute-start | bytes 245768 | tf_op jit(solution)/shard_map/ppermute | solution.py:613
  22.2 4.9 %collective-permute-start.1 = (f32[4,40,128]{2,1,0:T(8,128)S(1)}, f32[4,40,128]{2,1,0:T(8,128)S(1)}, u32[]{:S(2)}, u32[]{:S(2)}) collective-permute-start(f32[4,40,128]{2,1,0:T(8,128)S(1)} %get-tuple-element.37.carried_ref), channel_id=1, source_target_pairs={{0,4},{1,5},{2,6},{3,7},{4,0},{5,1},{6,2},{7,3},{8,9},{9,8},{10,11... | collective-permute-start | bytes 245768 | tf_op jit(solution)/shard_map/ppermute | solution.py:613
  23.9 3.2 %collective-permute-start.12 = (f32[8,16,128]{2,1,0:T(8,128)S(1)}, f32[8,16,128]{2,1,0:T(8,128)S(1)}, u32[]{:S(2)}, u32[]{:S(2)}) collective-permute-start(f32[8,16,128]{2,1,0:T(8,128)S(1)} %shard_map.126), channel_id=1, source_target_pairs={{0,1},{1,0},{2,3},{3,2},{4,5},{5,4},{6,7},{7,6},{8,9},{9,8},{10,11... | collective-permute-start | bytes 196616 | tf_op jit(solution)/shard_map/ppermute | solution.py:706
  25.6 7.1 %collective-permute-start.5 = (f32[4,40,128]{2,1,0:T(8,128)S(1)}, f32[4,40,128]{2,1,0:T(8,128)S(1)}, u32[]{:S(2)}, u32[]{:S(2)}) collective-permute-start(f32[4,40,128]{2,1,0:T(8,128)S(1)} %shard_map.119), channel_id=1, source_target_pairs={{0,1},{1,0},{2,3},{3,2},{4,8},{5,9},{6,10},{7,11},{8,4},{9,5},{10,... | collective-permute-start | bytes 245768 | tf_op jit(solution)/shard_map/ppermute | solution.py:613
  27.1 6.2 %collective-permute-start.2 = (f32[4,40,128]{2,1,0:T(8,128)S(1)}, f32[4,40,128]{2,1,0:T(8,128)S(1)}, u32[]{:S(2)}, u32[]{:S(2)}) collective-permute-start(f32[4,40,128]{2,1,0:T(8,128)S(1)} %shard_map.117), channel_id=1, source_target_pairs={{0,1},{1,0},{2,3},{3,2},{4,8},{5,9},{6,10},{7,11},{8,4},{9,5},{10,... | collective-permute-start | bytes 245768 | tf_op jit(solution)/shard_map/ppermute | solution.py:613
  27.2 4.5 %collective-permute-start.13 = (f32[8,16,128]{2,1,0:T(8,128)S(1)}, f32[8,16,128]{2,1,0:T(8,128)S(1)}, u32[]{:S(2)}, u32[]{:S(2)}) collective-permute-start(f32[8,16,128]{2,1,0:T(8,128)S(1)} %add.22.refs_0_), channel_id=1, source_target_pairs={{0,2},{1,3},{2,0},{3,1},{4,6},{5,7},{6,4},{7,5},{8,10},{9,11},{10,... | collective-permute-start | bytes 196616 | tf_op jit(solution)/shard_map/ppermute | solution.py:708
  32.6 2.9 %collective-permute-start.20 = (f32[4,80,128]{2,1,0:T(8,128)S(1)}, f32[4,80,128]{2,1,0:T(8,128)S(1)}, u32[]{:S(2)}, u32[]{:S(2)}) collective-permute-start(f32[4,80,128]{2,1,0:T(8,128)S(1)} %get-tuple-element.46.carried_ref), channel_id=1, source_target_pairs={{0,1},{1,0},{2,3},{3,2},{4,5},{5,4},{6,7},{7,6},{8,12},{9,13},{10,... | collective-permute-start | bytes 491528 | tf_op jit(solution)/shard_map/ppermute | solution.py:613
  32.7 1.5 %collective-permute-start.6 = (f32[4,40,128]{2,1,0:T(8,128)S(1)}, f32[4,40,128]{2,1,0:T(8,128)S(1)}, u32[]{:S(2)}, u32[]{:S(2)}) collective-permute-start(f32[4,40,128]{2,1,0:T(8,128)S(1)} %shard_map.120), channel_id=1, source_target_pairs={{0,1},{1,0},{2,3},{3,2},{4,5},{5,4},{6,7},{7,6},{8,12},{9,13},{10,... | collective-permute-start | bytes 245768 | tf_op jit(solution)/shard_map/ppermute | solution.py:613
  33.3 1.3 %collective-permute-start.3 = (f32[4,40,128]{2,1,0:T(8,128)S(1)}, f32[4,40,128]{2,1,0:T(8,128)S(1)}, u32[]{:S(2)}, u32[]{:S(2)}) collective-permute-start(f32[4,40,128]{2,1,0:T(8,128)S(1)} %shard_map.118), channel_id=1, source_target_pairs={{0,1},{1,0},{2,3},{3,2},{4,5},{5,4},{6,7},{7,6},{8,12},{9,13},{10,... | collective-permute-start | bytes 245768 | tf_op jit(solution)/shard_map/ppermute | solution.py:613
  35.3 1.3 %collective-permute-start.7 = (f32[8,16,128]{2,1,0:T(8,128)S(1)}, f32[8,16,128]{2,1,0:T(8,128)S(1)}, u32[]{:S(2)}, u32[]{:S(2)}) collective-permute-start(f32[8,16,128]{2,1,0:T(8,128)S(1)} %shard_map.121), channel_id=1, source_target_pairs={{0,1},{1,0},{2,3},{3,2},{4,5},{5,4},{6,7},{7,6},{8,9},{9,8},{10,11... | collective-permute-start | bytes 196616 | tf_op jit(solution)/shard_map/ppermute | solution.py:706
  35.6 8.2 %collective-permute-start.21 = (f32[4,80,128]{2,1,0:T(8,128)S(1)}, f32[4,80,128]{2,1,0:T(8,128)S(1)}, u32[]{:S(2)}, u32[]{:S(2)}) collective-permute-start(f32[4,80,128]{2,1,0:T(8,128)S(1)} %shard_map.133), channel_id=1, source_target_pairs={{0,1},{1,0},{2,3},{3,2},{4,8},{5,9},{6,10},{7,11},{8,4},{9,5},{10,... | collective-permute-start | bytes 491528 | tf_op jit(solution)/shard_map/ppermute | solution.py:613
  36.6 4.3 %collective-permute-start.8 = (f32[8,16,128]{2,1,0:T(8,128)S(1)}, f32[8,16,128]{2,1,0:T(8,128)S(1)}, u32[]{:S(2)}, u32[]{:S(2)}) collective-permute-start(f32[8,16,128]{2,1,0:T(8,128)S(1)} %add.21.refs_0_), channel_id=1, source_target_pairs={{0,2},{1,3},{2,0},{3,1},{4,6},{5,7},{6,4},{7,5},{8,10},{9,11},{10,... | collective-permute-start | bytes 196616 | tf_op jit(solution)/shard_map/ppermute | solution.py:708
  41.7 1.3 %collective-permute-start.17 = (f32[4,40,128]{2,1,0:T(8,128)S(1)}, f32[4,40,128]{2,1,0:T(8,128)S(1)}, u32[]{:S(2)}, u32[]{:S(2)}) collective-permute-start(f32[4,40,128]{2,1,0:T(8,128)S(1)} %get-tuple-element.45.carried_ref), channel_id=1, source_target_pairs={{0,1},{1,0},{2,3},{3,2},{4,5},{5,4},{6,7},{7,6},{8,12},{9,13},{10,... | collective-permute-start | bytes 245768 | tf_op jit(solution)/shard_map/ppermute | solution.py:613
  41.8 1.5 %collective-permute-start.14 = (f32[4,40,128]{2,1,0:T(8,128)S(1)}, f32[4,40,128]{2,1,0:T(8,128)S(1)}, u32[]{:S(2)}, u32[]{:S(2)}) collective-permute-start(f32[4,40,128]{2,1,0:T(8,128)S(1)} %get-tuple-element.44.carried_ref), channel_id=1, source_target_pairs={{0,1},{1,0},{2,3},{3,2},{4,5},{5,4},{6,7},{7,6},{8,12},{9,13},{10,... | collective-permute-start | bytes 245768 | tf_op jit(solution)/shard_map/ppermute | solution.py:613
  43.1 14.8 %collective-permute-start.18 = (f32[4,40,128]{2,1,0:T(8,128)S(1)}, f32[4,40,128]{2,1,0:T(8,128)S(1)}, u32[]{:S(2)}, u32[]{:S(2)}) collective-permute-start(f32[4,40,128]{2,1,0:T(8,128)S(1)} %shard_map.131), channel_id=1, source_target_pairs={{0,1},{1,0},{2,3},{3,2},{4,8},{5,9},{6,10},{7,11},{8,4},{9,5},{10,... | collective-permute-start | bytes 245768 | tf_op jit(solution)/shard_map/ppermute | solution.py:613
  43.4 15.2 %collective-permute-start.15 = (f32[4,40,128]{2,1,0:T(8,128)S(1)}, f32[4,40,128]{2,1,0:T(8,128)S(1)}, u32[]{:S(2)}, u32[]{:S(2)}) collective-permute-start(f32[4,40,128]{2,1,0:T(8,128)S(1)} %shard_map.129), channel_id=1, source_target_pairs={{0,1},{1,0},{2,3},{3,2},{4,8},{5,9},{6,10},{7,11},{8,4},{9,5},{10,... | collective-permute-start | bytes 245768 | tf_op jit(solution)/shard_map/ppermute | solution.py:613
  43.8 16.9 %copy-start.1 = (f32[160,8,128]{2,1,0:T(8,128)S(1)}, f32[160,8,128]{2,1,0:T(8,128)}, u32[]{:S(2)}) copy-start(f32[160,8,128]{2,1,0:T(8,128)} %r_ref.3) | copy-start | bytes 1966084
  43.9 19.9 %collective-permute-start.22 = (f32[4,80,128]{2,1,0:T(8,128)S(1)}, f32[4,80,128]{2,1,0:T(8,128)S(1)}, u32[]{:S(2)}, u32[]{:S(2)}) collective-permute-start(f32[4,80,128]{2,1,0:T(8,128)S(1)} %shard_map.134), channel_id=1, source_target_pairs={{0,4},{1,5},{2,6},{3,7},{4,0},{5,1},{6,2},{7,3},{8,9},{9,8},{10,11... | collective-permute-start | bytes 491528 | tf_op jit(solution)/shard_map/ppermute | solution.py:613
  57.9 4.9 %collective-permute-start.19 = (f32[4,40,128]{2,1,0:T(8,128)S(1)}, f32[4,40,128]{2,1,0:T(8,128)S(1)}, u32[]{:S(2)}, u32[]{:S(2)}) collective-permute-start(f32[4,40,128]{2,1,0:T(8,128)S(1)} %shard_map.132), channel_id=1, source_target_pairs={{0,4},{1,5},{2,6},{3,7},{4,0},{5,1},{6,2},{7,3},{8,9},{9,8},{10,11... | collective-permute-start | bytes 245768 | tf_op jit(solution)/shard_map/ppermute | solution.py:613
  58.6 5.1 %collective-permute-start.16 = (f32[4,40,128]{2,1,0:T(8,128)S(1)}, f32[4,40,128]{2,1,0:T(8,128)S(1)}, u32[]{:S(2)}, u32[]{:S(2)}) collective-permute-start(f32[4,40,128]{2,1,0:T(8,128)S(1)} %shard_map.130), channel_id=1, source_target_pairs={{0,4},{1,5},{2,6},{3,7},{4,0},{5,1},{6,2},{7,3},{8,9},{9,8},{10,11... | collective-permute-start | bytes 245768 | tf_op jit(solution)/shard_map/ppermute | solution.py:613
  64.8 4.6 %collective-permute-start.23 = (f32[168,128]{1,0:T(8,128)S(1)}, f32[168,128]{1,0:T(8,128)S(1)}, u32[]{:S(2)}, u32[]{:S(2)}) collective-permute-start(f32[168,128]{1,0:T(8,128)S(1)} %get-tuple-element.47.own_ref), channel_id=1, source_target_pairs={{0,16},{16,0},{1,17},{17,1},{2,18},{18,2},{3,19},{19,3},{4,20},{20... | collective-permute-start | bytes 258056 | tf_op jit(solution)/shard_map/ppermute | solution.py:586
  69.7 1.2 %collective-permute-start.24 = (f32[8,128]{1,0:T(8,128)S(1)}, f32[8,128]{1,0:T(8,128)S(1)}, u32[]{:S(2)}, u32[]{:S(2)}) collective-permute-start(f32[8,128]{1,0:T(8,128)S(1)} %get-tuple-element.48), channel_id=1, source_target_pairs={{0,1},{1,0},{2,3},{3,2},{4,5},{5,4},{6,7},{7,6},{8,9},{9,8},{10,11... | collective-permute-start | bytes 12296 | tf_op jit(solution)/shard_map/ppermute | solution.py:624
  70.9 3.6 %collective-permute-start.25 = (f32[8,128]{1,0:T(8,128)S(1)}, f32[8,128]{1,0:T(8,128)S(1)}, u32[]{:S(2)}, u32[]{:S(2)}) collective-permute-start(f32[8,128]{1,0:T(8,128)S(1)} %add.23), channel_id=1, source_target_pairs={{0,2},{1,3},{2,0},{3,1},{4,6},{5,7},{6,4},{7,5},{8,10},{9,11},{10,... | collective-permute-start | bytes 12296 | tf_op jit(solution)/shard_map/ppermute | solution.py:624
  74.5 4.8 %collective-permute-start.26 = (f32[8,128]{1,0:T(8,128)S(1)}, f32[8,128]{1,0:T(8,128)S(1)}, u32[]{:S(2)}, u32[]{:S(2)}) collective-permute-start(f32[8,128]{1,0:T(8,128)S(1)} %add.24), channel_id=1, source_target_pairs={{0,4},{4,0},{8,12},{12,8},{1,5},{5,1},{9,13},{13,9},{2,6},{6,2},{1... | collective-permute-start | bytes 12296 | tf_op jit(solution)/shard_map/ppermute | solution.py:624
  75.9 4.5 %collective-permute-start.27 = (f32[8,128]{1,0:T(8,128)S(1)}, f32[8,128]{1,0:T(8,128)S(1)}, u32[]{:S(2)}, u32[]{:S(2)}) collective-permute-start(f32[8,128]{1,0:T(8,128)S(1)} %add.24), channel_id=1, source_target_pairs={{0,8},{4,12},{8,0},{12,4},{1,9},{5,13},{9,1},{13,5},{2,10},{6,14},... | collective-permute-start | bytes 12296 | tf_op jit(solution)/shard_map/ppermute | solution.py:624
  75.9 5.4 %collective-permute-start.28 = (f32[8,128]{1,0:T(8,128)S(1)}, f32[8,128]{1,0:T(8,128)S(1)}, u32[]{:S(2)}, u32[]{:S(2)}) collective-permute-start(f32[8,128]{1,0:T(8,128)S(1)} %add.24), channel_id=1, source_target_pairs={{0,12},{4,8},{8,4},{12,0},{1,13},{5,9},{9,5},{13,1},{2,14},{6,10},... | collective-permute-start | bytes 12296 | tf_op jit(solution)/shard_map/ppermute | solution.py:624
  (4 other events, 15.4 us)

commit v4 on v2

--- a/solution.py
+++ b/solution.py
@@ -272,10 +272,9 @@
     rows, columns = pairs * r, 3 * pairs * c
     exact = functools.partial(jnp.dot, precision=lax.Precision.HIGHEST, preferred_element_type=f32)
     block = lambda at, size: jnp.floor((at + 0.5) * (1.0 / size))
-    at_row, at_column = iota((rows, r), 0), iota((c, columns), 1)
-    pick_row = (at_row - block(at_row, r) * r == iota((rows, r), 1)).astype(f32)
+    at_column = iota((c, columns), 1)
     pick_column = (at_column - block(at_column, c) * c == iota((c, columns), 0)).astype(f32)
-    everywhere = exact(exact(pick_row, source), pick_column)
+    everywhere = jnp.concatenate([exact(source, pick_column)] * pairs, axis=0)
     column = iota((1, columns), 1)
     part = block(column, pairs * c)
     own = block(iota((rows, 1), 0), r) == block(column - part * (pairs * c), c)
@@ -622,7 +621,9 @@
     masks = [0]
     for s in steps:
         masks = masks + [m ^ s for m in masks]
-    got = [lax.ppermute(v, axes, [(i, i ^ m) for i in range(total)]) for m in masks[1:]]
+    got = []
+    for m in masks[:0:-1] if len(masks) < 4 else (masks[3], masks[1], masks[2]):
+        got.append(lax.ppermute(v, axes, [(i, i ^ m) for i in range(total)]))
     for g in got:
         v = v + g
     return v
@@ -662,7 +663,7 @@
         functools.partial(k_tables, rows, cells),
         (sds(rows, cells), sds(2, 8, cells), jax.ShapeDtypeStruct((rows, 3 * cells, 2 * cells), bf16), sds(8, cells)),
         [decays],
-        cost=10**9,
+        cost=4 * 10**8,
     )
     inside, carried = call(
         functools.partial(k_lon_fwd, rows, k, cells), (sds(rows, k, cells), sds(4 * rows, k)), [direction, tables]

time: 72.9 us -> 71.8 us (0.985)
  Pallas kernels: 12.9 us -> 11.9 us
    pallas_call x32, Pallas kernels: 12.9 us -> 11.9 us  [call(): pl.pallas_call(body, out_shape=outs, in_specs=specs or [VM] * len(ins), o...]
  transfers between devices with their start and end apart: 35 -> 35, of which waited for: 17 -> 17; matrix products, arithmetic and copies ran while one was open for 0% -> 0% of each run, Pallas kernels for 12% -> 10%
where the time goes in v4:
time: 71.8 us; the launch traced here: 71.7 us
  starting transfers between devices  38.6 us (54%)
  waiting for transfers between devices  19.4 us (27%)
  Pallas kernels  11.9 us (17%)
  between operations  1.01 us (1%)
  other arithmetic  0.77 us (1%)
    ppermute x24, starting transfers between devices, lat_carry(): got[c][i].append(lax.ppermute(v, ('lat', 'mem'), pairs))  24.7 us
    pallas_call x32, Pallas kernels, call(): pl.pallas_call(body, out_shape=outs, in_specs=specs or [VM] * len(ins), o...  11.9 us
    ppermute x24, waiting for transfers between devices, lat_carry(): got[c][i].append(lax.ppermute(v, ('lat', 'mem'), pairs))  8.18 us
    ppermute x5, starting transfers between devices, all_sum(): got.append(lax.ppermute(v, axes, [(i, i ^ m) for i in range(total)]))  5.97 us
    ppermute x2, waiting for transfers between devices, lon_exchange(): lax.ppermute(carried, 'lon', [(j, (j + sign * r) % n) for j in range(n)])  4.89 us
    ppermute x2, starting transfers between devices, lon_exchange(): lax.ppermute(carried, 'lon', [(j, (j + sign * r) % n) for j in range(n)])  4.56 us
    ppermute x5, waiting for transfers between devices, all_sum(): got.append(lax.ppermute(v, axes, [(i, i ^ m) for i in range(total)]))  4.47 us
    ppermute x2, starting transfers between devices, iteration(): other = lax.ppermute(v, 'mem', [(i, i ^ step) for i in range(n_mem)])  2.65 us
  transfers between devices with their start and end apart: 35, of which 17 were waited for; matrix products, arithmetic and copies ran while one was open for 0% of the time, Pallas kernels for 10%

profile of v4, /device:TPU:0, one launch (start us, length us, event | category | flops | bytes accessed | tf_op | source)
XLA Modules:
  0.0 71.7 jit_solution(2494006270101944999)
XLA Ops:
  0.6 0.7 %pad_maximum_fusion = f32[136]{0:T(256)S(1)} fusion(f32[8]{0:T(128)} %param.15, f32[128]{0:T(128)} %param.16), kind=kLoop, calls=%fused_computation.1 | loop fusion | flops 136 | bytes 1088 | tf_op jit(solution)/shard_map/concatenate | solution.py:661
  2.4 3.0 %collective-permute-start = (f32[32,160]{1,0:T(8,128)S(1)}, f32[32,160]{1,0:T(8,128)S(1)}, u32[]{:S(2)}, u32[]{:S(2)}) collective-permute-start(f32[32,160]{1,0:T(8,128)S(1)} %get-tuple-element.33.refs_4_), channel_id=1, source_target_pairs={{0,16},{16,0},{1,17},{17,1},{2,18},{18,2},{3,19},{19,3},{4,20},{20... | collective-permute-start | bytes 61448 | tf_op jit(solution)/shard_map/ppermute | solution.py:586
  5.4 1.9 %collective-permute-done.refs_3_ = f32[32,160]{1,0:T(8,128)S(1)} collective-permute-done((f32[32,160]{1,0:T(8,128)S(1)}, f32[32,160]{1,0:T(8,128)S(1)}, u32[]{:S(2)}, u32[]{:S(2)}) %collective-permute-start) | collective-permute-done | bytes 20512 | tf_op jit(solution)/shard_map/ppermute | solution.py:586
  8.0 2.2 %collective-permute-start.12 = (f32[4,40,128]{2,1,0:T(8,128)S(1)}, f32[4,40,128]{2,1,0:T(8,128)S(1)}, u32[]{:S(2)}, u32[]{:S(2)}) collective-permute-start(f32[4,40,128]{2,1,0:T(8,128)S(1)} %get-tuple-element.45.carried_ref), channel_id=1, source_target_pairs={{0,4},{1,5},{2,6},{3,7},{4,0},{5,1},{6,2},{7,3},{8,9},{9,8},{10,11... | collective-permute-start | bytes 245768 | tf_op jit(solution)/shard_map/ppermute | solution.py:613
  10.2 1.9 %collective-permute-start.4 = (f32[4,40,128]{2,1,0:T(8,128)S(1)}, f32[4,40,128]{2,1,0:T(8,128)S(1)}, u32[]{:S(2)}, u32[]{:S(2)}) collective-permute-start(f32[4,40,128]{2,1,0:T(8,128)S(1)} %get-tuple-element.40.carried_ref), channel_id=1, source_target_pairs={{0,4},{1,5},{2,6},{3,7},{4,0},{5,1},{6,2},{7,3},{8,9},{9,8},{10,11... | collective-permute-start | bytes 245768 | tf_op jit(solution)/shard_map/ppermute | solution.py:613
  12.2 1.2 %collective-permute-done.12.got_ref.refs_9_ = f32[4,40,128]{2,1,0:T(8,128)S(1)} collective-permute-done((f32[4,40,128]{2,1,0:T(8,128)S(1)}, f32[4,40,128]{2,1,0:T(8,128)S(1)}, u32[]{:S(2)}, u32[]{:S(2)}) %collective-permute-start.12) | collective-permute-done | bytes 81952 | tf_op jit(solution)/shard_map/ppermute | solution.py:613
  13.5 1.9 %collective-permute-done.9.got_ref.refs_6_ = f32[4,40,128]{2,1,0:T(8,128)S(1)} collective-permute-done((f32[4,40,128]{2,1,0:T(8,128)S(1)}, f32[4,40,128]{2,1,0:T(8,128)S(1)}, u32[]{:S(2)}, u32[]{:S(2)}) %collective-permute-start.9) | collective-permute-done | bytes 81952 | tf_op jit(solution)/shard_map/ppermute | solution.py:613
  15.6 0.8 %collective-permute-done.4.got_ref.refs_9_ = f32[4,40,128]{2,1,0:T(8,128)S(1)} collective-permute-done((f32[4,40,128]{2,1,0:T(8,128)S(1)}, f32[4,40,128]{2,1,0:T(8,128)S(1)}, u32[]{:S(2)}, u32[]{:S(2)}) %collective-permute-start.4) | collective-permute-done | bytes 81952 | tf_op jit(solution)/shard_map/ppermute | solution.py:613
  16.5 0.8 %collective-permute-done.1.got_ref.refs_6_ = f32[4,40,128]{2,1,0:T(8,128)S(1)} collective-permute-done((f32[4,40,128]{2,1,0:T(8,128)S(1)}, f32[4,40,128]{2,1,0:T(8,128)S(1)}, u32[]{:S(2)}, u32[]{:S(2)}) %collective-permute-start.1) | collective-permute-done | bytes 81952 | tf_op jit(solution)/shard_map/ppermute | solution.py:613
  17.4 1.1 %shard_map.115 = (f32[2624,128]{1,0:T(8,128)S(1)}, f32[2624,128]{1,0:T(8,128)S(1)}) custom-call(bf16[20,32,8,128]{3,2,1,0:T(8,128)(2,1)S(1)} %copy-done.4), custom_call_target="tpu_custom_call" | custom-call | flops 1000000000 | bytes 1000 | tf_op jit(solution)/shard_map/pallas_call | solution.py:567
  19.9 0.8 %shard_map.116 = (f32[80,128]{1,0:T(8,128)S(1)}, bf16[320,240]{1,0:T(8,128)(2,1)S(1)}) custom-call(f32[8,32]{1,0:T(8,128)S(1)} %copy-done.5, s32[20]{0:T(128)S(1)} %copy-done.6), custom_call_target="tpu_custom_call" | custom-call | flops 1000000000 | bytes 1000 | tf_op jit(solution)/shard_map/pallas_call | solution.py:567
  22.9 1.6 %collective-permute-start.16 = (f32[8,16,128]{2,1,0:T(8,128)S(1)}, f32[8,16,128]{2,1,0:T(8,128)S(1)}, u32[]{:S(2)}, u32[]{:S(2)}) collective-permute-start(f32[8,16,128]{2,1,0:T(8,128)S(1)} %add.22.refs_0_), channel_id=1, source_target_pairs={{0,2},{1,3},{2,0},{3,1},{4,6},{5,7},{6,4},{7,5},{8,10},{9,11},{10,... | collective-permute-start | bytes 196616 | tf_op jit(solution)/shard_map/ppermute | solution.py:710
  24.5 1.1 %collective-permute-start.8 = (f32[8,16,128]{2,1,0:T(8,128)S(1)}, f32[8,16,128]{2,1,0:T(8,128)S(1)}, u32[]{:S(2)}, u32[]{:S(2)}) collective-permute-start(f32[8,16,128]{2,1,0:T(8,128)S(1)} %add.21.refs_0_), channel_id=1, source_target_pairs={{0,2},{1,3},{2,0},{3,1},{4,6},{5,7},{6,4},{7,5},{8,10},{9,11},{10,... | collective-permute-start | bytes 196616 | tf_op jit(solution)/shard_map/ppermute | solution.py:710
  25.8 1.6 %collective-permute-done.16.refs_1_ = f32[8,16,128]{2,1,0:T(8,128)S(1)} collective-permute-done((f32[8,16,128]{2,1,0:T(8,128)S(1)}, f32[8,16,128]{2,1,0:T(8,128)S(1)}, u32[]{:S(2)}, u32[]{:S(2)}) %collective-permute-start.16) | collective-permute-done | bytes 65568 | tf_op jit(solution)/shard_map/ppermute | solution.py:710
  27.4 0.8 %shard_map.129 = (f32[8,80,128]{2,1,0:T(8,128)S(1)}, f32[4,40,128]{2,1,0:T(8,128)S(1)}, f32[4,40,128]{2,1,0:T(8,128)S(1)}) custom-call(f32[8,16,128]{2,1,0:T(8,128)S(1)} %add.22.refs_0_, f32[8,16,128]{2,1,0:T(8,128)S(1)} %collective-permute-done.16.refs_1_, f32[32,8,128]{2,1,0:T(8,128)S(1)} %copy-done.3, f32[2624,128]{1,0:T(8,128)S(1)} %get-tuple-element.43.refs_3_, ...), custom_call_target="tpu_custom_call" | custom-call | tf_op jit(solution)/shard_map/pallas_call | solution.py:567
  28.8 0.8 %shard_map.123 = (f32[8,80,128]{2,1,0:T(8,128)S(1)}, f32[4,40,128]{2,1,0:T(8,128)S(1)}, f32[4,40,128]{2,1,0:T(8,128)S(1)}) custom-call(f32[8,16,128]{2,1,0:T(8,128)S(1)} %add.21.refs_0_, f32[8,16,128]{2,1,0:T(8,128)S(1)} %collective-permute-done.8.refs_1_, f32[32,8,128]{2,1,0:T(8,128)S(1)} %copy-done.3, f32[2624,128]{1,0:T(8,128)S(1)} %get-tuple-element.36.refs_3_, ...), custom_call_target="tpu_custom_call" | custom-call | tf_op jit(solution)/shard_map/pallas_call | solution.py:567
  31.7 0.8 %shard_map.130.refs_4_ = bf16[8,384,256]{2,1,0:T(8,128)(2,1)S(1)} custom-call(f32[8,128]{1,0:T(8,128)S(1)} %get-tuple-element.29.refs_1_.lon_ref), custom_call_target="tpu_custom_call" | custom-call | flops 1000000000 | bytes 1000 | tf_op jit(solution)/shard_map/pallas_call | solution.py:567
  32.6 13.8 %collective-permute-start.28 = (f32[4,40,128]{2,1,0:T(8,128)S(1)}, f32[4,40,128]{2,1,0:T(8,128)S(1)}, u32[]{:S(2)}, u32[]{:S(2)}) collective-permute-start(f32[4,40,128]{2,1,0:T(8,128)S(1)} %shard_map.138), channel_id=1, source_target_pairs={{0,4},{1,5},{2,6},{3,7},{4,0},{5,1},{6,2},{7,3},{8,9},{9,8},{10,11... | collective-permute-start | bytes 245768 | tf_op jit(solution)/shard_map/ppermute | solution.py:613
  46.9 1.6 %collective-permute-start.22 = (f32[4,40,128]{2,1,0:T(8,128)S(1)}, f32[4,40,128]{2,1,0:T(8,128)S(1)}, u32[]{:S(2)}, u32[]{:S(2)}) collective-permute-start(f32[4,40,128]{2,1,0:T(8,128)S(1)} %shard_map.134), channel_id=1, source_target_pairs={{0,4},{1,5},{2,6},{3,7},{4,0},{5,1},{6,2},{7,3},{8,9},{9,8},{10,11... | collective-permute-start | bytes 245768 | tf_op jit(solution)/shard_map/ppermute | solution.py:613
  49.1 0.9 %shard_map.139.refs_19_ = f32[160,128]{1,0:T(8,128)S(1)} custom-call(f32[160,8,128]{2,1,0:T(8,128)S(1)} %copy-done, f32[160,8,128]{2,1,0:T(8,128)S(1)} %copy-done.1, f32[8,128]{1,0:T(8,128)S(1)} %get-tuple-element.29.refs_1_.lon_ref), custom_call_target="tpu_custom_call" | custom-call | flops 1000000000 | bytes 1000 | tf_op jit(solution)/shard_map/pallas_call | solution.py:567
  50.0 1.6 %collective-permute-done.25.refs_13_ = f32[4,40,128]{2,1,0:T(8,128)S(1)} collective-permute-done((f32[4,40,128]{2,1,0:T(8,128)S(1)}, f32[4,40,128]{2,1,0:T(8,128)S(1)}, u32[]{:S(2)}, u32[]{:S(2)}) %collective-permute-start.25) | collective-permute-done | bytes 81952 | tf_op jit(solution)/shard_map/ppermute | solution.py:613
  51.6 0.9 %collective-permute-done.22.refs_10_ = f32[4,40,128]{2,1,0:T(8,128)S(1)} collective-permute-done((f32[4,40,128]{2,1,0:T(8,128)S(1)}, f32[4,40,128]{2,1,0:T(8,128)S(1)}, u32[]{:S(2)}, u32[]{:S(2)}) %collective-permute-start.22) | collective-permute-done | bytes 81952 | tf_op jit(solution)/shard_map/ppermute | solution.py:613
  52.5 0.9 %collective-permute-done.19.refs_7_ = f32[4,40,128]{2,1,0:T(8,128)S(1)} collective-permute-done((f32[4,40,128]{2,1,0:T(8,128)S(1)}, f32[4,40,128]{2,1,0:T(8,128)S(1)}, u32[]{:S(2)}, u32[]{:S(2)}) %collective-permute-start.19) | collective-permute-done | bytes 81952 | tf_op jit(solution)/shard_map/ppermute | solution.py:613
  53.4 1.0 %shard_map.140 = (f32[8,160,128]{2,1,0:T(8,128)S(1)}, f32[168,128]{1,0:T(8,128)S(1)}) custom-call(f32[8,80,128]{2,1,0:T(8,128)S(1)} %get-tuple-element.41.refs_0_, f32[8,80,128]{2,1,0:T(8,128)S(1)} %get-tuple-element.46.refs_1_, f32[2,8,128]{2,1,0:T(8,128)S(1)} %get-tuple-element.32.refs_2_.lat_ref.refs_1_.refs_6_, ...), custom_call_target="tpu_custom_call" | custom-call | tf_op jit(solution)/shard_map/pallas_call | solution.py:567
  54.5 1.6 %collective-permute-start.29 = (f32[168,128]{1,0:T(8,128)S(1)}, f32[168,128]{1,0:T(8,128)S(1)}, u32[]{:S(2)}, u32[]{:S(2)}) collective-permute-start(f32[168,128]{1,0:T(8,128)S(1)} %get-tuple-element.51.own_ref), channel_id=1, source_target_pairs={{0,16},{16,0},{1,17},{17,1},{2,18},{18,2},{3,19},{19,3},{4,20},{20... | collective-permute-start | bytes 258056 | tf_op jit(solution)/shard_map/ppermute | solution.py:586
  56.0 3.0 %collective-permute-done.29.other_ref = f32[168,128]{1,0:T(8,128)S(1)} collective-permute-done((f32[168,128]{1,0:T(8,128)S(1)}, f32[168,128]{1,0:T(8,128)S(1)}, u32[]{:S(2)}, u32[]{:S(2)}) %collective-permute-start.29) | collective-permute-done | bytes 86048 | tf_op jit(solution)/shard_map/ppermute | solution.py:586
  59.4 1.2 %collective-permute-done.30 = f32[8,128]{1,0:T(8,128)S(1)} collective-permute-done((f32[8,128]{1,0:T(8,128)S(1)}, f32[8,128]{1,0:T(8,128)S(1)}, u32[]{:S(2)}, u32[]{:S(2)}) %collective-permute-start.30) | collective-permute-done | bytes 4128 | tf_op jit(solution)/shard_map/ppermute | solution.py:626
  60.5 1.5 %collective-permute-start.31 = (f32[8,128]{1,0:T(8,128)S(1)}, f32[8,128]{1,0:T(8,128)S(1)}, u32[]{:S(2)}, u32[]{:S(2)}) collective-permute-start(f32[8,128]{1,0:T(8,128)S(1)} %add.23), channel_id=1, source_target_pairs={{0,2},{1,3},{2,0},{3,1},{4,6},{5,7},{6,4},{7,5},{8,10},{9,11},{10,... | collective-permute-start | bytes 12296 | tf_op jit(solution)/shard_map/ppermute | solution.py:626
  62.0 2.1 %collective-permute-done.31 = f32[8,128]{1,0:T(8,128)S(1)} collective-permute-done((f32[8,128]{1,0:T(8,128)S(1)}, f32[8,128]{1,0:T(8,128)S(1)}, u32[]{:S(2)}, u32[]{:S(2)}) %collective-permute-start.31) | collective-permute-done | bytes 4128 | tf_op jit(solution)/shard_map/ppermute | solution.py:626
  64.1 1.1 %collective-permute-start.33 = (f32[8,128]{1,0:T(8,128)S(1)}, f32[8,128]{1,0:T(8,128)S(1)}, u32[]{:S(2)}, u32[]{:S(2)}) collective-permute-start(f32[8,128]{1,0:T(8,128)S(1)} %add.24), channel_id=1, source_target_pairs={{0,4},{4,0},{8,12},{12,8},{1,5},{5,1},{9,13},{13,9},{2,6},{6,2},{1... | collective-permute-start | bytes 12296 | tf_op jit(solution)/shard_map/ppermute | solution.py:626
  65.2 3.3 %collective-permute-start.34 = (f32[8,128]{1,0:T(8,128)S(1)}, f32[8,128]{1,0:T(8,128)S(1)}, u32[]{:S(2)}, u32[]{:S(2)}) collective-permute-start(f32[8,128]{1,0:T(8,128)S(1)} %add.24), channel_id=1, source_target_pairs={{0,8},{4,12},{8,0},{12,4},{1,9},{5,13},{9,1},{13,5},{2,10},{6,14},... | collective-permute-start | bytes 12296 | tf_op jit(solution)/shard_map/ppermute | solution.py:626
  70.2 1.5 %shard_map.143 = (f32[160,8,128]{2,1,0:T(8,128)}, f32[160,8,128]{2,1,0:T(8,128)}, f32[160,8,128]{2,1,0:T(8,128)}) custom-call(f32[8,128]{1,0:T(8,128)S(1)} %add_add_fusion.sums_ref, f32[160,8,128]{2,1,0:T(8,128)S(1)} %copy-done.2, f32[160,8,128]{2,1,0:T(8,128)S(1)} %copy-done.1, f32[160,8,128]{2,1,0:T(8,128)S(1)} %copy-done, f32[160,8,128]{2,1,0:T(8,128)S(1)} %bitcast.2), custom_call_target="tpu_custom_call" | custom-call | tf_op jit(solution)/shard_map/pallas_call | solution.py:567
  (90 shorter events, 11.9 us)
Async XLA Ops:
  2.4 4.9 %collective-permute-start = (f32[32,160]{1,0:T(8,128)S(1)}, f32[32,160]{1,0:T(8,128)S(1)}, u32[]{:S(2)}, u32[]{:S(2)}) collective-permute-start(f32[32,160]{1,0:T(8,128)S(1)} %get-tuple-element.33.refs_4_), channel_id=1, source_target_pairs={{0,16},{16,0},{1,17},{17,1},{2,18},{18,2},{3,19},{19,3},{4,20},{20... | collective-permute-start | bytes 61448 | tf_op jit(solution)/shard_map/ppermute | solution.py:586
  8.0 5.5 %collective-permute-start.12 = (f32[4,40,128]{2,1,0:T(8,128)S(1)}, f32[4,40,128]{2,1,0:T(8,128)S(1)}, u32[]{:S(2)}, u32[]{:S(2)}) collective-permute-start(f32[4,40,128]{2,1,0:T(8,128)S(1)} %get-tuple-element.45.carried_ref), channel_id=1, source_target_pairs={{0,4},{1,5},{2,6},{3,7},{4,0},{5,1},{6,2},{7,3},{8,9},{9,8},{10,11... | collective-permute-start | bytes 245768 | tf_op jit(solution)/shard_map/ppermute | solution.py:613
  10.1 5.3 %collective-permute-start.9 = (f32[4,40,128]{2,1,0:T(8,128)S(1)}, f32[4,40,128]{2,1,0:T(8,128)S(1)}, u32[]{:S(2)}, u32[]{:S(2)}) collective-permute-start(f32[4,40,128]{2,1,0:T(8,128)S(1)} %get-tuple-element.44.carried_ref), channel_id=1, source_target_pairs={{0,4},{1,5},{2,6},{3,7},{4,0},{5,1},{6,2},{7,3},{8,9},{9,8},{10,11... | collective-permute-start | bytes 245768 | tf_op jit(solution)/shard_map/ppermute | solution.py:613
  10.2 6.2 %collective-permute-start.4 = (f32[4,40,128]{2,1,0:T(8,128)S(1)}, f32[4,40,128]{2,1,0:T(8,128)S(1)}, u32[]{:S(2)}, u32[]{:S(2)}) collective-permute-start(f32[4,40,128]{2,1,0:T(8,128)S(1)} %get-tuple-element.40.carried_ref), channel_id=1, source_target_pairs={{0,4},{1,5},{2,6},{3,7},{4,0},{5,1},{6,2},{7,3},{8,9},{9,8},{10,11... | collective-permute-start | bytes 245768 | tf_op jit(solution)/shard_map/ppermute | solution.py:613
  12.1 5.1 %collective-permute-start.1 = (f32[4,40,128]{2,1,0:T(8,128)S(1)}, f32[4,40,128]{2,1,0:T(8,128)S(1)}, u32[]{:S(2)}, u32[]{:S(2)}) collective-permute-start(f32[4,40,128]{2,1,0:T(8,128)S(1)} %get-tuple-element.39.carried_ref), channel_id=1, source_target_pairs={{0,4},{1,5},{2,6},{3,7},{4,0},{5,1},{6,2},{7,3},{8,9},{9,8},{10,11... | collective-permute-start | bytes 245768 | tf_op jit(solution)/shard_map/ppermute | solution.py:613
  13.5 5.0 %collective-permute-start.13 = (f32[4,40,128]{2,1,0:T(8,128)S(1)}, f32[4,40,128]{2,1,0:T(8,128)S(1)}, u32[]{:S(2)}, u32[]{:S(2)}) collective-permute-start(f32[4,40,128]{2,1,0:T(8,128)S(1)} %shard_map.126), channel_id=1, source_target_pairs={{0,1},{1,0},{2,3},{3,2},{4,8},{5,9},{6,10},{7,11},{8,4},{9,5},{10,... | collective-permute-start | bytes 245768 | tf_op jit(solution)/shard_map/ppermute | solution.py:613
  15.5 3.6 %collective-permute-start.10 = (f32[4,40,128]{2,1,0:T(8,128)S(1)}, f32[4,40,128]{2,1,0:T(8,128)S(1)}, u32[]{:S(2)}, u32[]{:S(2)}) collective-permute-start(f32[4,40,128]{2,1,0:T(8,128)S(1)} %shard_map.124), channel_id=1, source_target_pairs={{0,1},{1,0},{2,3},{3,2},{4,8},{5,9},{6,10},{7,11},{8,4},{9,5},{10,... | collective-permute-start | bytes 245768 | tf_op jit(solution)/shard_map/ppermute | solution.py:613
  16.4 2.8 %collective-permute-start.5 = (f32[4,40,128]{2,1,0:T(8,128)S(1)}, f32[4,40,128]{2,1,0:T(8,128)S(1)}, u32[]{:S(2)}, u32[]{:S(2)}) collective-permute-start(f32[4,40,128]{2,1,0:T(8,128)S(1)} %shard_map.119), channel_id=1, source_target_pairs={{0,1},{1,0},{2,3},{3,2},{4,8},{5,9},{6,10},{7,11},{8,4},{9,5},{10,... | collective-permute-start | bytes 245768 | tf_op jit(solution)/shard_map/ppermute | solution.py:613
  17.3 2.5 %collective-permute-start.2 = (f32[4,40,128]{2,1,0:T(8,128)S(1)}, f32[4,40,128]{2,1,0:T(8,128)S(1)}, u32[]{:S(2)}, u32[]{:S(2)}) collective-permute-start(f32[4,40,128]{2,1,0:T(8,128)S(1)} %shard_map.117), channel_id=1, source_target_pairs={{0,1},{1,0},{2,3},{3,2},{4,8},{5,9},{6,10},{7,11},{8,4},{9,5},{10,... | collective-permute-start | bytes 245768 | tf_op jit(solution)/shard_map/ppermute | solution.py:613
  18.5 2.2 %collective-permute-start.14 = (f32[4,40,128]{2,1,0:T(8,128)S(1)}, f32[4,40,128]{2,1,0:T(8,128)S(1)}, u32[]{:S(2)}, u32[]{:S(2)}) collective-permute-start(f32[4,40,128]{2,1,0:T(8,128)S(1)} %shard_map.127), channel_id=1, source_target_pairs={{0,1},{1,0},{2,3},{3,2},{4,5},{5,4},{6,7},{7,6},{8,12},{9,13},{10,... | collective-permute-start | bytes 245768 | tf_op jit(solution)/shard_map/ppermute | solution.py:613
  19.1 1.7 %collective-permute-start.11 = (f32[4,40,128]{2,1,0:T(8,128)S(1)}, f32[4,40,128]{2,1,0:T(8,128)S(1)}, u32[]{:S(2)}, u32[]{:S(2)}) collective-permute-start(f32[4,40,128]{2,1,0:T(8,128)S(1)} %shard_map.125), channel_id=1, source_target_pairs={{0,1},{1,0},{2,3},{3,2},{4,5},{5,4},{6,7},{7,6},{8,12},{9,13},{10,... | collective-permute-start | bytes 245768 | tf_op jit(solution)/shard_map/ppermute | solution.py:613
  19.2 2.7 %collective-permute-start.6 = (f32[4,40,128]{2,1,0:T(8,128)S(1)}, f32[4,40,128]{2,1,0:T(8,128)S(1)}, u32[]{:S(2)}, u32[]{:S(2)}) collective-permute-start(f32[4,40,128]{2,1,0:T(8,128)S(1)} %shard_map.120), channel_id=1, source_target_pairs={{0,1},{1,0},{2,3},{3,2},{4,5},{5,4},{6,7},{7,6},{8,12},{9,13},{10,... | collective-permute-start | bytes 245768 | tf_op jit(solution)/shard_map/ppermute | solution.py:613
  19.8 2.2 %collective-permute-start.3 = (f32[4,40,128]{2,1,0:T(8,128)S(1)}, f32[4,40,128]{2,1,0:T(8,128)S(1)}, u32[]{:S(2)}, u32[]{:S(2)}) collective-permute-start(f32[4,40,128]{2,1,0:T(8,128)S(1)} %shard_map.118), channel_id=1, source_target_pairs={{0,1},{1,0},{2,3},{3,2},{4,5},{5,4},{6,7},{7,6},{8,12},{9,13},{10,... | collective-permute-start | bytes 245768 | tf_op jit(solution)/shard_map/ppermute | solution.py:613
  22.6 1.8 %collective-permute-start.7 = (f32[8,16,128]{2,1,0:T(8,128)S(1)}, f32[8,16,128]{2,1,0:T(8,128)S(1)}, u32[]{:S(2)}, u32[]{:S(2)}) collective-permute-start(f32[8,16,128]{2,1,0:T(8,128)S(1)} %shard_map.121), channel_id=1, source_target_pairs={{0,1},{1,0},{2,3},{3,2},{4,5},{5,4},{6,7},{7,6},{8,9},{9,8},{10,11... | collective-permute-start | bytes 196616 | tf_op jit(solution)/shard_map/ppermute | solution.py:708
  22.9 4.5 %collective-permute-start.16 = (f32[8,16,128]{2,1,0:T(8,128)S(1)}, f32[8,16,128]{2,1,0:T(8,128)S(1)}, u32[]{:S(2)}, u32[]{:S(2)}) collective-permute-start(f32[8,16,128]{2,1,0:T(8,128)S(1)} %add.22.refs_0_), channel_id=1, source_target_pairs={{0,2},{1,3},{2,0},{3,1},{4,6},{5,7},{6,4},{7,5},{8,10},{9,11},{10,... | collective-permute-start | bytes 196616 | tf_op jit(solution)/shard_map/ppermute | solution.py:710
  24.5 4.3 %collective-permute-start.8 = (f32[8,16,128]{2,1,0:T(8,128)S(1)}, f32[8,16,128]{2,1,0:T(8,128)S(1)}, u32[]{:S(2)}, u32[]{:S(2)}) collective-permute-start(f32[8,16,128]{2,1,0:T(8,128)S(1)} %add.21.refs_0_), channel_id=1, source_target_pairs={{0,2},{1,3},{2,0},{3,1},{4,6},{5,7},{6,4},{7,5},{8,10},{9,11},{10,... | collective-permute-start | bytes 196616 | tf_op jit(solution)/shard_map/ppermute | solution.py:710
  28.2 2.0 %collective-permute-start.26 = (f32[4,40,128]{2,1,0:T(8,128)S(1)}, f32[4,40,128]{2,1,0:T(8,128)S(1)}, u32[]{:S(2)}, u32[]{:S(2)}) collective-permute-start(f32[4,40,128]{2,1,0:T(8,128)S(1)} %get-tuple-element.50.carried_ref), channel_id=1, source_target_pairs={{0,1},{1,0},{2,3},{3,2},{4,5},{5,4},{6,7},{7,6},{8,12},{9,13},{10,... | collective-permute-start | bytes 245768 | tf_op jit(solution)/shard_map/ppermute | solution.py:613
  28.2 2.1 %collective-permute-start.23 = (f32[4,40,128]{2,1,0:T(8,128)S(1)}, f32[4,40,128]{2,1,0:T(8,128)S(1)}, u32[]{:S(2)}, u32[]{:S(2)}) collective-permute-start(f32[4,40,128]{2,1,0:T(8,128)S(1)} %get-tuple-element.49.carried_ref), channel_id=1, source_target_pairs={{0,1},{1,0},{2,3},{3,2},{4,5},{5,4},{6,7},{7,6},{8,12},{9,13},{10,... | collective-permute-start | bytes 245768 | tf_op jit(solution)/shard_map/ppermute | solution.py:613
  29.7 1.5 %collective-permute-start.17 = (f32[4,40,128]{2,1,0:T(8,128)S(1)}, f32[4,40,128]{2,1,0:T(8,128)S(1)}, u32[]{:S(2)}, u32[]{:S(2)}) collective-permute-start(f32[4,40,128]{2,1,0:T(8,128)S(1)} %get-tuple-element.47.carried_ref), channel_id=1, source_target_pairs={{0,1},{1,0},{2,3},{3,2},{4,5},{5,4},{6,7},{7,6},{8,12},{9,13},{10,... | collective-permute-start | bytes 245768 | tf_op jit(solution)/shard_map/ppermute | solution.py:613
  30.2 2.3 %collective-permute-start.27 = (f32[4,40,128]{2,1,0:T(8,128)S(1)}, f32[4,40,128]{2,1,0:T(8,128)S(1)}, u32[]{:S(2)}, u32[]{:S(2)}) collective-permute-start(f32[4,40,128]{2,1,0:T(8,128)S(1)} %shard_map.137), channel_id=1, source_target_pairs={{0,1},{1,0},{2,3},{3,2},{4,8},{5,9},{6,10},{7,11},{8,4},{9,5},{10,... | collective-permute-start | bytes 245768 | tf_op jit(solution)/shard_map/ppermute | solution.py:613
  30.4 15.9 %collective-permute-start.24 = (f32[4,40,128]{2,1,0:T(8,128)S(1)}, f32[4,40,128]{2,1,0:T(8,128)S(1)}, u32[]{:S(2)}, u32[]{:S(2)}) collective-permute-start(f32[4,40,128]{2,1,0:T(8,128)S(1)} %shard_map.135), channel_id=1, source_target_pairs={{0,1},{1,0},{2,3},{3,2},{4,8},{5,9},{6,10},{7,11},{8,4},{9,5},{10,... | collective-permute-start | bytes 245768 | tf_op jit(solution)/shard_map/ppermute | solution.py:613
  31.0 15.9 %collective-permute-start.21 = (f32[4,40,128]{2,1,0:T(8,128)S(1)}, f32[4,40,128]{2,1,0:T(8,128)S(1)}, u32[]{:S(2)}, u32[]{:S(2)}) collective-permute-start(f32[4,40,128]{2,1,0:T(8,128)S(1)} %shard_map.133), channel_id=1, source_target_pairs={{0,1},{1,0},{2,3},{3,2},{4,8},{5,9},{6,10},{7,11},{8,4},{9,5},{10,... | collective-permute-start | bytes 245768 | tf_op jit(solution)/shard_map/ppermute | solution.py:613
  31.3 17.3 %collective-permute-start.18 = (f32[4,40,128]{2,1,0:T(8,128)S(1)}, f32[4,40,128]{2,1,0:T(8,128)S(1)}, u32[]{:S(2)}, u32[]{:S(2)}) collective-permute-start(f32[4,40,128]{2,1,0:T(8,128)S(1)} %shard_map.131), channel_id=1, source_target_pairs={{0,1},{1,0},{2,3},{3,2},{4,8},{5,9},{6,10},{7,11},{8,4},{9,5},{10,... | collective-permute-start | bytes 245768 | tf_op jit(solution)/shard_map/ppermute | solution.py:613
  32.6 17.5 %collective-permute-start.28 = (f32[4,40,128]{2,1,0:T(8,128)S(1)}, f32[4,40,128]{2,1,0:T(8,128)S(1)}, u32[]{:S(2)}, u32[]{:S(2)}) collective-permute-start(f32[4,40,128]{2,1,0:T(8,128)S(1)} %shard_map.138), channel_id=1, source_target_pairs={{0,4},{1,5},{2,6},{3,7},{4,0},{5,1},{6,2},{7,3},{8,9},{9,8},{10,11... | collective-permute-start | bytes 245768 | tf_op jit(solution)/shard_map/ppermute | solution.py:613
  46.4 5.3 %collective-permute-start.25 = (f32[4,40,128]{2,1,0:T(8,128)S(1)}, f32[4,40,128]{2,1,0:T(8,128)S(1)}, u32[]{:S(2)}, u32[]{:S(2)}) collective-permute-start(f32[4,40,128]{2,1,0:T(8,128)S(1)} %shard_map.136), channel_id=1, source_target_pairs={{0,4},{1,5},{2,6},{3,7},{4,0},{5,1},{6,2},{7,3},{8,9},{9,8},{10,11... | collective-permute-start | bytes 245768 | tf_op jit(solution)/shard_map/ppermute | solution.py:613
  46.9 5.6 %collective-permute-start.22 = (f32[4,40,128]{2,1,0:T(8,128)S(1)}, f32[4,40,128]{2,1,0:T(8,128)S(1)}, u32[]{:S(2)}, u32[]{:S(2)}) collective-permute-start(f32[4,40,128]{2,1,0:T(8,128)S(1)} %shard_map.134), channel_id=1, source_target_pairs={{0,4},{1,5},{2,6},{3,7},{4,0},{5,1},{6,2},{7,3},{8,9},{9,8},{10,11... | collective-permute-start | bytes 245768 | tf_op jit(solution)/shard_map/ppermute | solution.py:613
  48.6 4.8 %collective-permute-start.19 = (f32[4,40,128]{2,1,0:T(8,128)S(1)}, f32[4,40,128]{2,1,0:T(8,128)S(1)}, u32[]{:S(2)}, u32[]{:S(2)}) collective-permute-start(f32[4,40,128]{2,1,0:T(8,128)S(1)} %shard_map.132), channel_id=1, source_target_pairs={{0,4},{1,5},{2,6},{3,7},{4,0},{5,1},{6,2},{7,3},{8,9},{9,8},{10,11... | collective-permute-start | bytes 245768 | tf_op jit(solution)/shard_map/ppermute | solution.py:613
  54.5 4.6 %collective-permute-start.29 = (f32[168,128]{1,0:T(8,128)S(1)}, f32[168,128]{1,0:T(8,128)S(1)}, u32[]{:S(2)}, u32[]{:S(2)}) collective-permute-start(f32[168,128]{1,0:T(8,128)S(1)} %get-tuple-element.51.own_ref), channel_id=1, source_target_pairs={{0,16},{16,0},{1,17},{17,1},{2,18},{18,2},{3,19},{19,3},{4,20},{20... | collective-permute-start | bytes 258056 | tf_op jit(solution)/shard_map/ppermute | solution.py:586
  60.5 3.6 %collective-permute-start.31 = (f32[8,128]{1,0:T(8,128)S(1)}, f32[8,128]{1,0:T(8,128)S(1)}, u32[]{:S(2)}, u32[]{:S(2)}) collective-permute-start(f32[8,128]{1,0:T(8,128)S(1)} %add.23), channel_id=1, source_target_pairs={{0,2},{1,3},{2,0},{3,1},{4,6},{5,7},{6,4},{7,5},{8,10},{9,11},{10,... | collective-permute-start | bytes 12296 | tf_op jit(solution)/shard_map/ppermute | solution.py:626
  64.1 5.4 %collective-permute-start.32 = (f32[8,128]{1,0:T(8,128)S(1)}, f32[8,128]{1,0:T(8,128)S(1)}, u32[]{:S(2)}, u32[]{:S(2)}) collective-permute-start(f32[8,128]{1,0:T(8,128)S(1)} %add.24), channel_id=1, source_target_pairs={{0,12},{4,8},{8,4},{12,0},{1,13},{5,9},{9,5},{13,1},{2,14},{6,10},... | collective-permute-start | bytes 12296 | tf_op jit(solution)/shard_map/ppermute | solution.py:626
  64.1 5.4 %collective-permute-start.33 = (f32[8,128]{1,0:T(8,128)S(1)}, f32[8,128]{1,0:T(8,128)S(1)}, u32[]{:S(2)}, u32[]{:S(2)}) collective-permute-start(f32[8,128]{1,0:T(8,128)S(1)} %add.24), channel_id=1, source_target_pairs={{0,4},{4,0},{8,12},{12,8},{1,5},{5,1},{9,13},{13,9},{2,6},{6,2},{1... | collective-permute-start | bytes 12296 | tf_op jit(solution)/shard_map/ppermute | solution.py:626
  65.2 5.0 %collective-permute-start.34 = (f32[8,128]{1,0:T(8,128)S(1)}, f32[8,128]{1,0:T(8,128)S(1)}, u32[]{:S(2)}, u32[]{:S(2)}) collective-permute-start(f32[8,128]{1,0:T(8,128)S(1)} %add.24), channel_id=1, source_target_pairs={{0,8},{4,12},{8,0},{12,4},{1,9},{5,13},{9,1},{13,5},{2,10},{6,14},... | collective-permute-start | bytes 12296 | tf_op jit(solution)/shard_map/ppermute | solution.py:626
  (10 other events, 47.9 us)
